TPU v7x, 512 devices: a whole 4x8x8 slice. The times are simulated.
512 devices in a mesh: leaf: 8 (over x, core), front: 64 (over y, z).
Axes of the slice: x: 4, y: 8, z: 8, core: 2. Of those that a mesh axis runs over, the one named last changes fastest.
Arguments:
- rhs_leaf: float32 [8, 32, 229376], P('leaf', None, 'front'), may hold values from -6 to 6
- rhs_sep: float32 [8, 32, 8192], P('leaf', None, 'front'), may hold values from -6 to 6
- leaf_inv: float32 [8, 1792, 128, 128], P('leaf', 'front')
- leaf_update: float32 [8, 1792, 128, 128], P('leaf', 'front'), may hold values from -0.09375 to 0.09375
- update_rows: int32 [8, 1792, 128], P('leaf', 'front'), may hold values from 0 to 128, as said below
- update_owner: int32 [8, 1792, 1], P('leaf', 'front'), may hold values from 0 to 63; in each aligned block of 28 rows (0 to 27, 28 to 55, ..., all dimensions but the last counted through in order) no two rows name the same one
- sep_inv: float32 [8, 64, 128, 128], P('leaf', 'front')
- sep_couple: float32 [8, 64, 128, 128], P('leaf', 'front'), may hold values from -0.375 to 0.375
Outputs:
- x_leaf: float32 [8, 32, 229376], P('leaf', None, 'front')
- x_sep: float32 [8, 32, 8192], P('leaf', None, 'front')
Inputs may be any that keep to these rules, and one draw needn't show every extreme that they name: `update_rows`: within each leaf front the entries below 128 are distinct; the entries equal to 128 mark padded rows and come last in the front; some front has 64 padded rows. `update_owner`: at most 1 of the 28 leaf fronts held by one index of front have the same owner, and some index of front reaches 1.
All inputs are finite; a program needn't handle non-finite values.
Results may differ from a plain program's by a relative error of at most 0.0001.
Values sent between devices are 32-bit elements; how exact they have to be, the bound alone decides.
No kernel may reach another device: no remote copies, remote signals or barrier semaphores. Data moves between devices by JAX's collectives and lax.ppermute only.
A program may use at most 64 MiB of HBM per device.

v0:
```python
import jax
import jax.numpy as jnp
from jax import lax
from jax.sharding import PartitionSpec as P


def from_behind(value, axis, steps):
    count = lax.axis_size(axis)
    initial, last = (max(0, -steps), min(count, count - steps))
    return lax.ppermute(value, axis, [(source, source + steps) for source in range(initial, last)])


def apply_blocks(matrices, vectors):
    return jnp.einsum("bik,rbk->rbi", matrices, vectors, precision=lax.Precision.HIGHEST)


def apply_transposed(matrices, vectors):
    return jnp.einsum("bki,rbk->rbi", matrices, vectors, precision=lax.Precision.HIGHEST)


def apply_map(matrix, vectors):
    return jnp.einsum("ik,rk->ri", matrix, vectors, precision=lax.Precision.HIGHEST)


def apply_map_transposed(matrix, vectors):
    return jnp.einsum("ki,rk->ri", matrix, vectors, precision=lax.Precision.HIGHEST)


def per_device(
    rhs_leaf, rhs_sep, leaf_inv, leaf_update, update_rows, update_owner, sep_inv, sep_couple
):
    block_rows = leaf_inv.shape[-1]
    front_count = leaf_inv.shape[1]
    rhs_count = rhs_leaf.shape[1]
    fronts = lax.axis_size("front")
    groups = lax.axis_size("leaf")
    right_leaf = rhs_leaf[0].reshape(rhs_count, front_count, block_rows)
    leaf_y = apply_blocks(leaf_inv[0], right_leaf)
    updates = apply_blocks(leaf_update[0], leaf_y)
    row_index = update_rows[0]
    owners = update_owner[0]
    live_mask = row_index < block_rows
    updates = jnp.where(live_mask[None], updates, 0.0)
    local_rows = jnp.minimum(row_index, block_rows - 1)
    targets = owners * block_rows + local_rows
    dense_term = jnp.zeros((rhs_count, fronts * block_rows), jnp.float32)
    dense_term = dense_term.at[:, targets.reshape(-1)].add(updates.reshape(rhs_count, -1))
    collected = lax.psum_scatter(dense_term, "front", scatter_dimension=1, tiled=True)
    reduced = rhs_sep[0] - collected
    inv_block = sep_inv[0, 0]
    couple = sep_couple[0, 0]

    def forward_turn(turn_index, current):
        before = from_behind(current, "leaf", 1)
        return apply_map(inv_block, reduced - apply_map(couple, before))

    solved = lax.fori_loop(0, groups - 1, forward_turn, apply_map(inv_block, reduced))

    def backward_turn(turn_index, current):
        coupled = apply_map_transposed(couple, current)
        after = from_behind(coupled, "leaf", -1)
        return apply_map_transposed(inv_block, solved - after)

    x_sep = lax.fori_loop(0, groups - 1, backward_turn, apply_map_transposed(inv_block, solved))
    gathered = lax.all_gather(x_sep, "front", axis=1, tiled=True)
    picked = jnp.take(gathered, targets.reshape(-1), axis=1).reshape(
        rhs_count, front_count, block_rows
    )
    picked = jnp.where(live_mask[None], picked, 0.0)
    residue = leaf_y - apply_transposed(leaf_update[0], picked)
    x_leaf = apply_transposed(leaf_inv[0], residue)
    return (x_leaf.reshape(1, rhs_count, front_count * block_rows), x_sep[None])


def solution(mesh):
    placed = (
        P("leaf", None, "front"),
        P("leaf", None, "front"),
        P("leaf", "front", None, None),
        P("leaf", "front", None, None),
        P("leaf", "front", None),
        P("leaf", "front", None),
        P("leaf", "front", None, None),
        P("leaf", "front", None, None),
    )
    return jax.shard_map(
        per_device,
        mesh=mesh,
        in_specs=placed,
        out_specs=(P("leaf", None, "front"), P("leaf", None, "front")),
        check_vma=False,
    )
```

profile of v0, /device:TPU:1, one launch (start us, length us, event | category | flops | bytes accessed | tf_op | source)
XLA Modules:
  0.0 477.7 jit_solution(9119982957623492532)
XLA Ops:
  7.2 1.2 reshape_squeeze.3
  8.5 0.7 broadcast_compare_fusion
  9.2 4.4 fusion.14
  13.7 3.0 fusion.28
  16.7 1.8 copy.17
  18.6 23.2 %scatter_custom_fusion = f32[32,8192]{0,1:T(8,128)} fusion(s32[3584]{0:T(1024)S(1)} %fusion.41, f32[3584,32]{1,0:T(8,128)} %copy.17, f32[]{:T(128)} %constant.20.clone.1), kind=kCustom, calls=%fused_computation.5 | custom fusion | flops 114688 | bytes 1049088 | tf_op jit(solution)/shard_map/scatter-add | solution.py:47
  41.9 0.6 copy-done.6
  42.6 247.2 %reduce-scatter.2.cloned.1.call-done = f32[32,128]{0,1:T(8,128)} async-done(((f32[32,8192]{0,1:T(8,128)}), f32[32,128]{0,1:T(8,128)}) %reduce-scatter.2.cloned.1.call-update) | async-done | bytes 16400 | tf_op jit(solution)/shard_map/reduce_scatter | solution.py:48
  289.8 0.8 bitcast_subtract_fusion
  290.7 0.2 fusion.44
  291.0 42.7 %while.20 = (s32[]{:T(128)}, f32[32,128]{1,0:T(8,128)S(1)}, f32[128,128]{1,0:T(8,128)S(1)}, f32[32,128]{1,0:T(8,128)S(1)}, f32[128,128]{1,0:T(8,128)S(1)}, /*index=5*/s32[]{:T(128)}) while((s32[]{:T(128)}, f32[32,128]{1,0:T(8,128)S(1)}, f32[128,128]{1,0:T(8,128)S(1)}, f32[32,128]{1,0:T(8,128)S(1)}, f32[128,128]{1,0:T(8,128)S(1)}, ...), condition=%wide.region_3.4_spmd, body=%wide.region_2.3_spmd.sunk | while | flops 12587010 | bytes 278637 | solution.py:57
  291.0 8.4 %collective-permute-start = (f32[32,128]{1,0:T(8,128)S(1)}, f32[32,128]{1,0:T(8,128)S(1)}, u32[]{:S(2)}, u32[]{:S(2)}) collective-permute-start(f32[32,128]{1,0:T(8,128)S(1)} %get-tuple-element.157), channel_id=1, source_target_pairs={{0,64},{64,128},{128,192},{192,256},{256,320},{320,384},{384,448},... | collective-permute-start | bytes 49160 | tf_op jit(solution)/shard_map/while/body/eval_jaxpr/ppermute | solution.py:10
  299.4 0.8 collective-permute-done
  300.5 0.2 fusion.76
  300.7 4.2 collective-permute-start
  304.9 0.8 collective-permute-done
  306.2 4.2 collective-permute-start
  310.4 0.8 collective-permute-done
  311.7 4.2 collective-permute-start
  315.9 0.8 collective-permute-done
  317.2 4.2 collective-permute-start
  321.4 0.8 collective-permute-done
  322.7 4.2 collective-permute-start
  326.9 0.8 collective-permute-done
  328.2 4.2 collective-permute-start
  332.4 0.8 collective-permute-done
  333.9 38.3 %while.21 = (s32[]{:T(128)}, f32[32,128]{1,0:T(8,128)S(1)}, f32[128,128]{1,0:T(8,128)S(1)}, f32[32,128]{1,0:T(8,128)S(1)}, f32[128,128]{1,0:T(8,128)S(1)}, /*index=5*/s32[]{:T(128)}) while((s32[]{:T(128)}, f32[32,128]{1,0:T(8,128)S(1)}, f32[128,128]{1,0:T(8,128)S(1)}, f32[32,128]{1,0:T(8,128)S(1)}, f32[128,128]{1,0:T(8,128)S(1)}, ...), condition=%wide.region_5.6_spmd, body=%wide.region_4.5_spmd.sunk | while | flops 12587010 | bytes 278637 | solution.py:64
  334.0 1.9 collective-permute-start.1
  336.0 3.7 collective-permute-done.1
  340.0 1.9 collective-permute-start.1
  341.9 3.1 collective-permute-done.1
  345.4 1.9 collective-permute-start.1
  347.3 3.1 collective-permute-done.1
  350.8 1.9 collective-permute-start.1
  352.7 3.1 collective-permute-done.1
  356.2 1.9 collective-permute-start.1
  358.1 3.1 collective-permute-done.1
  361.6 1.9 collective-permute-start.1
  363.5 3.1 collective-permute-done.1
  367.0 1.9 collective-permute-start.1
  368.9 3.1 collective-permute-done.1
  372.2 0.7 copy.19
  373.1 79.6 %all-gather.2.cloned.1.call-done = f32[32,8192]{0,1:T(8,128)} async-done(((f32[32,128]{0,1:T(8,128)}), f32[32,8192]{0,1:T(8,128)}) %all-gather.2.cloned.1.call-update) | async-done | bytes 1048592 | tf_op jit(solution)/shard_map/all_gather | solution.py:65
  452.7 9.5 %gather_fusion = f32[3584,32]{1,0:T(8,128)} fusion(f32[32,8192]{0,1:T(8,128)} %all-gather.2.cloned.1.call-done, s32[4096]{0:T(1024)S(1)} %pad_clamp_fusion), kind=kCustom, calls=%fused_computation | custom fusion | bytes 931840 | tf_op jit(solution)/shard_map/jit(_take)/gather | solution.py:66
  462.3 5.8 %fusion.31 = f32[32,28,128]{2,0,1:T(8,128)S(1)} fusion(f32[32,28,128]{2,0,1:T(8,128)S(1)} %fusion.14, f32[1,28,128,128]{3,2,1,0:T(8,128)S(1)} %copy-done, f32[32,28,128]{0,2,1:T(8,128)} %bitcast.100, pred[28,128]{1,0:T(8,128)(4,1)S(1)} %compare_and_fusion, pred[28,128]{1,0:T(8,128)(4,1)S(1)} %bitcast.104), kind=kOutput, calls=%fused_computation.22 | convolution fusion | flops 176504832 | bytes 3218432 | tf_op jit(solution)/shard_map/bki,rbk->rbi/dot_general | solution.py:18
  468.0 1.7 fusion.17
  469.8 0.3 copy.20
  470.0 0.8 reshape.72
  (57 shorter events, 5.5 us)
Async XLA Ops:
  7.2 6.5 %copy-start = (f32[1,28,128,128]{3,2,1,0:T(8,128)S(1)}, f32[1,28,128,128]{3,2,1,0:T(8,128)}, u32[]{:S(2)}) copy-start(f32[1,28,128,128]{3,2,1,0:T(8,128)} %param.15) | copy-start | bytes 5505028
  7.2 282.7 %reduce-scatter.2.cloned.1.call-start = ((), (), s32[]{:S(2)}) async-start(), calls=%async_computation.1 | async-start | bytes 4259840 | tf_op jit(solution)/shard_map/reduce_scatter | solution.py:48
  16.6 1.9 copy-start.7
  16.6 1.9 copy-start.5
  41.8 0.7 copy-start.6
  41.8 248.9 %copy-start.1 = (f32[1,1,128,128]{3,2,1,0:T(8,128)S(1)}, f32[1,1,128,128]{3,2,1,0:T(8,128)}, u32[]{:S(2)}) copy-start(f32[1,1,128,128]{3,2,1,0:T(8,128)} %param.18) | copy-start | bytes 196612
  41.8 249.2 %copy-start.3 = (f32[1,1,128,128]{3,2,1,0:T(8,128)S(1)}, f32[1,1,128,128]{3,2,1,0:T(8,128)}, u32[]{:S(2)}) copy-start(f32[1,1,128,128]{3,2,1,0:T(8,128)} %param.19) | copy-start | bytes 196612
  41.8 410.9 %all-gather.2.cloned.1.call-start = ((), (), s32[]{:S(2)}) async-start(), calls=%async_computation.2 | async-start | bytes 4259840 | tf_op jit(solution)/shard_map/all_gather | solution.py:65
  291.0 9.2 %collective-permute-start = (f32[32,128]{1,0:T(8,128)S(1)}, f32[32,128]{1,0:T(8,128)S(1)}, u32[]{:S(2)}, u32[]{:S(2)}) collective-permute-start(f32[32,128]{1,0:T(8,128)S(1)} %get-tuple-element.157), channel_id=1, source_target_pairs={{0,64},{64,128},{128,192},{192,256},{256,320},{320,384},{384,448},... | collective-permute-start | bytes 49160 | tf_op jit(solution)/shard_map/while/body/eval_jaxpr/ppermute | solution.py:10
  300.7 5.1 %collective-permute-start = (f32[32,128]{1,0:T(8,128)S(1)}, f32[32,128]{1,0:T(8,128)S(1)}, u32[]{:S(2)}, u32[]{:S(2)}) collective-permute-start(f32[32,128]{1,0:T(8,128)S(1)} %get-tuple-element.157), channel_id=1, source_target_pairs={{0,64},{64,128},{128,192},{192,256},{256,320},{320,384},{384,448},... | collective-permute-start | bytes 49160 | tf_op jit(solution)/shard_map/while/body/eval_jaxpr/ppermute | solution.py:10
  306.2 5.1 %collective-permute-start = (f32[32,128]{1,0:T(8,128)S(1)}, f32[32,128]{1,0:T(8,128)S(1)}, u32[]{:S(2)}, u32[]{:S(2)}) collective-permute-start(f32[32,128]{1,0:T(8,128)S(1)} %get-tuple-element.157), channel_id=1, source_target_pairs={{0,64},{64,128},{128,192},{192,256},{256,320},{320,384},{384,448},... | collective-permute-start | bytes 49160 | tf_op jit(solution)/shard_map/while/body/eval_jaxpr/ppermute | solution.py:10
  311.7 5.1 %collective-permute-start = (f32[32,128]{1,0:T(8,128)S(1)}, f32[32,128]{1,0:T(8,128)S(1)}, u32[]{:S(2)}, u32[]{:S(2)}) collective-permute-start(f32[32,128]{1,0:T(8,128)S(1)} %get-tuple-element.157), channel_id=1, source_target_pairs={{0,64},{64,128},{128,192},{192,256},{256,320},{320,384},{384,448},... | collective-permute-start | bytes 49160 | tf_op jit(solution)/shard_map/while/body/eval_jaxpr/ppermute | solution.py:10
  317.2 5.1 %collective-permute-start = (f32[32,128]{1,0:T(8,128)S(1)}, f32[32,128]{1,0:T(8,128)S(1)}, u32[]{:S(2)}, u32[]{:S(2)}) collective-permute-start(f32[32,128]{1,0:T(8,128)S(1)} %get-tuple-element.157), channel_id=1, source_target_pairs={{0,64},{64,128},{128,192},{192,256},{256,320},{320,384},{384,448},... | collective-permute-start | bytes 49160 | tf_op jit(solution)/shard_map/while/body/eval_jaxpr/ppermute | solution.py:10
  322.7 5.1 %collective-permute-start = (f32[32,128]{1,0:T(8,128)S(1)}, f32[32,128]{1,0:T(8,128)S(1)}, u32[]{:S(2)}, u32[]{:S(2)}) collective-permute-start(f32[32,128]{1,0:T(8,128)S(1)} %get-tuple-element.157), channel_id=1, source_target_pairs={{0,64},{64,128},{128,192},{192,256},{256,320},{320,384},{384,448},... | collective-permute-start | bytes 49160 | tf_op jit(solution)/shard_map/while/body/eval_jaxpr/ppermute | solution.py:10
  328.2 5.1 %collective-permute-start = (f32[32,128]{1,0:T(8,128)S(1)}, f32[32,128]{1,0:T(8,128)S(1)}, u32[]{:S(2)}, u32[]{:S(2)}) collective-permute-start(f32[32,128]{1,0:T(8,128)S(1)} %get-tuple-element.157), channel_id=1, source_target_pairs={{0,64},{64,128},{128,192},{192,256},{256,320},{320,384},{384,448},... | collective-permute-start | bytes 49160 | tf_op jit(solution)/shard_map/while/body/eval_jaxpr/ppermute | solution.py:10
  334.0 5.6 %collective-permute-start.1 = (f32[32,128]{1,0:T(8,128)S(1)}, f32[32,128]{1,0:T(8,128)S(1)}, u32[]{:S(2)}, u32[]{:S(2)}) collective-permute-start(f32[32,128]{1,0:T(8,128)S(1)} %fusion.81), channel_id=1, source_target_pairs={{64,0},{128,64},{192,128},{256,192},{320,256},{384,320},{448,384},... | collective-permute-start | bytes 49160 | tf_op jit(solution)/shard_map/while/body/eval_jaxpr/ppermute | solution.py:10
  340.0 5.1 %collective-permute-start.1 = (f32[32,128]{1,0:T(8,128)S(1)}, f32[32,128]{1,0:T(8,128)S(1)}, u32[]{:S(2)}, u32[]{:S(2)}) collective-permute-start(f32[32,128]{1,0:T(8,128)S(1)} %fusion.81), channel_id=1, source_target_pairs={{64,0},{128,64},{192,128},{256,192},{320,256},{384,320},{448,384},... | collective-permute-start | bytes 49160 | tf_op jit(solution)/shard_map/while/body/eval_jaxpr/ppermute | solution.py:10
  345.4 5.1 %collective-permute-start.1 = (f32[32,128]{1,0:T(8,128)S(1)}, f32[32,128]{1,0:T(8,128)S(1)}, u32[]{:S(2)}, u32[]{:S(2)}) collective-permute-start(f32[32,128]{1,0:T(8,128)S(1)} %fusion.81), channel_id=1, source_target_pairs={{64,0},{128,64},{192,128},{256,192},{320,256},{384,320},{448,384},... | collective-permute-start | bytes 49160 | tf_op jit(solution)/shard_map/while/body/eval_jaxpr/ppermute | solution.py:10
  350.8 5.1 %collective-permute-start.1 = (f32[32,128]{1,0:T(8,128)S(1)}, f32[32,128]{1,0:T(8,128)S(1)}, u32[]{:S(2)}, u32[]{:S(2)}) collective-permute-start(f32[32,128]{1,0:T(8,128)S(1)} %fusion.81), channel_id=1, source_target_pairs={{64,0},{128,64},{192,128},{256,192},{320,256},{384,320},{448,384},... | collective-permute-start | bytes 49160 | tf_op jit(solution)/shard_map/while/body/eval_jaxpr/ppermute | solution.py:10
  356.2 5.1 %collective-permute-start.1 = (f32[32,128]{1,0:T(8,128)S(1)}, f32[32,128]{1,0:T(8,128)S(1)}, u32[]{:S(2)}, u32[]{:S(2)}) collective-permute-start(f32[32,128]{1,0:T(8,128)S(1)} %fusion.81), channel_id=1, source_target_pairs={{64,0},{128,64},{192,128},{256,192},{320,256},{384,320},{448,384},... | collective-permute-start | bytes 49160 | tf_op jit(solution)/shard_map/while/body/eval_jaxpr/ppermute | solution.py:10
  361.6 5.1 %collective-permute-start.1 = (f32[32,128]{1,0:T(8,128)S(1)}, f32[32,128]{1,0:T(8,128)S(1)}, u32[]{:S(2)}, u32[]{:S(2)}) collective-permute-start(f32[32,128]{1,0:T(8,128)S(1)} %fusion.81), channel_id=1, source_target_pairs={{64,0},{128,64},{192,128},{256,192},{320,256},{384,320},{448,384},... | collective-permute-start | bytes 49160 | tf_op jit(solution)/shard_map/while/body/eval_jaxpr/ppermute | solution.py:10
  367.0 5.1 %collective-permute-start.1 = (f32[32,128]{1,0:T(8,128)S(1)}, f32[32,128]{1,0:T(8,128)S(1)}, u32[]{:S(2)}, u32[]{:S(2)}) collective-permute-start(f32[32,128]{1,0:T(8,128)S(1)} %fusion.81), channel_id=1, source_target_pairs={{64,0},{128,64},{192,128},{256,192},{320,256},{384,320},{448,384},... | collective-permute-start | bytes 49160 | tf_op jit(solution)/shard_map/while/body/eval_jaxpr/ppermute | solution.py:10
  372.2 90.0 %copy-start.4 = (f32[32,128]{1,0:T(8,128)}, f32[32,128]{1,0:T(8,128)S(1)}, u32[]{:S(2)}) copy-start(f32[32,128]{1,0:T(8,128)S(1)} %get-tuple-element.57) | copy-start | bytes 49156
  462.3 5.8 %copy-start.2 = (f32[1,28,128,128]{3,2,1,0:T(8,128)S(1)}, f32[1,28,128,128]{3,2,1,0:T(8,128)}, u32[]{:S(2)}) copy-start(f32[1,28,128,128]{3,2,1,0:T(8,128)} %param.14) | copy-start | bytes 5505028
Sparse Core Ops, SparseCore 0:
  42.0 247.8 reduce-scatter.1
  373.1 79.5 all-gather.1
where the time goes:
time: 481 us; the launch traced here: 478 us
  waiting for transfers between devices  355 us (74%)
  starting transfers between devices  47.1 us (10%)
  other arithmetic  24.9 us (5%)
  matrix products  20.3 us (4%)
  local copies, waits for them, and re-layouts  15.4 us (3%)
  between operations  14.2 us (3%)
    reduce_scatter x1, waiting for transfers between devices, per_device(): lax.psum_scatter(dense_term, 'front', scatter_dimension=1, tiled=True)  247 us
    all_gather x1, waiting for transfers between devices, per_device(): gathered = lax.all_gather(x_sep, 'front', axis=1, tiled=True)  79.6 us
    ppermute x14, starting transfers between devices, from_behind(): lax.ppermute(value, axis, [(source, source + steps) for source in range(i...  47.1 us
    ppermute x14, waiting for transfers between devices, from_behind(): lax.ppermute(value, axis, [(source, source + steps) for source in range(i...  28.4 us
    scatter-add x1, other arithmetic, per_device(): dense_term.at[:, targets.reshape(-1)].add(updates.reshape(rhs_count, -1))  23.2 us
  transfers between devices with their start and end apart: 16, of which 16 were waited for; matrix products, arithmetic and copies ran while one was open for 0% of the time, Pallas kernels for 0%

commit v1 on v0

v1 whole, which is shorter than its diff:
```python
import jax
import jax.numpy as jnp
from jax import lax
from jax.experimental import pallas as pl
from jax.experimental.pallas import tpu as pltpu
from jax.sharding import PartitionSpec as P

NT = (((1,), (1,)), ((), ()))
NN = (((1,), (0,)), ((), ()))


def split(value):
    high = value.astype(jnp.bfloat16)
    low = (value - high.astype(jnp.float32)).astype(jnp.bfloat16)
    return high, low


def product(left, right, dims):
    rows = left.shape[0]
    left_high, left_low = split(left)
    right_high, right_low = split(right)
    both = lax.dot_general(
        jnp.concatenate([left_high, left_low], axis=0), right_high, dims, preferred_element_type=jnp.float32
    )
    cross = lax.dot_general(left_high, right_low, dims, preferred_element_type=jnp.float32)
    return both[:rows] + (both[rows:] + cross)


def select(left, chosen, dims):
    rows = left.shape[0]
    both = lax.dot_general(
        jnp.concatenate(split(left), axis=0), chosen, dims, preferred_element_type=jnp.float32
    )
    return both[:rows] + both[rows:]


def chosen_rows(row_index, block_rows):
    separator_row = lax.broadcasted_iota(jnp.int32, (block_rows, block_rows), 0)
    return jnp.where(separator_row == row_index, 1.0, 0.0).astype(jnp.bfloat16)


def leaf_forward(owner_ref, rhs_ref, inv_ref, update_ref, rows_ref, y_ref, dense_ref):
    step = pl.program_id(0)
    count, block_rows, _ = inv_ref.shape

    @pl.when(step == 0)
    def _():
        dense_ref[...] = jnp.zeros_like(dense_ref)

    for front in range(count):
        right = rhs_ref[:, front * block_rows : (front + 1) * block_rows]
        leaf_y = product(right, inv_ref[front], NT)
        y_ref[front] = leaf_y
        update = product(leaf_y, update_ref[front], NT)
        placed = select(update, chosen_rows(rows_ref[front], block_rows), NT)
        dense_ref[owner_ref[step * count + front]] = placed


def leaf_backward(owner_ref, x_ref, y_ref, inv_ref, update_ref, rows_ref, out_ref):
    step = pl.program_id(0)
    count, block_rows, _ = inv_ref.shape
    for front in range(count):
        owned = x_ref[owner_ref[step * count + front]]
        picked = select(owned, chosen_rows(rows_ref[front], block_rows), NN)
        residue = y_ref[front] - product(picked, update_ref[front], NN)
        out_ref[:, front * block_rows : (front + 1) * block_rows] = product(residue, inv_ref[front], NN)


def chain(group_ref, reduced_ref, blocks_ref, x_ref, y_scratch, x_scratch):
    groups = reduced_ref.shape[0]
    for group in range(groups):
        right = reduced_ref[group]
        if group:
            right = right - product(y_scratch[group - 1], blocks_ref[group, 1], NT)
        y_scratch[group] = product(right, blocks_ref[group, 0], NT)
    for group in range(groups - 1, -1, -1):
        right = y_scratch[group]
        if group < groups - 1:
            right = right - product(x_scratch[group + 1], blocks_ref[group + 1, 1], NN)
        x_scratch[group] = product(right, blocks_ref[group, 0], NN)
    x_ref[...] = x_scratch[group_ref[0]]


PER_STEP = 7
VMEM = pl.BlockSpec(memory_space=pltpu.VMEM)
SMEM = pl.BlockSpec(memory_space=pltpu.SMEM)
PARAMS = pltpu.CompilerParams(vmem_limit_bytes=32 << 20)


def per_device(
    rhs_leaf, rhs_sep, leaf_inv, leaf_update, update_rows, update_owner, sep_inv, sep_couple
):
    front_count, block_rows = leaf_inv.shape[1], leaf_inv.shape[3]
    rhs_count = rhs_leaf.shape[1]
    groups = lax.axis_size("leaf")
    fronts = lax.axis_size("front")
    right_leaf, inverse, coupling = rhs_leaf[0], leaf_inv[0], leaf_update[0]
    rows = update_rows.reshape(front_count, 1, block_rows)
    owners = update_owner.reshape(front_count)

    blocks = jnp.concatenate([sep_inv, sep_couple], axis=1)
    blocks = lax.all_gather(blocks, "leaf", axis=0, tiled=True)

    matrices = pl.BlockSpec((PER_STEP, block_rows, block_rows), lambda s: (s, 0, 0))
    lines = pl.BlockSpec((PER_STEP, 1, block_rows), lambda s: (s, 0, 0))
    vectors = pl.BlockSpec((PER_STEP, rhs_count, block_rows), lambda s: (s, 0, 0))
    columns = pl.BlockSpec((rhs_count, PER_STEP * block_rows), lambda s: (0, s))
    whole = pl.BlockSpec((fronts, rhs_count, block_rows), lambda s: (0, 0, 0))
    leaf_y, dense = pl.pallas_call(
        leaf_forward,
        grid=(front_count // PER_STEP,),
        in_specs=[SMEM, columns, matrices, matrices, lines],
        out_specs=[vectors, whole],
        out_shape=[
            jax.ShapeDtypeStruct((front_count, rhs_count, block_rows), jnp.float32),
            jax.ShapeDtypeStruct((fronts, rhs_count, block_rows), jnp.float32),
        ],
        compiler_params=PARAMS,
        name="leaf_forward",
    )(owners, right_leaf, inverse, coupling, rows)

    received = lax.all_to_all(dense, "front", 0, 0, tiled=True)
    reduced = rhs_sep[0] - jnp.sum(received, axis=0)
    reduced = lax.all_gather(reduced, "leaf", axis=0)
    x_sep = pl.pallas_call(
        chain,
        in_specs=[SMEM, VMEM, VMEM],
        out_specs=VMEM,
        out_shape=jax.ShapeDtypeStruct((rhs_count, block_rows), jnp.float32),
        scratch_shapes=[
            pltpu.VMEM((groups, rhs_count, block_rows), jnp.float32),
            pltpu.VMEM((groups, rhs_count, block_rows), jnp.float32),
        ],
        compiler_params=PARAMS,
        name="chain",
    )(lax.axis_index("leaf").reshape(1), reduced, blocks)

    copies = jnp.broadcast_to(x_sep[None], (fronts, rhs_count, block_rows))
    gathered = lax.all_to_all(copies, "front", 0, 0, tiled=True)
    x_leaf = pl.pallas_call(
        leaf_backward,
        grid=(front_count // PER_STEP,),
        in_specs=[SMEM, whole, vectors, matrices, matrices, lines],
        out_specs=columns,
        out_shape=jax.ShapeDtypeStruct((rhs_count, front_count * block_rows), jnp.float32),
        compiler_params=PARAMS,
        name="leaf_backward",
    )(owners, gathered, leaf_y, inverse, coupling, rows)
    return (x_leaf[None], x_sep[None])


def solution(mesh):
    placed = (
        P("leaf", None, "front"),
        P("leaf", None, "front"),
        P("leaf", "front", None, None),
        P("leaf", "front", None, None),
        P("leaf", "front", None),
        P("leaf", "front", None),
        P("leaf", "front", None, None),
        P("leaf", "front", None, None),
    )
    return jax.shard_map(
        per_device,
        mesh=mesh,
        in_specs=placed,
        out_specs=(P("leaf", None, "front"), P("leaf", None, "front")),
        check_vma=False,
    )
```

time: 481 us -> 139 us (0.29)
  waiting for transfers between devices: 355 us -> 26 us
  blocking collectives: 0 us -> 50.2 us
  starting transfers between devices: 47.1 us -> 17.3 us
  other arithmetic: 24.9 us -> 0.77 us
  Pallas kernels: 0 us -> 20.4 us
  matrix products: 20.3 us -> 0 us
  local copies, waits for them, and re-layouts: 15.4 us -> 7.59 us
    reduce_scatter x1 -> x0, waiting for transfers between devices: 247 us -> none  [per_device(): lax.psum_scatter(dense_term, 'front', scatter_dimension=1, tiled=True)]
    all_gather x1, waiting for transfers between devices: 79.6 us -> 0.01 us  [per_device(): blocks = lax.all_gather(blocks, 'leaf', axis=0, tiled=True)]
    ppermute x14 -> x0, starting transfers between devices: 47.1 us -> none  [from_behind(): lax.ppermute(value, axis, [(source, source + steps) for source in range(i...]
    all_to_all x0 -> x1, blocking collectives: none -> 33.4 us  [per_device(): gathered = lax.all_to_all(copies, 'front', 0, 0, tiled=True)]
    ppermute x14 -> x0, waiting for transfers between devices: 28.4 us -> none  [from_behind(): lax.ppermute(value, axis, [(source, source + steps) for source in range(i...]
    all_to_all x0 -> x1, waiting for transfers between devices: none -> 26 us  [per_device(): received = lax.all_to_all(dense, 'front', 0, 0, tiled=True)]
    scatter-add x1 -> x0, other arithmetic: 23.2 us -> none  [per_device(): dense_term.at[:, targets.reshape(-1)].add(updates.reshape(rhs_count, -1))]
    pallas_call x0 -> x3, Pallas kernels: none -> 20.4 us  [the longest x1 8.62 us: per_device(): pl.pallas_call(leaf_forward, grid=(front_count // PER_STEP,), in_specs=[S...]
  transfers between devices with their start and end apart: 16 -> 2, of which waited for: 16 -> 1; matrix products, arithmetic and copies ran while one was open for 0% -> 1% of each run, Pallas kernels for 0% -> 0%
where the time goes in v1:
time: 139 us; the launch traced here: 136 us
  blocking collectives  50.2 us (36%)
  waiting for transfers between devices  26 us (19%)
  Pallas kernels  20.4 us (15%)
  starting transfers between devices  17.3 us (12%)
  between operations  14.1 us (10%)
  local copies, waits for them, and re-layouts  7.59 us (5%)
    all_to_all x1, blocking collectives, per_device(): gathered = lax.all_to_all(copies, 'front', 0, 0, tiled=True)  33.4 us
    all_to_all x1, waiting for transfers between devices, per_device(): received = lax.all_to_all(dense, 'front', 0, 0, tiled=True)  26 us
    all_to_all x1, starting transfers between devices, per_device(): received = lax.all_to_all(dense, 'front', 0, 0, tiled=True)  17.3 us
    all_gather x1, blocking collectives, per_device(): reduced = lax.all_gather(reduced, 'leaf', axis=0)  16.8 us
    pallas_call x1, Pallas kernels, per_device(): pl.pallas_call(leaf_forward, grid=(front_count // PER_STEP,), in_specs=[S...  8.62 us
    pallas_call x1, Pallas kernels, per_device(): pl.pallas_call(leaf_backward, grid=(front_count // PER_STEP,), in_specs=[...  6.93 us
    unnamed x26, local copies, waits for them, and re-layouts  6.63 us
    pallas_call x1, Pallas kernels, per_device(): pl.pallas_call(chain, in_specs=[SMEM, VMEM, VMEM], out_specs=VMEM, out_sh...  4.89 us
  transfers between devices with their start and end apart: 2, of which 1 were waited for; matrix products, arithmetic and copies ran while one was open for 1% of the time, Pallas kernels for 0%

profile of v1, /device:TPU:1, one launch (start us, length us, event | category | flops | bytes accessed | tf_op | source)
XLA Modules:
  0.0 136.4 jit_solution(11924478081058917218)
XLA Ops:
  7.2 0.0 copy-start
  7.2 1.5 %copy-done = f32[1,28,128,128]{3,2,1,0:T(8,128)S(1)} copy-done((f32[1,28,128,128]{3,2,1,0:T(8,128)S(1)}, f32[1,28,128,128]{3,2,1,0:T(8,128)}, u32[]{:S(2)}) %copy-start) | copy-done | bytes 1835032
  8.7 0.0 copy-start.2
  8.7 1.5 %copy-done.2 = f32[1,28,128,128]{3,2,1,0:T(8,128)S(1)} copy-done((f32[1,28,128,128]{3,2,1,0:T(8,128)S(1)}, f32[1,28,128,128]{3,2,1,0:T(8,128)}, u32[]{:S(2)}) %copy-start.2) | copy-done | bytes 1835032
  10.2 0.0 copy-start.5
  10.2 1.0 copy-done.5
  11.2 0.0 copy-start.6
  11.2 0.7 copy-done.6
  11.9 0.0 copy-start.8
  11.9 0.7 copy-done.8
  12.6 8.6 %leaf_forward.1 = (f32[28,32,128]{2,1,0:T(8,128)S(1)}, f32[64,32,128]{2,1,0:T(8,128)}) custom-call(s32[28]{0:T(128)S(1)} %bitcast.17, f32[32,3584]{1,0:T(8,128)S(1)} %bitcast.14, f32[28,128,128]{2,1,0:T(8,128)S(1)} %bitcast.10, f32[28,128,128]{2,1,0:T(8,128)S(1)} %bitcast.12, s32[28,1,128]{2,1,0:T(1,128)S(1)} %bitcast.15), custom_call_target="tpu_custom_call" | custom-call | tf_op jit(solution)/shard_map/leaf_forward/pallas_call | solution.py:109
  21.2 0.0 copy-start.10
  21.2 0.0 copy-start.11
  21.2 0.0 copy-start.12
  21.2 17.3 %all-to-all-start = ((f32[64,32,128]{2,1,0:T(8,128)}), f32[64,32,128]{2,1,0:T(8,128)S(1)}, u32[]{:S(2)}, u32[]{:S(2)}) async-start(f32[64,32,128]{2,1,0:T(8,128)} %get-tuple-element.4), calls=%async_computation | async-start | bytes 2097152 | tf_op jit(solution)/shard_map/all_to_all | solution.py:122
  38.5 0.0 all-gather.2.cloned.1.call-start
  38.5 0.0 copy-done.10
  38.5 0.0 copy-done.11
  38.5 0.7 pad_maximum_fusion
  39.2 0.0 all-gather.2.cloned.1.call-update
  39.2 26.0 %all-to-all-done = f32[64,32,128]{2,1,0:T(8,128)S(1)} async-done(((f32[64,32,128]{2,1,0:T(8,128)}), f32[64,32,128]{2,1,0:T(8,128)S(1)}, u32[]{:S(2)}, u32[]{:S(2)}) %all-to-all-start) | async-done | bytes 1048608 | tf_op jit(solution)/shard_map/all_to_all | solution.py:122
  65.2 0.1 reduce_sum.11
  65.3 0.0 copy-done.12
  65.3 16.8 %all_gather.7.reduced_ref = f32[8,32,128]{2,1,0:T(8,128)S(1)} all-gather(f32[1,32,128]{2,1,0:T(8,128)S(1)} %bitcast_subtract_fusion), channel_id=1, replica_groups=mesh['leaf'=8,'front'=64] {'leaf'}, dimensions={0}, use_global_device_ids=true | all-gather | bytes 147456 | tf_op jit(solution)/shard_map/all_gather | solution.py:124
  82.1 0.0 all-gather.2.cloned.1.call-done.blocks_ref
  82.1 0.0 copy-start.4
  82.1 1.2 copy-done.4
  83.3 0.0 copy-start.3
  83.3 4.9 %chain.1 = f32[32,128]{1,0:T(8,128)} custom-call(s32[1]{0:T(128)} %bitcast.1.group_ref, f32[8,32,128]{2,1,0:T(8,128)S(1)} %all_gather.7.reduced_ref, f32[8,2,128,128]{3,2,1,0:T(8,128)S(1)} %copy-done.4), custom_call_target="tpu_custom_call" | custom-call | tf_op jit(solution)/shard_map/chain/pallas_call | solution.py:125
  88.2 0.0 copy-start.1
  88.2 0.0 copy-start.7
  88.2 0.0 copy-start.9
  88.2 1.0 broadcast_in_dim.12
  89.2 33.4 %all_to_all.10.x_ref = f32[64,32,128]{2,1,0:T(8,128)S(1)} all-to-all(f32[64,32,128]{2,1,0:T(8,128)S(1)} %broadcast_in_dim.12), channel_id=1, replica_groups=mesh['leaf'=8,'front'=64] {'front'}, dimensions={0} | all-to-all | bytes 2097152 | tf_op jit(solution)/shard_map/all_to_all | solution.py:139
  122.6 0.0 copy-done.3
  122.6 0.0 copy-done.1
  122.6 0.0 copy-done.7
  122.6 0.0 copy-done.9
  122.6 6.9 %leaf_backward.1 = f32[32,3584]{1,0:T(8,128)} custom-call(s32[28]{0:T(128)S(1)} %bitcast.18, f32[64,32,128]{2,1,0:T(8,128)S(1)} %all_to_all.10.x_ref, f32[28,32,128]{2,1,0:T(8,128)S(1)} %get-tuple-element.5.y_ref, f32[28,128,128]{2,1,0:T(8,128)S(1)} %bitcast.11, f32[28,128,128]{2,1,0:T(8,128)S(1)} %bitcast.13, s32[28,1,128]{2,1,0:T(1,128)S(1)} %bitcast.16), custom_call_target="tpu_custom_call" | custom-call | tf_op jit(solution)/shard_map/leaf_backward/pallas_call | solution.py:140
  (1 shorter events, 0.0 us)
Async XLA Ops:
  7.2 1.5 %copy-start = (f32[1,28,128,128]{3,2,1,0:T(8,128)S(1)}, f32[1,28,128,128]{3,2,1,0:T(8,128)}, u32[]{:S(2)}) copy-start(f32[1,28,128,128]{3,2,1,0:T(8,128)} %param.10) | copy-start | bytes 5505028
  8.7 1.5 %copy-start.2 = (f32[1,28,128,128]{3,2,1,0:T(8,128)S(1)}, f32[1,28,128,128]{3,2,1,0:T(8,128)}, u32[]{:S(2)}) copy-start(f32[1,28,128,128]{3,2,1,0:T(8,128)} %param.11) | copy-start | bytes 5505028
  10.2 1.0 copy-start.5
  11.2 0.7 copy-start.6
  11.9 0.7 copy-start.8
  21.2 17.3 %copy-start.10 = (f32[1,1,128,128]{3,2,1,0:T(8,128)S(1)}, f32[1,1,128,128]{3,2,1,0:T(8,128)}, u32[]{:S(2)}) copy-start(f32[1,1,128,128]{3,2,1,0:T(8,128)} %param.15) | copy-start | bytes 196612
  21.2 17.3 %copy-start.11 = (f32[1,1,128,128]{3,2,1,0:T(8,128)S(1)}, f32[1,1,128,128]{3,2,1,0:T(8,128)}, u32[]{:S(2)}) copy-start(f32[1,1,128,128]{3,2,1,0:T(8,128)} %param.14) | copy-start | bytes 196612
  21.2 44.1 %copy-start.12 = (f32[1,32,128]{2,1,0:T(8,128)S(1)}, f32[1,32,128]{2,1,0:T(8,128)}, u32[]{:S(2)}) copy-start(f32[1,32,128]{2,1,0:T(8,128)} %param.9) | copy-start | bytes 49156
  21.2 44.0 %all-to-all-start = ((f32[64,32,128]{2,1,0:T(8,128)}), f32[64,32,128]{2,1,0:T(8,128)S(1)}, u32[]{:S(2)}, u32[]{:S(2)}) async-start(f32[64,32,128]{2,1,0:T(8,128)} %get-tuple-element.4), calls=%async_computation | async-start | bytes 2097152 | tf_op jit(solution)/shard_map/all_to_all | solution.py:122
  38.5 43.6 %all-gather.2.cloned.1.call-start = ((), (), s32[]{:S(2)}) async-start(), calls=%async_computation.2 | async-start | bytes 1179648 | tf_op jit(solution)/shard_map/all_gather | solution.py:102
  82.1 1.2 copy-start.4
  83.3 39.2 %copy-start.3 = (f32[1,28,128,128]{3,2,1,0:T(8,128)S(1)}, f32[1,28,128,128]{3,2,1,0:T(8,128)}, u32[]{:S(2)}) copy-start(f32[1,28,128,128]{3,2,1,0:T(8,128)} %param.11) | copy-start | bytes 5505028
  88.2 34.4 %copy-start.1 = (f32[1,28,128,128]{3,2,1,0:T(8,128)S(1)}, f32[1,28,128,128]{3,2,1,0:T(8,128)}, u32[]{:S(2)}) copy-start(f32[1,28,128,128]{3,2,1,0:T(8,128)} %param.10) | copy-start | bytes 5505028
  88.2 34.4 %copy-start.7 = (s32[1,28,128]{2,0,1:T(1,128)S(1)}, s32[1,28,128]{2,0,1:T(1,128)}, u32[]{:S(2)}) copy-start(s32[1,28,128]{2,0,1:T(1,128)} %param.12) | copy-start | bytes 43012
  88.2 34.4 %copy-start.9 = (s32[1,28,1]{1,2,0:T(1,128)S(1)}, s32[1,28,1]{1,2,0:T(1,128)}, u32[]{:S(2)}) copy-start(s32[1,28,1]{1,2,0:T(1,128)} %param.13) | copy-start | bytes 340
Sparse Core Ops, SparseCore 0:
  42.0 30.1 all-gather.1

commit v2 on v1

v2 whole, which is shorter than its diff:
```python
import jax
import jax.numpy as jnp
from jax import lax
from jax.experimental import pallas as pl
from jax.experimental.pallas import tpu as pltpu
from jax.sharding import PartitionSpec as P

NT = (((1,), (1,)), ((), ()))
NN = (((1,), (0,)), ((), ()))


def split(value):
    high = value.astype(jnp.bfloat16)
    low = (value - high.astype(jnp.float32)).astype(jnp.bfloat16)
    return high, low


def product(left, right, dims):
    rows = left.shape[0]
    left_high, left_low = split(left)
    right_high, right_low = split(right)
    both = lax.dot_general(
        jnp.concatenate([left_high, left_low], axis=0), right_high, dims, preferred_element_type=jnp.float32
    )
    cross = lax.dot_general(left_high, right_low, dims, preferred_element_type=jnp.float32)
    return both[:rows] + (both[rows:] + cross)


def select(left, chosen, dims):
    rows = left.shape[0]
    both = lax.dot_general(
        jnp.concatenate(split(left), axis=0), chosen, dims, preferred_element_type=jnp.float32
    )
    return both[:rows] + both[rows:]


def chosen_rows(row_index, block_rows):
    separator_row = lax.broadcasted_iota(jnp.int32, (block_rows, block_rows), 0)
    return jnp.where(separator_row == row_index, 1.0, 0.0).astype(jnp.bfloat16)


def coupled_inverse(inv_ref, couple_ref, out_ref):
    coupled = product(inv_ref[...], couple_ref[...], NN)
    for copy in range(out_ref.shape[0]):
        out_ref[copy] = coupled


def leaf_forward(owner_ref, rhs_ref, inv_ref, update_ref, rows_ref, y_ref, dense_ref):
    step = pl.program_id(0)
    count, block_rows, _ = inv_ref.shape

    @pl.when(step == 0)
    def _():
        dense_ref[...] = jnp.zeros_like(dense_ref)

    for front in range(count):
        right = rhs_ref[:, front * block_rows : (front + 1) * block_rows]
        leaf_y = product(right, inv_ref[front], NT)
        y_ref[front] = leaf_y
        update = product(leaf_y, update_ref[front], NT)
        placed = select(update, chosen_rows(rows_ref[front], block_rows), NT)
        dense_ref[owner_ref[step * count + front]] = placed


def leaf_prepare(y_ref, inv_ref, update_ref, rows_ref, own_ref, high_ref, low_ref):
    count, block_rows, _ = inv_ref.shape
    for front in range(count):
        inverse = inv_ref[front]
        own_ref[front] = product(y_ref[front], inverse, NN)
        mapped_high, mapped_low = split(product(update_ref[front], inverse, NN))
        chosen = chosen_rows(rows_ref[front], block_rows)
        placed = lax.dot_general(chosen, mapped_high, NN, preferred_element_type=jnp.float32)
        placed = placed + lax.dot_general(chosen, mapped_low, NN, preferred_element_type=jnp.float32)
        high_ref[front], low_ref[front] = split(placed)


def reduce_right(received_ref, rhs_ref, inv_ref, out_ref):
    reduced = rhs_ref[...] - jnp.sum(received_ref[...], axis=0)
    solved = product(reduced, inv_ref[...], NT)
    for copy in range(out_ref.shape[0]):
        out_ref[copy] = solved


def chain(group_ref, right_ref, coupled_ref, inv_ref, x_ref, copies_ref, scratch):
    groups = right_ref.shape[0]
    scratch[0] = right_ref[0]
    for group in range(1, groups):
        scratch[group] = right_ref[group] - product(scratch[group - 1], coupled_ref[group], NT)
    for group in range(groups - 1, 0, -1):
        scratch[group - 1] = scratch[group - 1] - product(scratch[group], coupled_ref[group], NN)
    x_sep = product(scratch[group_ref[0]], inv_ref[...], NN)
    x_ref[...] = x_sep
    for copy in range(copies_ref.shape[0]):
        copies_ref[copy] = x_sep


def leaf_backward(owner_ref, x_ref, own_ref, high_ref, low_ref, out_ref):
    count, rows, block_rows = own_ref.shape
    for front in range(count):
        owned_high, owned_low = split(x_ref[owner_ref[front]])
        both = lax.dot_general(
            jnp.concatenate([owned_high, owned_low], axis=0),
            high_ref[front],
            NN,
            preferred_element_type=jnp.float32,
        )
        cross = lax.dot_general(owned_high, low_ref[front], NN, preferred_element_type=jnp.float32)
        mapped = both[:rows] + (both[rows:] + cross)
        out_ref[:, front * block_rows : (front + 1) * block_rows] = own_ref[front] - mapped


PER_STEP = 7
VMEM = pl.BlockSpec(memory_space=pltpu.VMEM)
SMEM = pl.BlockSpec(memory_space=pltpu.SMEM)
PARAMS = pltpu.CompilerParams(vmem_limit_bytes=32 << 20)


def floats(*shape):
    return jax.ShapeDtypeStruct(shape, jnp.float32)


def call(body, in_specs, out_specs, out_shape, **rest):
    return pl.pallas_call(
        body,
        in_specs=in_specs,
        out_specs=out_specs,
        out_shape=out_shape,
        compiler_params=PARAMS,
        name=body.__name__,
        **rest,
    )


def per_device(
    rhs_leaf, rhs_sep, leaf_inv, leaf_update, update_rows, update_owner, sep_inv, sep_couple
):
    front_count, size = leaf_inv.shape[1], leaf_inv.shape[3]
    width = rhs_leaf.shape[1]
    groups = lax.axis_size("leaf")
    fronts = lax.axis_size("front")
    right_leaf = rhs_leaf[0]
    inverse = pltpu.with_memory_space_constraint(leaf_inv[0], pltpu.HBM)
    coupling = pltpu.with_memory_space_constraint(leaf_update[0], pltpu.HBM)
    rows = update_rows.reshape(front_count, 1, size)
    owners = update_owner.reshape(front_count)
    separator_inverse, separator_couple = sep_inv[0, 0], sep_couple[0, 0]

    matrices = pl.BlockSpec((PER_STEP, size, size), lambda s: (s, 0, 0))
    lines = pl.BlockSpec((PER_STEP, 1, size), lambda s: (s, 0, 0))
    vectors = pl.BlockSpec((PER_STEP, width, size), lambda s: (s, 0, 0))
    columns = pl.BlockSpec((width, PER_STEP * size), lambda s: (0, s))
    whole = pl.BlockSpec((fronts, width, size), lambda s: (0, 0, 0))
    steps = (front_count // PER_STEP,)

    coupled = call(coupled_inverse, [VMEM, VMEM], VMEM, floats(groups, size, size))(
        separator_inverse, separator_couple
    )
    coupled = lax.all_to_all(coupled, "leaf", 0, 0, tiled=True)

    leaf_y, dense = call(
        leaf_forward,
        [SMEM, columns, matrices, matrices, lines],
        [vectors, whole],
        [floats(front_count, width, size), floats(fronts, width, size)],
        grid=steps,
    )(owners, right_leaf, inverse, coupling, rows)
    dense, coupled = lax.optimization_barrier((dense, coupled))
    received = lax.all_to_all(dense, "front", 0, 0, tiled=True)
    halves = jax.ShapeDtypeStruct((front_count, size, size), jnp.bfloat16)
    own, high, low = call(
        leaf_prepare,
        [vectors, matrices, matrices, lines],
        [vectors, matrices, matrices],
        [floats(front_count, width, size), halves, halves],
        grid=steps,
    )(leaf_y, inverse, coupling, rows)

    right = call(reduce_right, [VMEM, VMEM, VMEM], VMEM, floats(groups, width, size))(
        received, rhs_sep[0], separator_inverse
    )
    right = lax.all_to_all(right, "leaf", 0, 0, tiled=True)
    x_sep, copies = call(
        chain,
        [SMEM, VMEM, VMEM, VMEM],
        [VMEM, VMEM],
        [floats(width, size), floats(fronts, width, size)],
        scratch_shapes=[pltpu.VMEM((groups, width, size), jnp.float32)],
    )(lax.axis_index("leaf").reshape(1), right, coupled, separator_inverse)
    gathered = lax.all_to_all(copies, "front", 0, 0, tiled=True)
    x_leaf = call(
        leaf_backward, [SMEM, VMEM, VMEM, VMEM, VMEM], VMEM, floats(width, front_count * size)
    )(owners, gathered, own, high, low)
    return (x_leaf[None], x_sep[None])


def solution(mesh):
    placed = (
        P("leaf", None, "front"),
        P("leaf", None, "front"),
        P("leaf", "front", None, None),
        P("leaf", "front", None, None),
        P("leaf", "front", None),
        P("leaf", "front", None),
        P("leaf", "front", None, None),
        P("leaf", "front", None, None),
    )
    return jax.shard_map(
        per_device,
        mesh=mesh,
        in_specs=placed,
        out_specs=(P("leaf", None, "front"), P("leaf", None, "front")),
        check_vma=False,
    )
```

time: 139 us -> 119 us (0.86)
  the two profiles are of different devices: /device:TPU:1 before, /device:TPU:16 now
where the time goes in v2:
time: 119 us
  blocking collectives  46.9 us (39%)
  waiting for transfers between devices  28.7 us (24%)
  Pallas kernels  22.9 us (19%)
  starting transfers between devices  14.7 us (12%)
  local copies, waits for them, and re-layouts  4.84 us (4%)
    all_to_all x1, blocking collectives, per_device(): received = lax.all_to_all(dense, 'front', 0, 0, tiled=True)  46.9 us
    all_to_all x1, waiting for transfers between devices, per_device(): gathered = lax.all_to_all(copies, 'front', 0, 0, tiled=True)  21.9 us
    pallas_call x1, Pallas kernels, per_device(): call(leaf_forward, [SMEM, columns, matrices, matrices, lines], [vectors,...  8.24 us
    pallas_call x1, Pallas kernels, per_device(): call(leaf_prepare, [vectors, matrices, matrices, lines], [vectors, matric...  7.59 us
    all_to_all x1, waiting for transfers between devices, per_device(): right = lax.all_to_all(right, 'leaf', 0, 0, tiled=True)  6.14 us
    all_to_all x1, starting transfers between devices, per_device(): gathered = lax.all_to_all(copies, 'front', 0, 0, tiled=True)  6 us
    unnamed x22, local copies, waits for them, and re-layouts  4.84 us
    all_to_all x1, starting transfers between devices, per_device(): right = lax.all_to_all(right, 'leaf', 0, 0, tiled=True)  4.42 us
  transfers between devices with their start and end apart: 3, of which 3 were waited for; matrix products, arithmetic and copies ran while one was open for 0% of the time, Pallas kernels for 13%

profile of v2, /device:TPU:16, one launch (start us, length us, event | category | flops | bytes accessed | tf_op | source)
XLA Modules:
  0.0 118.8 jit_solution(602290388088443095)
XLA Ops:
  0.6 0.0 copy-start
  0.6 0.8 copy-done
  1.5 0.0 copy-start.5
  1.5 0.8 copy-done.5
  2.3 0.0 copy-start.2
  2.3 1.0 coupled_inverse.1
  3.3 4.3 %all-to-all-start = ((f32[8,128,128]{2,1,0:T(8,128)}), f32[8,128,128]{2,1,0:T(8,128)S(1)}, u32[]{:S(2)}, u32[]{:S(2)}) async-start(f32[8,128,128]{2,1,0:T(8,128)} %coupled_inverse.1), calls=%async_computation | async-start | bytes 1048576 | tf_op jit(solution)/shard_map/all_to_all | solution.py:158
  7.6 0.0 copy-done.2
  7.6 0.0 copy-start.6
  7.6 0.7 copy-done.6
  8.3 0.0 copy-start.9
  8.3 0.7 copy-done.9
  9.0 8.2 %leaf_forward.1 = (f32[28,32,128]{2,1,0:T(8,128)S(1)}, f32[64,32,128]{2,1,0:T(8,128)S(1)}) custom-call(s32[28]{0:T(128)S(1)} %bitcast.19, f32[32,3584]{1,0:T(8,128)S(1)} %bitcast.14, f32[28,128,128]{2,1,0:T(8,128)} %bitcast.21, f32[28,128,128]{2,1,0:T(8,128)} %bitcast.23, s32[28,1,128]{2,1,0:T(1,128)S(1)} %bitcast.16), custom_call_target="tpu_custom_call" | custom-call | tf_op jit(solution)/shard_map/leaf_forward/pallas_call | solution.py:160
  17.2 0.0 copy-start.1
  17.2 0.0 copy-start.8
  17.3 0.7 all-to-all-done.coupled_ref
  18.0 46.9 %all_to_all.20.received_ref = f32[64,32,128]{2,1,0:T(8,128)S(1)} all-to-all(f32[64,32,128]{2,1,0:T(8,128)S(1)} %get-tuple-element.12), channel_id=1, replica_groups=mesh['leaf'=8,'front'=64] {'front'}, dimensions={0} | all-to-all | bytes 2097152 | tf_op jit(solution)/shard_map/all_to_all | solution.py:168
  64.8 0.0 copy-done.1
  64.8 0.0 copy-done.8
  64.8 0.9 reduce_right.1
  65.7 0.0 copy-start.7
  65.7 4.4 %all-to-all-start.2 = ((f32[8,32,128]{2,1,0:T(8,128)}), f32[8,32,128]{2,1,0:T(8,128)S(1)}, u32[]{:S(2)}, u32[]{:S(2)}) async-start(f32[8,32,128]{2,1,0:T(8,128)} %reduce_right.1), calls=%async_computation.2 | async-start | bytes 262144 | tf_op jit(solution)/shard_map/all_to_all | solution.py:181
  70.1 6.1 %all-to-all-done.2.right_ref = f32[8,32,128]{2,1,0:T(8,128)S(1)} async-done(((f32[8,32,128]{2,1,0:T(8,128)}), f32[8,32,128]{2,1,0:T(8,128)S(1)}, u32[]{:S(2)}, u32[]{:S(2)}) %all-to-all-start.2) | async-done | bytes 131104 | tf_op jit(solution)/shard_map/all_to_all | solution.py:181
  76.3 3.3 %chain.1 = (f32[32,128]{1,0:T(8,128)}, f32[64,32,128]{2,1,0:T(8,128)}) custom-call(s32[1]{0:T(128)} %bitcast.1.group_ref, f32[8,32,128]{2,1,0:T(8,128)S(1)} %all-to-all-done.2.right_ref, f32[8,128,128]{2,1,0:T(8,128)S(1)} %all-to-all-done.coupled_ref, f32[128,128]{1,0:T(8,128)S(1)} %bitcast.13), custom_call_target="tpu_custom_call" | custom-call | tf_op jit(solution)/shard_map/chain/pallas_call | solution.py:182
  79.6 6.0 %all-to-all-start.3 = ((f32[64,32,128]{2,1,0:T(8,128)}), f32[64,32,128]{2,1,0:T(8,128)S(1)}, u32[]{:S(2)}, u32[]{:S(2)}) async-start(f32[64,32,128]{2,1,0:T(8,128)} %get-tuple-element.14), calls=%async_computation.3 | async-start | bytes 2097152 | tf_op jit(solution)/shard_map/all_to_all | solution.py:189
  85.6 0.0 copy-done.7
  85.6 0.0 copy-start.10
  85.6 7.6 %leaf_prepare.1 = (f32[28,32,128]{2,1,0:T(8,128)S(1)}, bf16[28,128,128]{2,1,0:T(8,128)(2,1)S(1)}, bf16[28,128,128]{2,1,0:T(8,128)(2,1)S(1)}) custom-call(f32[28,32,128]{2,1,0:T(8,128)S(1)} %get-tuple-element.15.y_ref, f32[28,128,128]{2,1,0:T(8,128)} %bitcast.22, f32[28,128,128]{2,1,0:T(8,128)} %bitcast.24, s32[28,1,128]{2,1,0:T(1,128)S(1)} %bitcast.17), custom_call_target="tpu_custom_call" | custom-call | tf_op jit(solution)/shard_map/leaf_prepare/pallas_call | solution.py:170
  93.2 0.0 copy-start.3
  93.2 0.8 copy-done.3
  94.0 21.9 %all-to-all-done.3.x_ref = f32[64,32,128]{2,1,0:T(8,128)S(1)} async-done(((f32[64,32,128]{2,1,0:T(8,128)}), f32[64,32,128]{2,1,0:T(8,128)S(1)}, u32[]{:S(2)}, u32[]{:S(2)}) %all-to-all-start.3) | async-done | bytes 1048608 | tf_op jit(solution)/shard_map/all_to_all | solution.py:189
  115.9 0.0 copy-done.10
  115.9 0.0 copy-start.4
  115.9 1.0 copy-done.4
  116.9 1.9 %leaf_backward.1 = f32[32,3584]{1,0:T(8,128)} custom-call(s32[28]{0:T(128)S(1)} %bitcast.20, f32[64,32,128]{2,1,0:T(8,128)S(1)} %all-to-all-done.3.x_ref, f32[28,32,128]{2,1,0:T(8,128)S(1)} %copy-done.4, bf16[28,128,128]{2,1,0:T(8,128)(2,1)S(1)} %get-tuple-element.17.high_ref, bf16[28,128,128]{2,1,0:T(8,128)(2,1)S(1)} %get-tuple-element.18.low_ref), custom_call_target="tpu_custom_call" | custom-call | tf_op jit(solution)/shard_map/leaf_backward/pallas_call | solution.py:190
Async XLA Ops:
  0.6 0.8 copy-start
  1.5 0.8 copy-start.5
  2.3 5.3 %copy-start.2 = (f32[1,32,3584]{2,1,0:T(8,128)S(1)}, f32[1,32,3584]{2,1,0:T(8,128)}, u32[]{:S(2)}) copy-start(f32[1,32,3584]{2,1,0:T(8,128)} %param.8) | copy-start | bytes 1376260
  3.3 14.6 %all-to-all-start = ((f32[8,128,128]{2,1,0:T(8,128)}), f32[8,128,128]{2,1,0:T(8,128)S(1)}, u32[]{:S(2)}, u32[]{:S(2)}) async-start(f32[8,128,128]{2,1,0:T(8,128)} %coupled_inverse.1), calls=%async_computation | async-start | bytes 1048576 | tf_op jit(solution)/shard_map/all_to_all | solution.py:158
  7.6 0.7 copy-start.6
  8.3 0.7 copy-start.9
  17.2 47.6 %copy-start.1 = (f32[1,1,128,128]{3,2,1,0:T(8,128)S(1)}, f32[1,1,128,128]{3,2,1,0:T(8,128)}, u32[]{:S(2)}) copy-start(f32[1,1,128,128]{3,2,1,0:T(8,128)} %param.14) | copy-start | bytes 196612
  17.2 47.6 %copy-start.8 = (f32[1,32,128]{2,1,0:T(8,128)S(1)}, f32[1,32,128]{2,1,0:T(8,128)}, u32[]{:S(2)}) copy-start(f32[1,32,128]{2,1,0:T(8,128)} %param.9) | copy-start | bytes 49156
  65.7 19.9 %copy-start.7 = (s32[1,28,128]{2,0,1:T(1,128)S(1)}, s32[1,28,128]{2,0,1:T(1,128)}, u32[]{:S(2)}) copy-start(s32[1,28,128]{2,0,1:T(1,128)} %param.12) | copy-start | bytes 43012
  65.7 10.6 %all-to-all-start.2 = ((f32[8,32,128]{2,1,0:T(8,128)}), f32[8,32,128]{2,1,0:T(8,128)S(1)}, u32[]{:S(2)}, u32[]{:S(2)}) async-start(f32[8,32,128]{2,1,0:T(8,128)} %reduce_right.1), calls=%async_computation.2 | async-start | bytes 262144 | tf_op jit(solution)/shard_map/all_to_all | solution.py:181
  79.6 36.3 %all-to-all-start.3 = ((f32[64,32,128]{2,1,0:T(8,128)}), f32[64,32,128]{2,1,0:T(8,128)S(1)}, u32[]{:S(2)}, u32[]{:S(2)}) async-start(f32[64,32,128]{2,1,0:T(8,128)} %get-tuple-element.14), calls=%async_computation.3 | async-start | bytes 2097152 | tf_op jit(solution)/shard_map/all_to_all | solution.py:189
  85.6 30.3 %copy-start.10 = (s32[1,28,1]{1,2,0:T(1,128)S(1)}, s32[1,28,1]{1,2,0:T(1,128)}, u32[]{:S(2)}) copy-start(s32[1,28,1]{1,2,0:T(1,128)} %param.13) | copy-start | bytes 340
  93.2 0.8 copy-start.3
  115.9 1.0 copy-start.4

commit v3 on v2

v3 whole, which is shorter than its diff:
```python
import jax
import jax.numpy as jnp
from jax import lax
from jax.experimental import pallas as pl
from jax.experimental.pallas import tpu as pltpu
from jax.sharding import PartitionSpec as P

NT = (((1,), (1,)), ((), ()))
NN = (((1,), (0,)), ((), ()))


def dot(left, right, dims):
    return lax.dot_general(left, right, dims, preferred_element_type=jnp.float32)


def split(value):
    high = value.astype(jnp.bfloat16)
    low = (value - high.astype(jnp.float32)).astype(jnp.bfloat16)
    return high, low


def three_parts(parts, rows, size):
    return parts[:rows, :size] + (parts[rows:, :size] + parts[:rows, size:])


def product(left, right, dims):
    along = 0 if dims is NT else 1
    parts = dot(jnp.concatenate(split(left), axis=0), jnp.concatenate(split(right), axis=along), dims)
    return three_parts(parts, left.shape[0], right.shape[0])


def select(left, chosen, dims):
    rows = left.shape[0]
    both = dot(jnp.concatenate(split(left), axis=0), chosen, dims)
    return both[:rows] + both[rows:]


def chosen_rows(row_index, block_rows):
    separator_row = lax.broadcasted_iota(jnp.int32, (block_rows, block_rows), 0)
    return jnp.where(separator_row == row_index, 1.0, 0.0).astype(jnp.bfloat16)


def leaf_forward(owner_ref, rhs_ref, inv_ref, update_ref, rows_ref, y_ref, dense_ref):
    step = pl.program_id(0)
    count, size, _ = inv_ref.shape

    @pl.when(step == 0)
    def _():
        dense_ref[...] = jnp.zeros_like(dense_ref)

    leaf_y = [product(rhs_ref[:, f * size : (f + 1) * size], inv_ref[f], NT) for f in range(count)]
    for f in range(count):
        y_ref[f] = leaf_y[f]
    updates = [product(leaf_y[f], update_ref[f], NT) for f in range(count)]
    placed = [select(updates[f], chosen_rows(rows_ref[f], size), NT) for f in range(count)]
    for f in range(count):
        dense_ref[owner_ref[step * count + f]] = placed[f]


def coupled_inverse(inv_ref, couple_ref, after_ref, out_ref):
    out_ref[0] = product(inv_ref[...], couple_ref[...], NN)


def leaf_prepare(y_ref, inv_ref, update_ref, rows_ref, own_ref, mapped_ref):
    count, size, _ = inv_ref.shape
    for f in range(count):
        inverse = inv_ref[f]
        own_ref[:, f * size : (f + 1) * size] = product(y_ref[f], inverse, NN)
        mapped = jnp.concatenate(split(product(update_ref[f], inverse, NN)), axis=1)
        placed = dot(chosen_rows(rows_ref[f], size), mapped, NN)
        mapped_ref[f] = jnp.concatenate(split(placed[:, :size] + placed[:, size:]), axis=1)


def reduce_right(received_ref, rhs_ref, inv_ref, out_ref):
    reduced = rhs_ref[...] - jnp.sum(received_ref[...], axis=0)
    solved = product(reduced, inv_ref[...], NT)
    for copy in range(out_ref.shape[0]):
        out_ref[copy] = solved


def chain(group_ref, right_ref, coupled_ref, inv_ref, x_ref, copies_ref, scratch):
    groups = right_ref.shape[0]
    own = group_ref[0]
    solved = [right_ref[0]]
    for group in range(1, groups):
        coupled = coupled_ref[jnp.bitwise_xor(own, group)]
        solved.append(right_ref[group] - product(solved[-1], coupled, NT))
    residue = solved[-1]
    scratch[groups - 1] = residue
    for group in range(groups - 1, 0, -1):
        coupled = coupled_ref[jnp.bitwise_xor(own, group)]
        residue = solved[group - 1] - product(residue, coupled, NN)
        scratch[group - 1] = residue
    x_sep = product(scratch[own], inv_ref[...], NN)
    x_ref[...] = x_sep
    for copy in range(copies_ref.shape[0]):
        copies_ref[copy] = x_sep


def leaf_backward(owner_ref, x_ref, own_hbm, mapped_ref, out_ref, own_ref, arrived):
    count, size, _ = mapped_ref.shape
    rows = out_ref.shape[0]
    fetch = pltpu.make_async_copy(own_hbm, own_ref, arrived)
    fetch.start()
    for f in range(count):
        owned = jnp.concatenate(split(x_ref[owner_ref[f]]), axis=0)
        out_ref[:, f * size : (f + 1) * size] = three_parts(dot(owned, mapped_ref[f], NN), rows, size)
    fetch.wait()
    out_ref[...] = own_ref[...] - out_ref[...]


FORWARD_STEP = 14
PREPARE_STEP = 7
VMEM = pl.BlockSpec(memory_space=pltpu.VMEM)
SMEM = pl.BlockSpec(memory_space=pltpu.SMEM)
ANY = pl.BlockSpec(memory_space=pl.ANY)
PARAMS = pltpu.CompilerParams(vmem_limit_bytes=32 << 20)


def floats(*shape):
    return jax.ShapeDtypeStruct(shape, jnp.float32)


def call(body, in_specs, out_specs, out_shape, **rest):
    return pl.pallas_call(
        body,
        in_specs=in_specs,
        out_specs=out_specs,
        out_shape=out_shape,
        compiler_params=PARAMS,
        name=body.__name__,
        **rest,
    )


def gather_by_bits(value, axis):
    count, bit = lax.axis_size(axis), 1
    while bit < count:
        pairs = [(source, source ^ bit) for source in range(count)]
        value = jnp.concatenate([value, lax.ppermute(value, axis, pairs)], axis=0)
        bit *= 2
    return value


def per_device(
    rhs_leaf, rhs_sep, leaf_inv, leaf_update, update_rows, update_owner, sep_inv, sep_couple
):
    front_count, size = leaf_inv.shape[1], leaf_inv.shape[3]
    width = rhs_leaf.shape[1]
    groups = lax.axis_size("leaf")
    fronts = lax.axis_size("front")

    def stay(value):
        return pltpu.with_memory_space_constraint(value, pltpu.HBM)

    right_leaf, inverse, coupling = stay(rhs_leaf[0]), stay(leaf_inv[0]), stay(leaf_update[0])
    rows = stay(update_rows.reshape(front_count, 1, size))
    owners = stay(update_owner.reshape(front_count))
    separator_inverse, separator_couple = sep_inv[0, 0], sep_couple[0, 0]

    def specs(step):
        matrices = pl.BlockSpec((step, size, size), lambda s: (s, 0, 0))
        lines = pl.BlockSpec((step, 1, size), lambda s: (s, 0, 0))
        vectors = pl.BlockSpec((step, width, size), lambda s: (s, 0, 0))
        columns = pl.BlockSpec((width, step * size), lambda s: (0, s))
        return matrices, lines, vectors, columns

    matrices, lines, vectors, columns = specs(FORWARD_STEP)
    whole = pl.BlockSpec((fronts, width, size), lambda s: (0, 0, 0))
    leaf_y, dense = call(
        leaf_forward,
        [SMEM, columns, matrices, matrices, lines],
        [vectors, whole],
        [floats(front_count, width, size), floats(fronts, width, size)],
        grid=(front_count // FORWARD_STEP,),
    )(owners, right_leaf, inverse, coupling, rows)
    received = lax.all_to_all(dense, "front", 0, 0, tiled=True)

    coupled = call(coupled_inverse, [VMEM, VMEM, ANY], VMEM, floats(1, size, size))(
        separator_inverse, separator_couple, leaf_y
    )
    coupled = gather_by_bits(coupled, "leaf")
    matrices, lines, vectors, columns = specs(PREPARE_STEP)
    own, mapped = call(
        leaf_prepare,
        [vectors, matrices, matrices, lines],
        [columns, pl.BlockSpec((PREPARE_STEP, size, 2 * size), lambda s: (s, 0, 0))],
        [
            floats(width, front_count * size),
            jax.ShapeDtypeStruct((front_count, size, 2 * size), jnp.bfloat16),
        ],
        grid=(front_count // PREPARE_STEP,),
    )(leaf_y, inverse, coupling, rows)

    own = stay(own)
    right = call(reduce_right, [VMEM, VMEM, VMEM], VMEM, floats(groups, width, size))(
        received, rhs_sep[0], separator_inverse
    )
    right = lax.all_to_all(right, "leaf", 0, 0, tiled=True)
    x_sep, copies = call(
        chain,
        [SMEM, VMEM, VMEM, VMEM],
        [VMEM, VMEM],
        [floats(width, size), floats(fronts, width, size)],
        scratch_shapes=[pltpu.VMEM((groups, width, size), jnp.float32)],
    )(lax.axis_index("leaf").reshape(1), right, coupled, separator_inverse)
    gathered = lax.all_to_all(copies, "front", 0, 0, tiled=True)
    x_leaf = call(
        leaf_backward,
        [SMEM, VMEM, ANY, VMEM],
        VMEM,
        floats(width, front_count * size),
        scratch_shapes=[
            pltpu.VMEM((width, front_count * size), jnp.float32),
            pltpu.SemaphoreType.DMA(()),
        ],
    )(owners, gathered, own, mapped)
    return (x_leaf[None], x_sep[None])


def solution(mesh):
    placed = (
        P("leaf", None, "front"),
        P("leaf", None, "front"),
        P("leaf", "front", None, None),
        P("leaf", "front", None, None),
        P("leaf", "front", None),
        P("leaf", "front", None),
        P("leaf", "front", None, None),
        P("leaf", "front", None, None),
    )
    return jax.shard_map(
        per_device,
        mesh=mesh,
        in_specs=placed,
        out_specs=(P("leaf", None, "front"), P("leaf", None, "front")),
        check_vma=False,
    )
```

time: 119 us -> 106 us (0.89)
  blocking collectives: 46.9 us -> 0 us
  starting transfers between devices: 14.7 us -> 36.7 us
  waiting for transfers between devices: 28.7 us -> 47.1 us
  local copies, waits for them, and re-layouts: 4.84 us -> 0.8 us
  Pallas kernels: 22.9 us -> 20.1 us
    all_to_all x1 -> x0, blocking collectives: 46.9 us -> none  [per_device(): received = lax.all_to_all(dense, 'front', 0, 0, tiled=True)]
    all_to_all x1, waiting for transfers between devices: 0.7 us -> 14.7 us  [per_device(): received = lax.all_to_all(dense, 'front', 0, 0, tiled=True)]
    all_to_all x1, starting transfers between devices: 4.3 us -> 16.6 us  [per_device(): received = lax.all_to_all(dense, 'front', 0, 0, tiled=True)]
    ppermute x0 -> x3, starting transfers between devices: none -> 10.3 us  [gather_by_bits(): value = jnp.concatenate([value, lax.ppermute(value, axis, pairs)], axis=0)]
    ppermute x0 -> x3, waiting for transfers between devices: none -> 5.27 us  [gather_by_bits(): value = jnp.concatenate([value, lax.ppermute(value, axis, pairs)], axis=0)]
    unnamed x22 -> x8, local copies, waits for them, and re-layouts: 4.84 us -> 0.8 us
    pallas_call x1, Pallas kernels: 8.24 us -> 4.71 us  [per_device(): call(leaf_forward, [SMEM, columns, matrices, matrices, lines], [vectors,...]
  transfers between devices with their start and end apart: 3 -> 6, of which waited for: 3 -> 5; matrix products, arithmetic and copies ran while one was open for 0% -> 0% of each run, Pallas kernels for 13% -> 9%
where the time goes in v3:
time: 106 us; the launch traced here: 105 us
  waiting for transfers between devices  47.1 us (44%)
  starting transfers between devices  36.7 us (35%)
  Pallas kernels  20.1 us (19%)
    all_to_all x1, waiting for transfers between devices, per_device(): gathered = lax.all_to_all(copies, 'front', 0, 0, tiled=True)  21 us
    all_to_all x1, starting transfers between devices, per_device(): received = lax.all_to_all(dense, 'front', 0, 0, tiled=True)  16.6 us
    all_to_all x1, waiting for transfers between devices, per_device(): received = lax.all_to_all(dense, 'front', 0, 0, tiled=True)  14.7 us
    ppermute x3, starting transfers between devices, gather_by_bits(): value = jnp.concatenate([value, lax.ppermute(value, axis, pairs)], axis=0)  10.3 us
    pallas_call x1, Pallas kernels, per_device(): call(leaf_prepare, [vectors, matrices, matrices, lines], [columns, pl.Blo...  8.48 us
    all_to_all x1, waiting for transfers between devices, per_device(): right = lax.all_to_all(right, 'leaf', 0, 0, tiled=True)  6.08 us
    all_to_all x1, starting transfers between devices, per_device(): gathered = lax.all_to_all(copies, 'front', 0, 0, tiled=True)  5.69 us
    ppermute x3, waiting for transfers between devices, gather_by_bits(): value = jnp.concatenate([value, lax.ppermute(value, axis, pairs)], axis=0)  5.27 us
  transfers between devices with their start and end apart: 6, of which 5 were waited for; matrix products, arithmetic and copies ran while one was open for 0% of the time, Pallas kernels for 9%

profile of v3, /device:TPU:16, one launch (start us, length us, event | category | flops | bytes accessed | tf_op | source)
XLA Modules:
  0.0 105.5 jit_solution(2060816137619502805)
XLA Ops:
  0.6 4.7 %leaf_forward.1 = (f32[28,32,128]{2,1,0:T(8,128)S(1)}, f32[64,32,128]{2,1,0:T(8,128)}) custom-call(s32[28]{0:T(128)} %bitcast.24, f32[32,3584]{1,0:T(8,128)} %bitcast.20, f32[28,128,128]{2,1,0:T(8,128)} %bitcast.16, f32[28,128,128]{2,1,0:T(8,128)} %bitcast.18, s32[28,1,128]{2,1,0:T(1,128)} %bitcast.22), custom_call_target="tpu_custom_call" | custom-call | tf_op jit(solution)/shard_map/leaf_forward/pallas_call | solution.py:170
  5.3 0.0 copy-start
  5.3 0.0 copy-start.2
  5.3 0.0 copy-start.3
  5.3 16.6 %all-to-all-start = ((f32[64,32,128]{2,1,0:T(8,128)}), f32[64,32,128]{2,1,0:T(8,128)S(1)}, u32[]{:S(2)}, u32[]{:S(2)}) async-start(f32[64,32,128]{2,1,0:T(8,128)} %get-tuple-element.8), calls=%async_computation | async-start | bytes 2097152 | tf_op jit(solution)/shard_map/all_to_all | solution.py:177
  22.0 0.0 copy-done
  22.0 0.0 copy-done.2
  22.0 0.2 coupled_inverse.1
  22.2 1.9 %collective-permute-start = (f32[1,128,128]{2,1,0:T(8,128)S(1)}, f32[1,128,128]{2,1,0:T(8,128)S(1)}, u32[]{:S(2)}, u32[]{:S(2)}) collective-permute-start(f32[1,128,128]{2,1,0:T(8,128)S(1)} %coupled_inverse.1), channel_id=1, source_target_pairs={{0,64},{64,0},{128,192},{192,128},{256,320},{320,256},{384,448},{4... | collective-permute-start | bytes 196616 | tf_op jit(solution)/shard_map/ppermute | solution.py:140
  24.1 1.2 %collective-permute-done = f32[1,128,128]{2,1,0:T(8,128)S(1)} collective-permute-done((f32[1,128,128]{2,1,0:T(8,128)S(1)}, f32[1,128,128]{2,1,0:T(8,128)S(1)}, u32[]{:S(2)}, u32[]{:S(2)}) %collective-permute-start) | collective-permute-done | bytes 65568 | tf_op jit(solution)/shard_map/ppermute | solution.py:140
  25.3 3.4 %collective-permute-start.1 = (f32[2,128,128]{2,1,0:T(8,128)S(1)}, f32[2,128,128]{2,1,0:T(8,128)S(1)}, u32[]{:S(2)}, u32[]{:S(2)}) collective-permute-start(f32[2,128,128]{2,1,0:T(8,128)S(1)} %pad_maximum_fusion.2), channel_id=1, source_target_pairs={{0,128},{64,192},{128,0},{192,64},{256,384},{320,448},{384,256},{4... | collective-permute-start | bytes 393224 | tf_op jit(solution)/shard_map/ppermute | solution.py:140
  28.7 4.0 %collective-permute-done.1 = f32[2,128,128]{2,1,0:T(8,128)S(1)} collective-permute-done((f32[2,128,128]{2,1,0:T(8,128)S(1)}, f32[2,128,128]{2,1,0:T(8,128)S(1)}, u32[]{:S(2)}, u32[]{:S(2)}) %collective-permute-start.1) | collective-permute-done | bytes 131104 | tf_op jit(solution)/shard_map/ppermute | solution.py:140
  32.8 4.9 %collective-permute-start.2 = (f32[4,128,128]{2,1,0:T(8,128)S(1)}, f32[4,128,128]{2,1,0:T(8,128)S(1)}, u32[]{:S(2)}, u32[]{:S(2)}) collective-permute-start(f32[4,128,128]{2,1,0:T(8,128)S(1)} %pad_maximum_fusion.1), channel_id=1, source_target_pairs={{0,256},{64,320},{128,384},{192,448},{256,0},{320,64},{384,128},{4... | collective-permute-start | bytes 786440 | tf_op jit(solution)/shard_map/ppermute | solution.py:140
  37.8 14.7 %all-to-all-done.received_ref = f32[64,32,128]{2,1,0:T(8,128)S(1)} async-done(((f32[64,32,128]{2,1,0:T(8,128)}), f32[64,32,128]{2,1,0:T(8,128)S(1)}, u32[]{:S(2)}, u32[]{:S(2)}) %all-to-all-start) | async-done | bytes 1048608 | tf_op jit(solution)/shard_map/all_to_all | solution.py:177
  52.5 0.0 copy-done.3
  52.5 0.9 reduce_right.1
  53.4 4.2 %all-to-all-start.1 = ((f32[8,32,128]{2,1,0:T(8,128)}), f32[8,32,128]{2,1,0:T(8,128)S(1)}, u32[]{:S(2)}, u32[]{:S(2)}) async-start(f32[8,32,128]{2,1,0:T(8,128)} %reduce_right.1), calls=%async_computation.1 | async-start | bytes 262144 | tf_op jit(solution)/shard_map/all_to_all | solution.py:199
  57.5 0.0 collective-permute-done.2
  57.6 6.1 %all-to-all-done.1.right_ref = f32[8,32,128]{2,1,0:T(8,128)S(1)} async-done(((f32[8,32,128]{2,1,0:T(8,128)}), f32[8,32,128]{2,1,0:T(8,128)S(1)}, u32[]{:S(2)}, u32[]{:S(2)}) %all-to-all-start.1) | async-done | bytes 131104 | tf_op jit(solution)/shard_map/all_to_all | solution.py:199
  63.7 3.1 %chain.1 = (f32[32,128]{1,0:T(8,128)}, f32[64,32,128]{2,1,0:T(8,128)}) custom-call(s32[1]{0:T(128)} %bitcast.1.group_ref, f32[8,32,128]{2,1,0:T(8,128)S(1)} %all-to-all-done.1.right_ref, f32[8,128,128]{2,1,0:T(8,128)S(1)} %pad_maximum_fusion.coupled_ref, f32[128,128]{1,0:T(8,128)S(1)} %bitcast.13), custom_call_target="tpu_custom_call" | custom-call | tf_op jit(solution)/shard_map/chain/pallas_call | solution.py:200
  66.7 5.7 %all-to-all-start.2 = ((f32[64,32,128]{2,1,0:T(8,128)}), f32[64,32,128]{2,1,0:T(8,128)S(1)}, u32[]{:S(2)}, u32[]{:S(2)}) async-start(f32[64,32,128]{2,1,0:T(8,128)} %get-tuple-element.10), calls=%async_computation.2 | async-start | bytes 2097152 | tf_op jit(solution)/shard_map/all_to_all | solution.py:207
  72.4 8.5 %leaf_prepare.1 = (f32[32,3584]{1,0:T(8,128)S(1)}, bf16[28,128,256]{2,1,0:T(8,128)(2,1)S(1)}) custom-call(f32[28,32,128]{2,1,0:T(8,128)S(1)} %get-tuple-element.9.after_ref.y_ref, f32[28,128,128]{2,1,0:T(8,128)} %bitcast.17, f32[28,128,128]{2,1,0:T(8,128)} %bitcast.19, s32[28,1,128]{2,1,0:T(1,128)} %bitcast.23), custom_call_target="tpu_custom_call" | custom-call | tf_op jit(solution)/shard_map/leaf_prepare/pallas_call | solution.py:184
  80.9 0.0 copy-start.1
  80.9 0.8 copy-done.1
  81.7 21.0 %all-to-all-done.2.x_ref = f32[64,32,128]{2,1,0:T(8,128)S(1)} async-done(((f32[64,32,128]{2,1,0:T(8,128)}), f32[64,32,128]{2,1,0:T(8,128)S(1)}, u32[]{:S(2)}, u32[]{:S(2)}) %all-to-all-start.2) | async-done | bytes 1048608 | tf_op jit(solution)/shard_map/all_to_all | solution.py:207
  102.7 2.8 %leaf_backward.1 = f32[32,3584]{1,0:T(8,128)} custom-call(s32[28]{0:T(128)} %bitcast.25, f32[64,32,128]{2,1,0:T(8,128)S(1)} %all-to-all-done.2.x_ref, f32[32,3584]{1,0:T(8,128)} %copy-done.1, bf16[28,128,256]{2,1,0:T(8,128)(2,1)S(1)} %get-tuple-element.12.mapped_ref), custom_call_target="tpu_custom_call" | custom-call | tf_op jit(solution)/shard_map/leaf_backward/pallas_call | solution.py:208
  (3 shorter events, 0.1 us)
Async XLA Ops:
  5.3 16.6 %copy-start = (f32[1,1,128,128]{3,2,1,0:T(8,128)S(1)}, f32[1,1,128,128]{3,2,1,0:T(8,128)}, u32[]{:S(2)}) copy-start(f32[1,1,128,128]{3,2,1,0:T(8,128)} %param.14) | copy-start | bytes 196612
  5.3 16.6 %copy-start.2 = (f32[1,1,128,128]{3,2,1,0:T(8,128)S(1)}, f32[1,1,128,128]{3,2,1,0:T(8,128)}, u32[]{:S(2)}) copy-start(f32[1,1,128,128]{3,2,1,0:T(8,128)} %param.15) | copy-start | bytes 196612
  5.3 47.1 %copy-start.3 = (f32[1,32,128]{2,1,0:T(8,128)S(1)}, f32[1,32,128]{2,1,0:T(8,128)}, u32[]{:S(2)}) copy-start(f32[1,32,128]{2,1,0:T(8,128)} %param.9) | copy-start | bytes 49156
  5.3 47.1 %all-to-all-start = ((f32[64,32,128]{2,1,0:T(8,128)}), f32[64,32,128]{2,1,0:T(8,128)S(1)}, u32[]{:S(2)}, u32[]{:S(2)}) async-start(f32[64,32,128]{2,1,0:T(8,128)} %get-tuple-element.8), calls=%async_computation | async-start | bytes 2097152 | tf_op jit(solution)/shard_map/all_to_all | solution.py:177
  22.2 3.1 %collective-permute-start = (f32[1,128,128]{2,1,0:T(8,128)S(1)}, f32[1,128,128]{2,1,0:T(8,128)S(1)}, u32[]{:S(2)}, u32[]{:S(2)}) collective-permute-start(f32[1,128,128]{2,1,0:T(8,128)S(1)} %coupled_inverse.1), channel_id=1, source_target_pairs={{0,64},{64,0},{128,192},{192,128},{256,320},{320,256},{384,448},{4... | collective-permute-start | bytes 196616 | tf_op jit(solution)/shard_map/ppermute | solution.py:140
  25.3 7.5 %collective-permute-start.1 = (f32[2,128,128]{2,1,0:T(8,128)S(1)}, f32[2,128,128]{2,1,0:T(8,128)S(1)}, u32[]{:S(2)}, u32[]{:S(2)}) collective-permute-start(f32[2,128,128]{2,1,0:T(8,128)S(1)} %pad_maximum_fusion.2), channel_id=1, source_target_pairs={{0,128},{64,192},{128,0},{192,64},{256,384},{320,448},{384,256},{4... | collective-permute-start | bytes 393224 | tf_op jit(solution)/shard_map/ppermute | solution.py:140
  32.8 24.7 %collective-permute-start.2 = (f32[4,128,128]{2,1,0:T(8,128)S(1)}, f32[4,128,128]{2,1,0:T(8,128)S(1)}, u32[]{:S(2)}, u32[]{:S(2)}) collective-permute-start(f32[4,128,128]{2,1,0:T(8,128)S(1)} %pad_maximum_fusion.1), channel_id=1, source_target_pairs={{0,256},{64,320},{128,384},{192,448},{256,0},{320,64},{384,128},{4... | collective-permute-start | bytes 786440 | tf_op jit(solution)/shard_map/ppermute | solution.py:140
  53.4 10.3 %all-to-all-start.1 = ((f32[8,32,128]{2,1,0:T(8,128)}), f32[8,32,128]{2,1,0:T(8,128)S(1)}, u32[]{:S(2)}, u32[]{:S(2)}) async-start(f32[8,32,128]{2,1,0:T(8,128)} %reduce_right.1), calls=%async_computation.1 | async-start | bytes 262144 | tf_op jit(solution)/shard_map/all_to_all | solution.py:199
  66.7 36.0 %all-to-all-start.2 = ((f32[64,32,128]{2,1,0:T(8,128)}), f32[64,32,128]{2,1,0:T(8,128)S(1)}, u32[]{:S(2)}, u32[]{:S(2)}) async-start(f32[64,32,128]{2,1,0:T(8,128)} %get-tuple-element.10), calls=%async_computation.2 | async-start | bytes 2097152 | tf_op jit(solution)/shard_map/all_to_all | solution.py:207
  80.9 0.8 copy-start.1

commit v4 on v3

--- a/solution.py
+++ b/solution.py
@@ -40,9 +40,19 @@
     return jnp.where(separator_row == row_index, 1.0, 0.0).astype(jnp.bfloat16)
 
 
-def leaf_forward(owner_ref, rhs_ref, inv_ref, update_ref, rows_ref, y_ref, dense_ref):
+def place_of(owner, own_class):
+    y, z = owner >> EDGE_BITS, owner & (EDGE - 1)
+    relative = jnp.bitwise_xor(((y & 1) << 1) | (z & 1), own_class)
+    return relative, ((y >> 1) << (EDGE_BITS - 1)) | (z >> 1)
+
+
+def leaf_forward(
+    class_ref, owner_ref, rhs_ref, inv_ref, update_ref, rows_ref, y_ref, *rest
+):
+    *class_refs, dense_ref = rest
     step = pl.program_id(0)
     count, size, _ = inv_ref.shape
+    members = class_refs[0].shape[0]
 
     @pl.when(step == 0)
     def _():
@@ -54,7 +64,13 @@
     updates = [product(leaf_y[f], update_ref[f], NT) for f in range(count)]
     placed = [select(updates[f], chosen_rows(rows_ref[f], size), NT) for f in range(count)]
     for f in range(count):
-        dense_ref[owner_ref[step * count + f]] = placed[f]
+        relative, place = place_of(owner_ref[step * count + f], class_ref[0])
+        dense_ref[relative * members + place] = placed[f]
+
+    @pl.when(step == pl.num_programs(0) - 1)
+    def _():
+        for k, class_ref_k in enumerate(class_refs):
+            class_ref_k[...] = dense_ref[k * members : (k + 1) * members]
 
 
 def coupled_inverse(inv_ref, couple_ref, after_ref, out_ref):
@@ -97,18 +113,27 @@
         copies_ref[copy] = x_sep
 
 
-def leaf_backward(owner_ref, x_ref, own_hbm, mapped_ref, out_ref, own_ref, arrived):
+def leaf_backward(
+    class_ref, owner_ref, x0_ref, x1_ref, x2_ref, x3_ref, own_hbm, mapped_ref, out_ref, x_ref, own_ref, arrived
+):
     count, size, _ = mapped_ref.shape
     rows = out_ref.shape[0]
+    members = x0_ref.shape[0]
     fetch = pltpu.make_async_copy(own_hbm, own_ref, arrived)
     fetch.start()
+    for k, class_ref_k in enumerate((x0_ref, x1_ref, x2_ref, x3_ref)):
+        x_ref[k * members : (k + 1) * members] = class_ref_k[...]
     for f in range(count):
-        owned = jnp.concatenate(split(x_ref[owner_ref[f]]), axis=0)
+        relative, place = place_of(owner_ref[f], class_ref[0])
+        owned = jnp.concatenate(split(x_ref[relative * members + place]), axis=0)
         out_ref[:, f * size : (f + 1) * size] = three_parts(dot(owned, mapped_ref[f], NN), rows, size)
     fetch.wait()
     out_ref[...] = own_ref[...] - out_ref[...]
 
 
+EDGE_BITS = 3
+EDGE = 1 << EDGE_BITS
+CLASSES = 4
 FORWARD_STEP = 14
 PREPARE_STEP = 7
 VMEM = pl.BlockSpec(memory_space=pltpu.VMEM)
@@ -133,6 +158,38 @@
     )
 
 
+def pair(index):
+    return index ^ 1
+
+
+def other_pair(index):
+    return (index - 1 if index % 2 == 0 else index + 1) % EDGE
+
+
+def exchange_classes(values):
+    moves = (
+        lambda y, z: (y, pair(z)),
+        lambda y, z: (pair(y), z),
+        lambda y, z: (other_pair(y), other_pair(z)),
+    )
+    result = [values[0]]
+    for value, move in zip(values[1:], moves):
+        pairs = []
+        for source in range(EDGE * EDGE):
+            y, z = move(source // EDGE, source % EDGE)
+            pairs.append((source, y * EDGE + z))
+        result.append(lax.ppermute(value, "front", pairs))
+    return result
+
+
+def exchange_members(value):
+    half = range(EDGE // 2)
+    groups = [
+        [(2 * i + a) * EDGE + 2 * j + b for i in half for j in half] for a in range(2) for b in range(2)
+    ]
+    return lax.all_to_all(value, "front", 0, 0, tiled=True, axis_index_groups=groups)
+
+
 def gather_by_bits(value, axis):
     count, bit = lax.axis_size(axis), 1
     while bit < count:
@@ -166,15 +223,20 @@
         return matrices, lines, vectors, columns
 
     matrices, lines, vectors, columns = specs(FORWARD_STEP)
-    whole = pl.BlockSpec((fronts, width, size), lambda s: (0, 0, 0))
-    leaf_y, dense = call(
+    members = fronts // CLASSES
+    one_class = pl.BlockSpec((members, width, size), lambda s: (0, 0, 0))
+    front = lax.axis_index("front")
+    own_class = (((front >> (EDGE_BITS - 1)) & 2) | (front & 1)).reshape(1)
+    leaf_y, *by_class = call(
         leaf_forward,
-        [SMEM, columns, matrices, matrices, lines],
-        [vectors, whole],
-        [floats(front_count, width, size), floats(fronts, width, size)],
+        [SMEM, SMEM, columns, matrices, matrices, lines],
+        [vectors] + [one_class] * CLASSES,
+        [floats(front_count, width, size)] + [floats(members, width, size)] * CLASSES,
         grid=(front_count // FORWARD_STEP,),
-    )(owners, right_leaf, inverse, coupling, rows)
-    received = lax.all_to_all(dense, "front", 0, 0, tiled=True)
+        scratch_shapes=[pltpu.VMEM((fronts, width, size), jnp.float32)],
+    )(own_class, owners, right_leaf, inverse, coupling, rows)
+    first, second, third, fourth = exchange_classes(by_class)
+    received = exchange_members((first + second) + (third + fourth))
 
     coupled = call(coupled_inverse, [VMEM, VMEM, ANY], VMEM, floats(1, size, size))(
         separator_inverse, separator_couple, leaf_y
@@ -201,20 +263,22 @@
         chain,
         [SMEM, VMEM, VMEM, VMEM],
         [VMEM, VMEM],
-        [floats(width, size), floats(fronts, width, size)],
+        [floats(width, size), floats(members, width, size)],
         scratch_shapes=[pltpu.VMEM((groups, width, size), jnp.float32)],
     )(lax.axis_index("leaf").reshape(1), right, coupled, separator_inverse)
-    gathered = lax.all_to_all(copies, "front", 0, 0, tiled=True)
+    gathered, own, mapped = lax.optimization_barrier((exchange_members(copies), own, mapped))
+    gathered = exchange_classes([gathered] * CLASSES)
     x_leaf = call(
         leaf_backward,
-        [SMEM, VMEM, ANY, VMEM],
+        [SMEM, SMEM, VMEM, VMEM, VMEM, VMEM, ANY, VMEM],
         VMEM,
         floats(width, front_count * size),
         scratch_shapes=[
+            pltpu.VMEM((fronts, width, size), jnp.float32),
             pltpu.VMEM((width, front_count * size), jnp.float32),
             pltpu.SemaphoreType.DMA(()),
         ],
-    )(owners, gathered, own, mapped)
+    )(own_class, owners, *gathered, own, mapped)
     return (x_leaf[None], x_sep[None])
 
 

time: 106 us -> 104 us (0.981)
  the two profiles are of different devices: /device:TPU:16 before, /device:TPU:1 now
where the time goes in v4:
time: 104 us; the launch traced here: 103 us
  starting transfers between devices  57.8 us (56%)
  waiting for transfers between devices  23.8 us (23%)
  Pallas kernels  18.8 us (18%)
    ppermute x6, starting transfers between devices, exchange_classes(): result.append(lax.ppermute(value, 'front', pairs))  28.8 us
    all_to_all x2, waiting for transfers between devices, exchange_members(): lax.all_to_all(value, 'front', 0, 0, tiled=True, axis_index_groups=groups)  11.6 us
    ppermute x3, starting transfers between devices, gather_by_bits(): value = jnp.concatenate([value, lax.ppermute(value, axis, pairs)], axis=0)  11.2 us
    all_to_all x2, starting transfers between devices, exchange_members(): lax.all_to_all(value, 'front', 0, 0, tiled=True, axis_index_groups=groups)  9.66 us
    pallas_call x1, Pallas kernels, per_device(): call(leaf_prepare, [vectors, matrices, matrices, lines], [columns, pl.Blo...  8.48 us
    all_to_all x1, starting transfers between devices, per_device(): right = lax.all_to_all(right, 'leaf', 0, 0, tiled=True)  8.19 us
    ppermute x6, waiting for transfers between devices, exchange_classes(): result.append(lax.ppermute(value, 'front', pairs))  6.09 us
    all_to_all x1, waiting for transfers between devices, per_device(): right = lax.all_to_all(right, 'leaf', 0, 0, tiled=True)  5.23 us
  transfers between devices with their start and end apart: 12, of which 7 were waited for; matrix products, arithmetic and copies ran while one was open for 1% of the time, Pallas kernels for 9%

profile of v4, /device:TPU:1, one launch (start us, length us, event | category | flops | bytes accessed | tf_op | source)
XLA Modules:
  0.0 103.0 jit_solution(2848948367685528158)
XLA Ops:
  0.6 0.0 copy-start
  0.6 0.0 copy-start.2
  0.7 3.9 %leaf_forward.1 = (f32[28,32,128]{2,1,0:T(8,128)S(1)}, f32[16,32,128]{2,1,0:T(8,128)S(1)}, f32[16,32,128]{2,1,0:T(8,128)S(1)}, f32[16,32,128]{2,1,0:T(8,128)S(1)}, f32[16,32,128]{2,1,0:T(8,128)S(1)}) custom-call(s32[1]{0:T(128)} %bitcast.class_ref, s32[28]{0:T(128)} %bitcast.25, f32[32,3584]{1,0:T(8,128)} %bitcast.21, f32[28,128,128]{2,1,0:T(8,128)} %bitcast.17, ...), custom_call_target="tpu_custom_call" | custom-call | tf_op jit(solution)/shard_map/leaf_forward/pallas_call | solution.py:230
  4.5 0.0 copy-start.3
  4.5 4.8 %collective-permute-start = (f32[16,32,128]{2,1,0:T(8,128)S(1)}, f32[16,32,128]{2,1,0:T(8,128)S(1)}, u32[]{:S(2)}, u32[]{:S(2)}) collective-permute-start(f32[16,32,128]{2,1,0:T(8,128)S(1)} %get-tuple-element.15), channel_id=1, source_target_pairs={{0,1},{1,0},{2,3},{3,2},{4,5},{5,4},{6,7},{7,6},{8,9},{9,8},{10,11... | collective-permute-start | bytes 786440 | tf_op jit(solution)/shard_map/ppermute | solution.py:181
  9.4 3.2 %collective-permute-start.1 = (f32[16,32,128]{2,1,0:T(8,128)S(1)}, f32[16,32,128]{2,1,0:T(8,128)S(1)}, u32[]{:S(2)}, u32[]{:S(2)}) collective-permute-start(f32[16,32,128]{2,1,0:T(8,128)S(1)} %get-tuple-element.16), channel_id=1, source_target_pairs={{0,8},{1,9},{2,10},{3,11},{4,12},{5,13},{6,14},{7,15},{8,0},{9,1},... | collective-permute-start | bytes 786440 | tf_op jit(solution)/shard_map/ppermute | solution.py:181
  12.6 11.5 %collective-permute-start.2 = (f32[16,32,128]{2,1,0:T(8,128)S(1)}, f32[16,32,128]{2,1,0:T(8,128)S(1)}, u32[]{:S(2)}, u32[]{:S(2)}) collective-permute-start(f32[16,32,128]{2,1,0:T(8,128)S(1)} %get-tuple-element.17), channel_id=1, source_target_pairs={{0,63},{1,58},{2,57},{3,60},{4,59},{5,62},{6,61},{7,56},{8,23},{9,... | collective-permute-start | bytes 786440 | tf_op jit(solution)/shard_map/ppermute | solution.py:181
  24.1 0.0 copy-done
  24.1 0.0 copy-done.2
  24.1 0.2 coupled_inverse.1
  24.3 3.4 %collective-permute-start.3 = (f32[1,128,128]{2,1,0:T(8,128)S(1)}, f32[1,128,128]{2,1,0:T(8,128)S(1)}, u32[]{:S(2)}, u32[]{:S(2)}) collective-permute-start(f32[1,128,128]{2,1,0:T(8,128)S(1)} %coupled_inverse.1), channel_id=1, source_target_pairs={{0,64},{64,0},{128,192},{192,128},{256,320},{320,256},{384,448},{4... | collective-permute-start | bytes 196616 | tf_op jit(solution)/shard_map/ppermute | solution.py:197
  27.8 0.9 collective-permute-done.3
  28.7 3.1 %collective-permute-start.4 = (f32[2,128,128]{2,1,0:T(8,128)S(1)}, f32[2,128,128]{2,1,0:T(8,128)S(1)}, u32[]{:S(2)}, u32[]{:S(2)}) collective-permute-start(f32[2,128,128]{2,1,0:T(8,128)S(1)} %pad_maximum_fusion.2), channel_id=1, source_target_pairs={{0,128},{64,192},{128,0},{192,64},{256,384},{320,448},{384,256},{4... | collective-permute-start | bytes 393224 | tf_op jit(solution)/shard_map/ppermute | solution.py:197
  31.8 0.0 collective-permute-done
  31.8 0.0 collective-permute-done.1
  31.8 0.0 collective-permute-done.2
  31.8 0.8 add_add_fusion
  32.6 6.1 %all-to-all-start = ((f32[16,32,128]{2,1,0:T(8,128)}), f32[16,32,128]{2,1,0:T(8,128)S(1)}, u32[]{:S(2)}, u32[]{:S(2)}) async-start(f32[16,32,128]{2,1,0:T(8,128)} %add_add_fusion), calls=%async_computation | async-start | bytes 524288 | tf_op jit(solution)/shard_map/all_to_all | solution.py:190
  38.7 0.0 collective-permute-done.4
  38.8 4.7 %collective-permute-start.5 = (f32[4,128,128]{2,1,0:T(8,128)S(1)}, f32[4,128,128]{2,1,0:T(8,128)S(1)}, u32[]{:S(2)}, u32[]{:S(2)}) collective-permute-start(f32[4,128,128]{2,1,0:T(8,128)S(1)} %pad_maximum_fusion.1), channel_id=1, source_target_pairs={{0,256},{64,320},{128,384},{192,448},{256,0},{320,64},{384,128},{4... | collective-permute-start | bytes 786440 | tf_op jit(solution)/shard_map/ppermute | solution.py:197
  43.4 7.4 %all-to-all-done.received_ref = f32[16,32,128]{2,1,0:T(8,128)S(1)} async-done(((f32[16,32,128]{2,1,0:T(8,128)}), f32[16,32,128]{2,1,0:T(8,128)S(1)}, u32[]{:S(2)}, u32[]{:S(2)}) %all-to-all-start) | async-done | bytes 262176 | tf_op jit(solution)/shard_map/all_to_all | solution.py:190
  50.8 0.0 copy-done.3
  50.8 0.8 reduce_right.1
  51.6 8.2 %all-to-all-start.1 = ((f32[8,32,128]{2,1,0:T(8,128)}), f32[8,32,128]{2,1,0:T(8,128)S(1)}, u32[]{:S(2)}, u32[]{:S(2)}) async-start(f32[8,32,128]{2,1,0:T(8,128)} %reduce_right.1), calls=%async_computation.1 | async-start | bytes 262144 | tf_op jit(solution)/shard_map/all_to_all | solution.py:261
  59.8 0.0 collective-permute-done.5
  59.9 5.2 %all-to-all-done.1.right_ref = f32[8,32,128]{2,1,0:T(8,128)S(1)} async-done(((f32[8,32,128]{2,1,0:T(8,128)}), f32[8,32,128]{2,1,0:T(8,128)S(1)}, u32[]{:S(2)}, u32[]{:S(2)}) %all-to-all-start.1) | async-done | bytes 131104 | tf_op jit(solution)/shard_map/all_to_all | solution.py:261
  65.1 2.7 %chain.1 = (f32[32,128]{1,0:T(8,128)}, f32[16,32,128]{2,1,0:T(8,128)}) custom-call(s32[1]{0:T(128)} %bitcast.2.group_ref, f32[8,32,128]{2,1,0:T(8,128)S(1)} %all-to-all-done.1.right_ref, f32[8,128,128]{2,1,0:T(8,128)S(1)} %pad_maximum_fusion.coupled_ref, f32[128,128]{1,0:T(8,128)S(1)} %bitcast.14), custom_call_target="tpu_custom_call" | custom-call | tf_op jit(solution)/shard_map/chain/pallas_call | solution.py:262
  67.8 3.5 %all-to-all-start.2 = ((f32[16,32,128]{2,1,0:T(8,128)}), f32[16,32,128]{2,1,0:T(8,128)S(1)}, u32[]{:S(2)}, u32[]{:S(2)}) async-start(f32[16,32,128]{2,1,0:T(8,128)} %get-tuple-element.19), calls=%async_computation.2 | async-start | bytes 524288 | tf_op jit(solution)/shard_map/all_to_all | solution.py:190
  71.3 8.5 %leaf_prepare.1 = (f32[32,3584]{1,0:T(8,128)S(1)}, bf16[28,128,256]{2,1,0:T(8,128)(2,1)S(1)}) custom-call(f32[28,32,128]{2,1,0:T(8,128)S(1)} %get-tuple-element.18.after_ref.y_ref, f32[28,128,128]{2,1,0:T(8,128)} %bitcast.18, f32[28,128,128]{2,1,0:T(8,128)} %bitcast.20, s32[28,1,128]{2,1,0:T(1,128)} %bitcast.24), custom_call_target="tpu_custom_call" | custom-call | tf_op jit(solution)/shard_map/leaf_prepare/pallas_call | solution.py:246
  79.8 0.0 copy-start.1
  79.8 0.8 copy-done.1
  80.6 4.2 %all-to-all-done.2.x0_ref = f32[16,32,128]{2,1,0:T(8,128)S(1)} async-done(((f32[16,32,128]{2,1,0:T(8,128)}), f32[16,32,128]{2,1,0:T(8,128)S(1)}, u32[]{:S(2)}, u32[]{:S(2)}) %all-to-all-start.2) | async-done | bytes 262176 | tf_op jit(solution)/shard_map/all_to_all | solution.py:190
  84.8 2.3 %collective-permute-start.8 = (f32[16,32,128]{2,1,0:T(8,128)S(1)}, f32[16,32,128]{2,1,0:T(8,128)S(1)}, u32[]{:S(2)}, u32[]{:S(2)}) collective-permute-start(f32[16,32,128]{2,1,0:T(8,128)S(1)} %all-to-all-done.2.x0_ref), channel_id=1, source_target_pairs={{0,63},{1,58},{2,57},{3,60},{4,59},{5,62},{6,61},{7,56},{8,23},{9,... | collective-permute-start | bytes 786440 | tf_op jit(solution)/shard_map/ppermute | solution.py:181
  87.1 4.6 %collective-permute-start.7 = (f32[16,32,128]{2,1,0:T(8,128)S(1)}, f32[16,32,128]{2,1,0:T(8,128)S(1)}, u32[]{:S(2)}, u32[]{:S(2)}) collective-permute-start(f32[16,32,128]{2,1,0:T(8,128)S(1)} %all-to-all-done.2.x0_ref), channel_id=1, source_target_pairs={{0,8},{1,9},{2,10},{3,11},{4,12},{5,13},{6,14},{7,15},{8,0},{9,1},... | collective-permute-start | bytes 786440 | tf_op jit(solution)/shard_map/ppermute | solution.py:181
  91.7 2.4 %collective-permute-start.6 = (f32[16,32,128]{2,1,0:T(8,128)S(1)}, f32[16,32,128]{2,1,0:T(8,128)S(1)}, u32[]{:S(2)}, u32[]{:S(2)}) collective-permute-start(f32[16,32,128]{2,1,0:T(8,128)S(1)} %all-to-all-done.2.x0_ref), channel_id=1, source_target_pairs={{0,1},{1,0},{2,3},{3,2},{4,5},{5,4},{6,7},{7,6},{8,9},{9,8},{10,11... | collective-permute-start | bytes 786440 | tf_op jit(solution)/shard_map/ppermute | solution.py:181
  94.1 1.8 %collective-permute-done.8.x3_ref = f32[16,32,128]{2,1,0:T(8,128)S(1)} collective-permute-done((f32[16,32,128]{2,1,0:T(8,128)S(1)}, f32[16,32,128]{2,1,0:T(8,128)S(1)}, u32[]{:S(2)}, u32[]{:S(2)}) %collective-permute-start.8) | collective-permute-done | bytes 262176 | tf_op jit(solution)/shard_map/ppermute | solution.py:181
  95.8 1.6 %collective-permute-done.7.x2_ref = f32[16,32,128]{2,1,0:T(8,128)S(1)} collective-permute-done((f32[16,32,128]{2,1,0:T(8,128)S(1)}, f32[16,32,128]{2,1,0:T(8,128)S(1)}, u32[]{:S(2)}, u32[]{:S(2)}) %collective-permute-start.7) | collective-permute-done | bytes 262176 | tf_op jit(solution)/shard_map/ppermute | solution.py:181
  97.4 2.8 %collective-permute-done.6.x1_ref = f32[16,32,128]{2,1,0:T(8,128)S(1)} collective-permute-done((f32[16,32,128]{2,1,0:T(8,128)S(1)}, f32[16,32,128]{2,1,0:T(8,128)S(1)}, u32[]{:S(2)}, u32[]{:S(2)}) %collective-permute-start.6) | collective-permute-done | bytes 262176 | tf_op jit(solution)/shard_map/ppermute | solution.py:181
  100.2 2.8 %leaf_backward.1 = f32[32,3584]{1,0:T(8,128)} custom-call(s32[1]{0:T(128)} %bitcast.class_ref, s32[28]{0:T(128)} %bitcast.26, f32[16,32,128]{2,1,0:T(8,128)S(1)} %all-to-all-done.2.x0_ref, f32[16,32,128]{2,1,0:T(8,128)S(1)} %collective-permute-done.6.x1_ref, f32[16,32,128]{2,1,0:T(8,128)S(1)} %collective-permute-done.7.x2_ref, ...), custom_call_target="tpu_custom_call" | custom-call | tf_op jit(solution)/shard_map/leaf_backward/pallas_call | solution.py:271
  (3 shorter events, 0.1 us)
Async XLA Ops:
  0.6 23.5 %copy-start = (f32[1,1,128,128]{3,2,1,0:T(8,128)S(1)}, f32[1,1,128,128]{3,2,1,0:T(8,128)}, u32[]{:S(2)}) copy-start(f32[1,1,128,128]{3,2,1,0:T(8,128)} %param.14) | copy-start | bytes 196612
  0.6 23.5 %copy-start.2 = (f32[1,1,128,128]{3,2,1,0:T(8,128)S(1)}, f32[1,1,128,128]{3,2,1,0:T(8,128)}, u32[]{:S(2)}) copy-start(f32[1,1,128,128]{3,2,1,0:T(8,128)} %param.15) | copy-start | bytes 196612
  4.5 46.3 %copy-start.3 = (f32[1,32,128]{2,1,0:T(8,128)S(1)}, f32[1,32,128]{2,1,0:T(8,128)}, u32[]{:S(2)}) copy-start(f32[1,32,128]{2,1,0:T(8,128)} %param.9) | copy-start | bytes 49156
  4.5 27.2 %collective-permute-start = (f32[16,32,128]{2,1,0:T(8,128)S(1)}, f32[16,32,128]{2,1,0:T(8,128)S(1)}, u32[]{:S(2)}, u32[]{:S(2)}) collective-permute-start(f32[16,32,128]{2,1,0:T(8,128)S(1)} %get-tuple-element.15), channel_id=1, source_target_pairs={{0,1},{1,0},{2,3},{3,2},{4,5},{5,4},{6,7},{7,6},{8,9},{9,8},{10,11... | collective-permute-start | bytes 786440 | tf_op jit(solution)/shard_map/ppermute | solution.py:181
  9.4 22.4 %collective-permute-start.1 = (f32[16,32,128]{2,1,0:T(8,128)S(1)}, f32[16,32,128]{2,1,0:T(8,128)S(1)}, u32[]{:S(2)}, u32[]{:S(2)}) collective-permute-start(f32[16,32,128]{2,1,0:T(8,128)S(1)} %get-tuple-element.16), channel_id=1, source_target_pairs={{0,8},{1,9},{2,10},{3,11},{4,12},{5,13},{6,14},{7,15},{8,0},{9,1},... | collective-permute-start | bytes 786440 | tf_op jit(solution)/shard_map/ppermute | solution.py:181
  12.6 19.2 %collective-permute-start.2 = (f32[16,32,128]{2,1,0:T(8,128)S(1)}, f32[16,32,128]{2,1,0:T(8,128)S(1)}, u32[]{:S(2)}, u32[]{:S(2)}) collective-permute-start(f32[16,32,128]{2,1,0:T(8,128)S(1)} %get-tuple-element.17), channel_id=1, source_target_pairs={{0,63},{1,58},{2,57},{3,60},{4,59},{5,62},{6,61},{7,56},{8,23},{9,... | collective-permute-start | bytes 786440 | tf_op jit(solution)/shard_map/ppermute | solution.py:181
  24.3 4.3 %collective-permute-start.3 = (f32[1,128,128]{2,1,0:T(8,128)S(1)}, f32[1,128,128]{2,1,0:T(8,128)S(1)}, u32[]{:S(2)}, u32[]{:S(2)}) collective-permute-start(f32[1,128,128]{2,1,0:T(8,128)S(1)} %coupled_inverse.1), channel_id=1, source_target_pairs={{0,64},{64,0},{128,192},{192,128},{256,320},{320,256},{384,448},{4... | collective-permute-start | bytes 196616 | tf_op jit(solution)/shard_map/ppermute | solution.py:197
  28.7 10.1 %collective-permute-start.4 = (f32[2,128,128]{2,1,0:T(8,128)S(1)}, f32[2,128,128]{2,1,0:T(8,128)S(1)}, u32[]{:S(2)}, u32[]{:S(2)}) collective-permute-start(f32[2,128,128]{2,1,0:T(8,128)S(1)} %pad_maximum_fusion.2), channel_id=1, source_target_pairs={{0,128},{64,192},{128,0},{192,64},{256,384},{320,448},{384,256},{4... | collective-permute-start | bytes 393224 | tf_op jit(solution)/shard_map/ppermute | solution.py:197
  32.6 18.2 %all-to-all-start = ((f32[16,32,128]{2,1,0:T(8,128)}), f32[16,32,128]{2,1,0:T(8,128)S(1)}, u32[]{:S(2)}, u32[]{:S(2)}) async-start(f32[16,32,128]{2,1,0:T(8,128)} %add_add_fusion), calls=%async_computation | async-start | bytes 524288 | tf_op jit(solution)/shard_map/all_to_all | solution.py:190
  38.8 21.1 %collective-permute-start.5 = (f32[4,128,128]{2,1,0:T(8,128)S(1)}, f32[4,128,128]{2,1,0:T(8,128)S(1)}, u32[]{:S(2)}, u32[]{:S(2)}) collective-permute-start(f32[4,128,128]{2,1,0:T(8,128)S(1)} %pad_maximum_fusion.1), channel_id=1, source_target_pairs={{0,256},{64,320},{128,384},{192,448},{256,0},{320,64},{384,128},{4... | collective-permute-start | bytes 786440 | tf_op jit(solution)/shard_map/ppermute | solution.py:197
  51.6 13.5 %all-to-all-start.1 = ((f32[8,32,128]{2,1,0:T(8,128)}), f32[8,32,128]{2,1,0:T(8,128)S(1)}, u32[]{:S(2)}, u32[]{:S(2)}) async-start(f32[8,32,128]{2,1,0:T(8,128)} %reduce_right.1), calls=%async_computation.1 | async-start | bytes 262144 | tf_op jit(solution)/shard_map/all_to_all | solution.py:261
  67.8 17.0 %all-to-all-start.2 = ((f32[16,32,128]{2,1,0:T(8,128)}), f32[16,32,128]{2,1,0:T(8,128)S(1)}, u32[]{:S(2)}, u32[]{:S(2)}) async-start(f32[16,32,128]{2,1,0:T(8,128)} %get-tuple-element.19), calls=%async_computation.2 | async-start | bytes 524288 | tf_op jit(solution)/shard_map/all_to_all | solution.py:190
  79.8 0.8 copy-start.1
  84.8 11.0 %collective-permute-start.8 = (f32[16,32,128]{2,1,0:T(8,128)S(1)}, f32[16,32,128]{2,1,0:T(8,128)S(1)}, u32[]{:S(2)}, u32[]{:S(2)}) collective-permute-start(f32[16,32,128]{2,1,0:T(8,128)S(1)} %all-to-all-done.2.x0_ref), channel_id=1, source_target_pairs={{0,63},{1,58},{2,57},{3,60},{4,59},{5,62},{6,61},{7,56},{8,23},{9,... | collective-permute-start | bytes 786440 | tf_op jit(solution)/shard_map/ppermute | solution.py:181
  87.1 10.3 %collective-permute-start.7 = (f32[16,32,128]{2,1,0:T(8,128)S(1)}, f32[16,32,128]{2,1,0:T(8,128)S(1)}, u32[]{:S(2)}, u32[]{:S(2)}) collective-permute-start(f32[16,32,128]{2,1,0:T(8,128)S(1)} %all-to-all-done.2.x0_ref), channel_id=1, source_target_pairs={{0,8},{1,9},{2,10},{3,11},{4,12},{5,13},{6,14},{7,15},{8,0},{9,1},... | collective-permute-start | bytes 786440 | tf_op jit(solution)/shard_map/ppermute | solution.py:181
  91.7 8.5 %collective-permute-start.6 = (f32[16,32,128]{2,1,0:T(8,128)S(1)}, f32[16,32,128]{2,1,0:T(8,128)S(1)}, u32[]{:S(2)}, u32[]{:S(2)}) collective-permute-start(f32[16,32,128]{2,1,0:T(8,128)S(1)} %all-to-all-done.2.x0_ref), channel_id=1, source_target_pairs={{0,1},{1,0},{2,3},{3,2},{4,5},{5,4},{6,7},{7,6},{8,9},{9,8},{10,11... | collective-permute-start | bytes 786440 | tf_op jit(solution)/shard_map/ppermute | solution.py:181

commit v5 on v3

--- a/solution.py
+++ b/solution.py
@@ -40,6 +40,12 @@
     return jnp.where(separator_row == row_index, 1.0, 0.0).astype(jnp.bfloat16)
 
 
+def slot_of(owner):
+    y, z = owner >> EDGE_BITS, owner & (EDGE - 1)
+    place = ((y >> 1) << (EDGE_BITS - 1)) | (z >> 1)
+    return (((y & 1) << 1) | (z & 1)) * (EDGE * EDGE // CLASSES) + place
+
+
 def leaf_forward(owner_ref, rhs_ref, inv_ref, update_ref, rows_ref, y_ref, dense_ref):
     step = pl.program_id(0)
     count, size, _ = inv_ref.shape
@@ -54,7 +60,7 @@
     updates = [product(leaf_y[f], update_ref[f], NT) for f in range(count)]
     placed = [select(updates[f], chosen_rows(rows_ref[f], size), NT) for f in range(count)]
     for f in range(count):
-        dense_ref[owner_ref[step * count + f]] = placed[f]
+        dense_ref[slot_of(owner_ref[step * count + f])] = placed[f]
 
 
 def coupled_inverse(inv_ref, couple_ref, after_ref, out_ref):
@@ -97,18 +103,37 @@
         copies_ref[copy] = x_sep
 
 
-def leaf_backward(owner_ref, x_ref, own_hbm, mapped_ref, out_ref, own_ref, arrived):
+def leaf_backward(owner_ref, x_ref, own_hbm, mapped_ref, out_hbm, own_ref, out_ref, own_arrived, stored):
     count, size, _ = mapped_ref.shape
     rows = out_ref.shape[0]
-    fetch = pltpu.make_async_copy(own_hbm, own_ref, arrived)
+    fetch = pltpu.make_async_copy(own_hbm, own_ref, own_arrived)
     fetch.start()
-    for f in range(count):
-        owned = jnp.concatenate(split(x_ref[owner_ref[f]]), axis=0)
-        out_ref[:, f * size : (f + 1) * size] = three_parts(dot(owned, mapped_ref[f], NN), rows, size)
-    fetch.wait()
-    out_ref[...] = own_ref[...] - out_ref[...]
-
-
+    width = BACKWARD_CHUNK * size
+    stores = []
+    for first in range(0, count, BACKWARD_CHUNK):
+        mapped = []
+        for f in range(first, first + BACKWARD_CHUNK):
+            owned = jnp.concatenate(split(x_ref[slot_of(owner_ref[f])]), axis=0)
+            mapped.append(three_parts(dot(owned, mapped_ref[f], NN), rows, size))
+        if first == 0:
+            fetch.wait()
+        for k, value in enumerate(mapped):
+            here = slice((first + k) * size, (first + k + 1) * size)
+            out_ref[:, here] = own_ref[:, here] - value
+        here = slice(first * size, first * size + width)
+        store = pltpu.make_async_copy(
+            out_ref.at[:, here], out_hbm.at[:, here], stored.at[first // BACKWARD_CHUNK]
+        )
+        store.start()
+        stores.append(store)
+    for store in stores:
+        store.wait()
+
+
+EDGE_BITS = 3
+EDGE = 1 << EDGE_BITS
+CLASSES = 4
+BACKWARD_CHUNK = 7
 FORWARD_STEP = 14
 PREPARE_STEP = 7
 VMEM = pl.BlockSpec(memory_space=pltpu.VMEM)
@@ -133,6 +158,31 @@
     )
 
 
+def exchange(value, groups_of_leaf):
+    fronts = lax.axis_size("front")
+    groups = [
+        [leaf * fronts + front for front in group]
+        for leaf in range(lax.axis_size("leaf"))
+        for group in groups_of_leaf(leaf)
+    ]
+    return lax.all_to_all(value, ("leaf", "front"), 0, 0, tiled=True, axis_index_groups=groups)
+
+
+def neighbours(leaf):
+    groups = []
+    for y in range(leaf % 2, EDGE + leaf % 2, 2):
+        for z in range(leaf % 2, EDGE + leaf % 2, 2):
+            four = [((y + a) % EDGE, (z + b) % EDGE) for a in range(2) for b in range(2)]
+            four.sort(key=lambda at: (at[0] % 2, at[1] % 2))
+            groups.append([a * EDGE + b for a, b in four])
+    return groups
+
+
+def members(leaf):
+    half = range(EDGE // 2)
+    return [[(2 * i + a) * EDGE + 2 * j + b for i in half for j in half] for a in range(2) for b in range(2)]
+
+
 def gather_by_bits(value, axis):
     count, bit = lax.axis_size(axis), 1
     while bit < count:
@@ -174,7 +224,8 @@
         [floats(front_count, width, size), floats(fronts, width, size)],
         grid=(front_count // FORWARD_STEP,),
     )(owners, right_leaf, inverse, coupling, rows)
-    received = lax.all_to_all(dense, "front", 0, 0, tiled=True)
+    received = exchange(dense, neighbours).reshape(CLASSES, fronts // CLASSES, width, size)
+    received = exchange(jnp.sum(received, axis=0), members)
 
     coupled = call(coupled_inverse, [VMEM, VMEM, ANY], VMEM, floats(1, size, size))(
         separator_inverse, separator_couple, leaf_y
@@ -201,18 +252,22 @@
         chain,
         [SMEM, VMEM, VMEM, VMEM],
         [VMEM, VMEM],
-        [floats(width, size), floats(fronts, width, size)],
+        [floats(width, size), floats(fronts // CLASSES, width, size)],
         scratch_shapes=[pltpu.VMEM((groups, width, size), jnp.float32)],
     )(lax.axis_index("leaf").reshape(1), right, coupled, separator_inverse)
-    gathered = lax.all_to_all(copies, "front", 0, 0, tiled=True)
+    gathered, own, mapped = lax.optimization_barrier((exchange(copies, members), own, mapped))
+    gathered = jnp.broadcast_to(gathered[None], (CLASSES, *gathered.shape)).reshape(fronts, width, size)
+    gathered = exchange(gathered, neighbours)
     x_leaf = call(
         leaf_backward,
         [SMEM, VMEM, ANY, VMEM],
-        VMEM,
+        ANY,
         floats(width, front_count * size),
         scratch_shapes=[
             pltpu.VMEM((width, front_count * size), jnp.float32),
+            pltpu.VMEM((width, front_count * size), jnp.float32),
             pltpu.SemaphoreType.DMA(()),
+            pltpu.SemaphoreType.DMA((front_count // BACKWARD_CHUNK,)),
         ],
     )(owners, gathered, own, mapped)
     return (x_leaf[None], x_sep[None])

time: 106 us -> 98.6 us (0.930)
  the two profiles are of different devices: /device:TPU:16 before, /device:TPU:1 now
where the time goes in v5:
time: 98.6 us; the launch traced here: 97.9 us
  starting transfers between devices  41.1 us (42%)
  waiting for transfers between devices  20.8 us (21%)
  Pallas kernels  19.6 us (20%)
  blocking collectives  14 us (14%)
    all_to_all x3, starting transfers between devices, exchange(): lax.all_to_all(value, ('leaf', 'front'), 0, 0, tiled=True, axis_index_gro...  24 us
    all_to_all x3, waiting for transfers between devices, exchange(): lax.all_to_all(value, ('leaf', 'front'), 0, 0, tiled=True, axis_index_gro...  14.4 us
    all_to_all x1, blocking collectives, exchange(): lax.all_to_all(value, ('leaf', 'front'), 0, 0, tiled=True, axis_index_gro...  14 us
    ppermute x3, starting transfers between devices, gather_by_bits(): value = jnp.concatenate([value, lax.ppermute(value, axis, pairs)], axis=0)  9.69 us
    pallas_call x1, Pallas kernels, per_device(): call(leaf_prepare, [vectors, matrices, matrices, lines], [columns, pl.Blo...  8.47 us
    all_to_all x1, starting transfers between devices, per_device(): right = lax.all_to_all(right, 'leaf', 0, 0, tiled=True)  7.4 us
    all_to_all x1, waiting for transfers between devices, per_device(): right = lax.all_to_all(right, 'leaf', 0, 0, tiled=True)  5.23 us
    pallas_call x1, Pallas kernels, per_device(): call(leaf_forward, [SMEM, columns, matrices, matrices, lines], [vectors,...  4.71 us
  transfers between devices with their start and end apart: 7, of which 5 were waited for; matrix products, arithmetic and copies ran while one was open for 1% of the time, Pallas kernels for 10%

profile of v5, /device:TPU:1, one launch (start us, length us, event | category | flops | bytes accessed | tf_op | source)
XLA Modules:
  0.0 97.9 jit_solution(543399688295007986)
XLA Ops:
  0.6 4.7 %leaf_forward.1 = (f32[28,32,128]{2,1,0:T(8,128)S(1)}, f32[64,32,128]{2,1,0:T(8,128)}) custom-call(s32[28]{0:T(128)} %bitcast.28, f32[32,3584]{1,0:T(8,128)} %bitcast.24, f32[28,128,128]{2,1,0:T(8,128)} %bitcast.18, f32[28,128,128]{2,1,0:T(8,128)} %bitcast.20, s32[28,1,128]{2,1,0:T(1,128)} %bitcast.26), custom_call_target="tpu_custom_call" | custom-call | tf_op jit(solution)/shard_map/leaf_forward/pallas_call | solution.py:220
  5.3 0.0 copy-start
  5.3 0.0 copy-start.2
  5.3 13.9 %all-to-all-start = ((f32[64,32,128]{2,1,0:T(8,128)}), f32[64,32,128]{2,1,0:T(8,128)S(1)}, u32[]{:S(2)}, u32[]{:S(2)}) async-start(f32[64,32,128]{2,1,0:T(8,128)} %get-tuple-element.11), calls=%async_computation | async-start | bytes 2097152 | tf_op jit(solution)/shard_map/all_to_all | solution.py:168
  19.2 0.0 copy-start.3
  19.3 0.0 copy-done
  19.3 0.0 copy-done.2
  19.3 0.2 coupled_inverse.1
  19.4 1.9 %collective-permute-start = (f32[1,128,128]{2,1,0:T(8,128)S(1)}, f32[1,128,128]{2,1,0:T(8,128)S(1)}, u32[]{:S(2)}, u32[]{:S(2)}) collective-permute-start(f32[1,128,128]{2,1,0:T(8,128)S(1)} %coupled_inverse.1), channel_id=1, source_target_pairs={{0,64},{64,0},{128,192},{192,128},{256,320},{320,256},{384,448},{4... | collective-permute-start | bytes 196616 | tf_op jit(solution)/shard_map/ppermute | solution.py:190
  21.4 1.2 %collective-permute-done = f32[1,128,128]{2,1,0:T(8,128)S(1)} collective-permute-done((f32[1,128,128]{2,1,0:T(8,128)S(1)}, f32[1,128,128]{2,1,0:T(8,128)S(1)}, u32[]{:S(2)}, u32[]{:S(2)}) %collective-permute-start) | collective-permute-done | bytes 65568 | tf_op jit(solution)/shard_map/ppermute | solution.py:190
  22.6 3.1 %collective-permute-start.1 = (f32[2,128,128]{2,1,0:T(8,128)S(1)}, f32[2,128,128]{2,1,0:T(8,128)S(1)}, u32[]{:S(2)}, u32[]{:S(2)}) collective-permute-start(f32[2,128,128]{2,1,0:T(8,128)S(1)} %pad_maximum_fusion.2), channel_id=1, source_target_pairs={{0,128},{64,192},{128,0},{192,64},{256,384},{320,448},{384,256},{4... | collective-permute-start | bytes 393224 | tf_op jit(solution)/shard_map/ppermute | solution.py:190
  25.7 3.0 %all-to-all-done = f32[64,32,128]{2,1,0:T(8,128)S(1)} async-done(((f32[64,32,128]{2,1,0:T(8,128)}), f32[64,32,128]{2,1,0:T(8,128)S(1)}, u32[]{:S(2)}, u32[]{:S(2)}) %all-to-all-start) | async-done | bytes 1048608 | tf_op jit(solution)/shard_map/all_to_all | solution.py:168
  28.7 0.8 reduce_sum.9
  29.5 5.9 %all-to-all-start.1 = ((f32[16,32,128]{2,1,0:T(8,128)}), f32[16,32,128]{2,1,0:T(8,128)S(1)}, u32[]{:S(2)}, u32[]{:S(2)}) async-start(f32[16,32,128]{2,1,0:T(8,128)} %reduce_sum.9), calls=%async_computation.1 | async-start | bytes 524288 | tf_op jit(solution)/shard_map/all_to_all | solution.py:168
  35.5 0.0 collective-permute-done.1
  35.5 4.7 %collective-permute-start.2 = (f32[4,128,128]{2,1,0:T(8,128)S(1)}, f32[4,128,128]{2,1,0:T(8,128)S(1)}, u32[]{:S(2)}, u32[]{:S(2)}) collective-permute-start(f32[4,128,128]{2,1,0:T(8,128)S(1)} %pad_maximum_fusion.1), channel_id=1, source_target_pairs={{0,256},{64,320},{128,384},{192,448},{256,0},{320,64},{384,128},{4... | collective-permute-start | bytes 786440 | tf_op jit(solution)/shard_map/ppermute | solution.py:190
  40.2 7.6 %all-to-all-done.1.received_ref = f32[16,32,128]{2,1,0:T(8,128)S(1)} async-done(((f32[16,32,128]{2,1,0:T(8,128)}), f32[16,32,128]{2,1,0:T(8,128)S(1)}, u32[]{:S(2)}, u32[]{:S(2)}) %all-to-all-start.1) | async-done | bytes 262176 | tf_op jit(solution)/shard_map/all_to_all | solution.py:168
  47.8 0.0 copy-done.3
  47.8 0.8 reduce_right.1
  48.6 7.4 %all-to-all-start.2 = ((f32[8,32,128]{2,1,0:T(8,128)}), f32[8,32,128]{2,1,0:T(8,128)S(1)}, u32[]{:S(2)}, u32[]{:S(2)}) async-start(f32[8,32,128]{2,1,0:T(8,128)} %reduce_right.1), calls=%async_computation.2 | async-start | bytes 262144 | tf_op jit(solution)/shard_map/all_to_all | solution.py:250
  56.0 0.0 collective-permute-done.2
  56.1 5.2 %all-to-all-done.2.right_ref = f32[8,32,128]{2,1,0:T(8,128)S(1)} async-done(((f32[8,32,128]{2,1,0:T(8,128)}), f32[8,32,128]{2,1,0:T(8,128)S(1)}, u32[]{:S(2)}, u32[]{:S(2)}) %all-to-all-start.2) | async-done | bytes 131104 | tf_op jit(solution)/shard_map/all_to_all | solution.py:250
  61.3 2.7 %chain.1 = (f32[32,128]{1,0:T(8,128)}, f32[16,32,128]{2,1,0:T(8,128)}) custom-call(s32[1]{0:T(128)} %bitcast.1.group_ref, f32[8,32,128]{2,1,0:T(8,128)S(1)} %all-to-all-done.2.right_ref, f32[8,128,128]{2,1,0:T(8,128)S(1)} %pad_maximum_fusion.coupled_ref, f32[128,128]{1,0:T(8,128)S(1)} %bitcast.15), custom_call_target="tpu_custom_call" | custom-call | tf_op jit(solution)/shard_map/chain/pallas_call | solution.py:251
  64.0 4.1 %all-to-all-start.3 = ((f32[16,32,128]{2,1,0:T(8,128)}), f32[16,32,128]{2,1,0:T(8,128)S(1)}, u32[]{:S(2)}, u32[]{:S(2)}) async-start(f32[16,32,128]{2,1,0:T(8,128)} %get-tuple-element.13), calls=%async_computation.3 | async-start | bytes 524288 | tf_op jit(solution)/shard_map/all_to_all | solution.py:168
  68.1 8.5 %leaf_prepare.1 = (f32[32,3584]{1,0:T(8,128)S(1)}, bf16[28,128,256]{2,1,0:T(8,128)(2,1)S(1)}) custom-call(f32[28,32,128]{2,1,0:T(8,128)S(1)} %get-tuple-element.12.after_ref.y_ref, f32[28,128,128]{2,1,0:T(8,128)} %bitcast.19, f32[28,128,128]{2,1,0:T(8,128)} %bitcast.21, s32[28,1,128]{2,1,0:T(1,128)} %bitcast.27), custom_call_target="tpu_custom_call" | custom-call | tf_op jit(solution)/shard_map/leaf_prepare/pallas_call | solution.py:235
  76.6 0.0 copy-start.1
  76.6 0.8 copy-done.1
  77.4 3.7 %all-to-all-done.3 = f32[16,32,128]{2,1,0:T(8,128)S(1)} async-done(((f32[16,32,128]{2,1,0:T(8,128)}), f32[16,32,128]{2,1,0:T(8,128)S(1)}, u32[]{:S(2)}, u32[]{:S(2)}) %all-to-all-start.3) | async-done | bytes 262176 | tf_op jit(solution)/shard_map/all_to_all | solution.py:168
  81.1 0.1 broadcast_in_dim.12
  81.2 14.0 %all_to_all.25.x_ref = f32[64,32,128]{2,1,0:T(8,128)S(1)} all-to-all(f32[64,32,128]{2,1,0:T(8,128)S(1)} %bitcast.22), channel_id=1, replica_groups={{0,1,8,9},{2,3,10,11},{4,5,12,13},{6,7,14,15},{16,17,24,25},{18,19,26,2..., dimensions={0} | all-to-all | bytes 2097152 | tf_op jit(solution)/shard_map/all_to_all | solution.py:168
  95.2 2.7 %leaf_backward.1 = f32[32,3584]{1,0:T(8,128)} custom-call(s32[28]{0:T(128)} %bitcast.29, f32[64,32,128]{2,1,0:T(8,128)S(1)} %all_to_all.25.x_ref, f32[32,3584]{1,0:T(8,128)} %copy-done.1, bf16[28,128,256]{2,1,0:T(8,128)(2,1)S(1)} %get-tuple-element.18.mapped_ref), custom_call_target="tpu_custom_call" | custom-call | tf_op jit(solution)/shard_map/leaf_backward/pallas_call | solution.py:261
  (3 shorter events, 0.1 us)
Async XLA Ops:
  5.3 13.9 %copy-start = (f32[1,1,128,128]{3,2,1,0:T(8,128)S(1)}, f32[1,1,128,128]{3,2,1,0:T(8,128)}, u32[]{:S(2)}) copy-start(f32[1,1,128,128]{3,2,1,0:T(8,128)} %param.14) | copy-start | bytes 196612
  5.3 13.9 %copy-start.2 = (f32[1,1,128,128]{3,2,1,0:T(8,128)S(1)}, f32[1,1,128,128]{3,2,1,0:T(8,128)}, u32[]{:S(2)}) copy-start(f32[1,1,128,128]{3,2,1,0:T(8,128)} %param.15) | copy-start | bytes 196612
  5.3 23.4 %all-to-all-start = ((f32[64,32,128]{2,1,0:T(8,128)}), f32[64,32,128]{2,1,0:T(8,128)S(1)}, u32[]{:S(2)}, u32[]{:S(2)}) async-start(f32[64,32,128]{2,1,0:T(8,128)} %get-tuple-element.11), calls=%async_computation | async-start | bytes 2097152 | tf_op jit(solution)/shard_map/all_to_all | solution.py:168
  19.2 28.6 %copy-start.3 = (f32[1,32,128]{2,1,0:T(8,128)S(1)}, f32[1,32,128]{2,1,0:T(8,128)}, u32[]{:S(2)}) copy-start(f32[1,32,128]{2,1,0:T(8,128)} %param.9) | copy-start | bytes 49156
  19.4 3.1 %collective-permute-start = (f32[1,128,128]{2,1,0:T(8,128)S(1)}, f32[1,128,128]{2,1,0:T(8,128)S(1)}, u32[]{:S(2)}, u32[]{:S(2)}) collective-permute-start(f32[1,128,128]{2,1,0:T(8,128)S(1)} %coupled_inverse.1), channel_id=1, source_target_pairs={{0,64},{64,0},{128,192},{192,128},{256,320},{320,256},{384,448},{4... | collective-permute-start | bytes 196616 | tf_op jit(solution)/shard_map/ppermute | solution.py:190
  22.6 12.9 %collective-permute-start.1 = (f32[2,128,128]{2,1,0:T(8,128)S(1)}, f32[2,128,128]{2,1,0:T(8,128)S(1)}, u32[]{:S(2)}, u32[]{:S(2)}) collective-permute-start(f32[2,128,128]{2,1,0:T(8,128)S(1)} %pad_maximum_fusion.2), channel_id=1, source_target_pairs={{0,128},{64,192},{128,0},{192,64},{256,384},{320,448},{384,256},{4... | collective-permute-start | bytes 393224 | tf_op jit(solution)/shard_map/ppermute | solution.py:190
  29.5 18.3 %all-to-all-start.1 = ((f32[16,32,128]{2,1,0:T(8,128)}), f32[16,32,128]{2,1,0:T(8,128)S(1)}, u32[]{:S(2)}, u32[]{:S(2)}) async-start(f32[16,32,128]{2,1,0:T(8,128)} %reduce_sum.9), calls=%async_computation.1 | async-start | bytes 524288 | tf_op jit(solution)/shard_map/all_to_all | solution.py:168
  35.5 20.5 %collective-permute-start.2 = (f32[4,128,128]{2,1,0:T(8,128)S(1)}, f32[4,128,128]{2,1,0:T(8,128)S(1)}, u32[]{:S(2)}, u32[]{:S(2)}) collective-permute-start(f32[4,128,128]{2,1,0:T(8,128)S(1)} %pad_maximum_fusion.1), channel_id=1, source_target_pairs={{0,256},{64,320},{128,384},{192,448},{256,0},{320,64},{384,128},{4... | collective-permute-start | bytes 786440 | tf_op jit(solution)/shard_map/ppermute | solution.py:190
  48.6 12.7 %all-to-all-start.2 = ((f32[8,32,128]{2,1,0:T(8,128)}), f32[8,32,128]{2,1,0:T(8,128)S(1)}, u32[]{:S(2)}, u32[]{:S(2)}) async-start(f32[8,32,128]{2,1,0:T(8,128)} %reduce_right.1), calls=%async_computation.2 | async-start | bytes 262144 | tf_op jit(solution)/shard_map/all_to_all | solution.py:250
  64.0 17.1 %all-to-all-start.3 = ((f32[16,32,128]{2,1,0:T(8,128)}), f32[16,32,128]{2,1,0:T(8,128)S(1)}, u32[]{:S(2)}, u32[]{:S(2)}) async-start(f32[16,32,128]{2,1,0:T(8,128)} %get-tuple-element.13), calls=%async_computation.3 | async-start | bytes 524288 | tf_op jit(solution)/shard_map/all_to_all | solution.py:168
  76.6 0.8 copy-start.1

commit v6 on v5

--- a/solution.py
+++ b/solution.py
@@ -67,14 +67,14 @@
     out_ref[0] = product(inv_ref[...], couple_ref[...], NN)
 
 
-def leaf_prepare(y_ref, inv_ref, update_ref, rows_ref, own_ref, mapped_ref):
+def leaf_prepare(y_ref, inv_ref, update_ref, rows_ref, mapped_ref):
     count, size, _ = inv_ref.shape
     for f in range(count):
         inverse = inv_ref[f]
-        own_ref[:, f * size : (f + 1) * size] = product(y_ref[f], inverse, NN)
+        mapped_ref[f, size:] = jnp.concatenate(split(product(y_ref[f], inverse, NN)), axis=1)
         mapped = jnp.concatenate(split(product(update_ref[f], inverse, NN)), axis=1)
         placed = dot(chosen_rows(rows_ref[f], size), mapped, NN)
-        mapped_ref[f] = jnp.concatenate(split(placed[:, :size] + placed[:, size:]), axis=1)
+        mapped_ref[f, :size] = jnp.concatenate(split(placed[:, :size] + placed[:, size:]), axis=1)
 
 
 def reduce_right(received_ref, rhs_ref, inv_ref, out_ref):
@@ -103,29 +103,23 @@
         copies_ref[copy] = x_sep
 
 
-def leaf_backward(owner_ref, x_ref, own_hbm, mapped_ref, out_hbm, own_ref, out_ref, own_arrived, stored):
-    count, size, _ = mapped_ref.shape
+def leaf_backward(owner_ref, x_ref, mapped_ref, out_hbm, out_ref, stored):
+    count = mapped_ref.shape[0]
     rows = out_ref.shape[0]
-    fetch = pltpu.make_async_copy(own_hbm, own_ref, own_arrived)
-    fetch.start()
-    width = BACKWARD_CHUNK * size
+    size = out_ref.shape[1] // count
     stores = []
-    for first in range(0, count, BACKWARD_CHUNK):
-        mapped = []
-        for f in range(first, first + BACKWARD_CHUNK):
-            owned = jnp.concatenate(split(x_ref[slot_of(owner_ref[f])]), axis=0)
-            mapped.append(three_parts(dot(owned, mapped_ref[f], NN), rows, size))
-        if first == 0:
-            fetch.wait()
-        for k, value in enumerate(mapped):
-            here = slice((first + k) * size, (first + k + 1) * size)
-            out_ref[:, here] = own_ref[:, here] - value
-        here = slice(first * size, first * size + width)
-        store = pltpu.make_async_copy(
-            out_ref.at[:, here], out_hbm.at[:, here], stored.at[first // BACKWARD_CHUNK]
-        )
-        store.start()
-        stores.append(store)
+    for f in range(count):
+        owned = jnp.concatenate(split(x_ref[slot_of(owner_ref[f])]), axis=0)
+        picked = three_parts(dot(owned, mapped_ref[f, :size], NN), rows, size)
+        own = mapped_ref[f, size:].astype(jnp.float32)
+        out_ref[:, f * size : (f + 1) * size] = (own[:, :size] + own[:, size:]) - picked
+        if (f + 1) % BACKWARD_CHUNK == 0:
+            here = slice((f + 1 - BACKWARD_CHUNK) * size, (f + 1) * size)
+            store = pltpu.make_async_copy(
+                out_ref.at[:, here], out_hbm.at[:, here], stored.at[f // BACKWARD_CHUNK]
+            )
+            store.start()
+            stores.append(store)
     for store in stores:
         store.wait()
 
@@ -232,20 +226,20 @@
     )
     coupled = gather_by_bits(coupled, "leaf")
     matrices, lines, vectors, columns = specs(PREPARE_STEP)
-    own, mapped = call(
+    mapped = call(
         leaf_prepare,
         [vectors, matrices, matrices, lines],
-        [columns, pl.BlockSpec((PREPARE_STEP, size, 2 * size), lambda s: (s, 0, 0))],
-        [
-            floats(width, front_count * size),
-            jax.ShapeDtypeStruct((front_count, size, 2 * size), jnp.bfloat16),
-        ],
+        pl.BlockSpec((PREPARE_STEP, size + width, 2 * size), lambda s: (s, 0, 0)),
+        jax.ShapeDtypeStruct((front_count, size + width, 2 * size), jnp.bfloat16),
         grid=(front_count // PREPARE_STEP,),
     )(leaf_y, inverse, coupling, rows)
 
-    own = stay(own)
     right = call(reduce_right, [VMEM, VMEM, VMEM], VMEM, floats(groups, width, size))(
         received, rhs_sep[0], separator_inverse
+    )
+    group = lax.axis_index("leaf").reshape(1)
+    right, coupled, group, separator_inverse = lax.optimization_barrier(
+        (right, coupled, group, separator_inverse)
     )
     right = lax.all_to_all(right, "leaf", 0, 0, tiled=True)
     x_sep, copies = call(
@@ -254,22 +248,20 @@
         [VMEM, VMEM],
         [floats(width, size), floats(fronts // CLASSES, width, size)],
         scratch_shapes=[pltpu.VMEM((groups, width, size), jnp.float32)],
-    )(lax.axis_index("leaf").reshape(1), right, coupled, separator_inverse)
-    gathered, own, mapped = lax.optimization_barrier((exchange(copies, members), own, mapped))
+    )(group, right, coupled, separator_inverse)
+    gathered, mapped = lax.optimization_barrier((exchange(copies, members), mapped))
     gathered = jnp.broadcast_to(gathered[None], (CLASSES, *gathered.shape)).reshape(fronts, width, size)
     gathered = exchange(gathered, neighbours)
     x_leaf = call(
         leaf_backward,
-        [SMEM, VMEM, ANY, VMEM],
+        [SMEM, VMEM, VMEM],
         ANY,
         floats(width, front_count * size),
         scratch_shapes=[
             pltpu.VMEM((width, front_count * size), jnp.float32),
-            pltpu.VMEM((width, front_count * size), jnp.float32),
-            pltpu.SemaphoreType.DMA(()),
             pltpu.SemaphoreType.DMA((front_count // BACKWARD_CHUNK,)),
         ],
-    )(owners, gathered, own, mapped)
+    )(update_owner.reshape(front_count), gathered, mapped)
     return (x_leaf[None], x_sep[None])
 
 

time: 98.6 us -> 101 us (1.024)
  blocking collectives: 14 us -> 27.3 us
  waiting for transfers between devices: 20.8 us -> 15.7 us
  starting transfers between devices: 41.1 us -> 37.8 us
  Pallas kernels: 19.6 us -> 17.8 us
    all_to_all x0 -> x1, blocking collectives: none -> 12.5 us  [per_device(): right = lax.all_to_all(right, 'leaf', 0, 0, tiled=True)]
    all_to_all x1 -> x0, starting transfers between devices: 7.4 us -> none  [per_device(): right = lax.all_to_all(right, 'leaf', 0, 0, tiled=True)]
    ppermute x3, waiting for transfers between devices: 1.23 us -> 6.87 us  [gather_by_bits(): value = jnp.concatenate([value, lax.ppermute(value, axis, pairs)], axis=0)]
    all_to_all x3, waiting for transfers between devices: 14.4 us -> 8.83 us  [exchange(): lax.all_to_all(value, ('leaf', 'front'), 0, 0, tiled=True, axis_index_gro...]
    all_to_all x1 -> x0, waiting for transfers between devices: 5.23 us -> none  [per_device(): right = lax.all_to_all(right, 'leaf', 0, 0, tiled=True)]
    all_to_all x3, starting transfers between devices: 24 us -> 28.1 us  [exchange(): lax.all_to_all(value, ('leaf', 'front'), 0, 0, tiled=True, axis_index_gro...]
    pallas_call x2, Pallas kernels: 11.2 us -> 10.1 us  [the longest x1 8.46 us: per_device(): call(leaf_prepare, [vectors, matrices, matrices, lines], pl.BlockSpec((PR...]
  transfers between devices with their start and end apart: 7 -> 6, of which waited for: 5 -> 5; matrix products, arithmetic and copies ran while one was open for 1% -> 1% of each run, Pallas kernels for 10% -> 9%
where the time goes in v6:
time: 101 us; the launch traced here: 100 us
  starting transfers between devices  37.8 us (37%)
  blocking collectives  27.3 us (27%)
  Pallas kernels  17.8 us (18%)
  waiting for transfers between devices  15.7 us (16%)
    all_to_all x3, starting transfers between devices, exchange(): lax.all_to_all(value, ('leaf', 'front'), 0, 0, tiled=True, axis_index_gro...  28.1 us
    all_to_all x1, blocking collectives, exchange(): lax.all_to_all(value, ('leaf', 'front'), 0, 0, tiled=True, axis_index_gro...  14.8 us
    all_to_all x1, blocking collectives, per_device(): right = lax.all_to_all(right, 'leaf', 0, 0, tiled=True)  12.5 us
    ppermute x3, starting transfers between devices, gather_by_bits(): value = jnp.concatenate([value, lax.ppermute(value, axis, pairs)], axis=0)  9.69 us
    all_to_all x3, waiting for transfers between devices, exchange(): lax.all_to_all(value, ('leaf', 'front'), 0, 0, tiled=True, axis_index_gro...  8.83 us
    pallas_call x1, Pallas kernels, per_device(): call(leaf_prepare, [vectors, matrices, matrices, lines], pl.BlockSpec((PR...  8.46 us
    ppermute x3, waiting for transfers between devices, gather_by_bits(): value = jnp.concatenate([value, lax.ppermute(value, axis, pairs)], axis=0)  6.87 us
    pallas_call x1, Pallas kernels, per_device(): call(leaf_forward, [SMEM, columns, matrices, matrices, lines], [vectors,...  4.71 us
  transfers between devices with their start and end apart: 6, of which 5 were waited for; matrix products, arithmetic and copies ran while one was open for 1% of the time, Pallas kernels for 9%

profile of v6, /device:TPU:1, one launch (start us, length us, event | category | flops | bytes accessed | tf_op | source)
XLA Modules:
  0.0 100.3 jit_solution(9905925804740312499)
XLA Ops:
  0.6 4.7 %leaf_forward.1 = (f32[28,32,128]{2,1,0:T(8,128)S(1)}, f32[64,32,128]{2,1,0:T(8,128)}) custom-call(s32[28]{0:T(128)} %bitcast.18, f32[32,3584]{1,0:T(8,128)} %bitcast.26, f32[28,128,128]{2,1,0:T(8,128)} %bitcast.20, f32[28,128,128]{2,1,0:T(8,128)} %bitcast.22, s32[28,1,128]{2,1,0:T(1,128)} %bitcast.28), custom_call_target="tpu_custom_call" | custom-call | tf_op jit(solution)/shard_map/leaf_forward/pallas_call | solution.py:214
  5.3 0.0 copy-start
  5.3 0.0 copy-start.1
  5.3 13.9 %all-to-all-start = ((f32[64,32,128]{2,1,0:T(8,128)}), f32[64,32,128]{2,1,0:T(8,128)S(1)}, u32[]{:S(2)}, u32[]{:S(2)}) async-start(f32[64,32,128]{2,1,0:T(8,128)} %get-tuple-element.12), calls=%async_computation | async-start | bytes 2097152 | tf_op jit(solution)/shard_map/all_to_all | solution.py:162
  19.2 0.0 copy-done
  19.2 0.0 copy-done.1
  19.2 0.2 coupled_inverse.1
  19.4 0.0 copy-start.2
  19.4 1.9 %collective-permute-start = (f32[1,128,128]{2,1,0:T(8,128)S(1)}, f32[1,128,128]{2,1,0:T(8,128)S(1)}, u32[]{:S(2)}, u32[]{:S(2)}) collective-permute-start(f32[1,128,128]{2,1,0:T(8,128)S(1)} %coupled_inverse.1), channel_id=1, source_target_pairs={{0,64},{64,0},{128,192},{192,128},{256,320},{320,256},{384,448},{4... | collective-permute-start | bytes 196616 | tf_op jit(solution)/shard_map/ppermute | solution.py:184
  21.4 1.2 %collective-permute-done = f32[1,128,128]{2,1,0:T(8,128)S(1)} collective-permute-done((f32[1,128,128]{2,1,0:T(8,128)S(1)}, f32[1,128,128]{2,1,0:T(8,128)S(1)}, u32[]{:S(2)}, u32[]{:S(2)}) %collective-permute-start) | collective-permute-done | bytes 65568 | tf_op jit(solution)/shard_map/ppermute | solution.py:184
  22.6 3.1 %collective-permute-start.1 = (f32[2,128,128]{2,1,0:T(8,128)S(1)}, f32[2,128,128]{2,1,0:T(8,128)S(1)}, u32[]{:S(2)}, u32[]{:S(2)}) collective-permute-start(f32[2,128,128]{2,1,0:T(8,128)S(1)} %pad_maximum_fusion.2), channel_id=1, source_target_pairs={{0,128},{64,192},{128,0},{192,64},{256,384},{320,448},{384,256},{4... | collective-permute-start | bytes 393224 | tf_op jit(solution)/shard_map/ppermute | solution.py:184
  25.7 3.0 %all-to-all-done = f32[64,32,128]{2,1,0:T(8,128)S(1)} async-done(((f32[64,32,128]{2,1,0:T(8,128)}), f32[64,32,128]{2,1,0:T(8,128)S(1)}, u32[]{:S(2)}, u32[]{:S(2)}) %all-to-all-start) | async-done | bytes 1048608 | tf_op jit(solution)/shard_map/all_to_all | solution.py:162
  28.7 0.8 reduce_sum.9
  29.5 5.9 %all-to-all-start.1 = ((f32[16,32,128]{2,1,0:T(8,128)}), f32[16,32,128]{2,1,0:T(8,128)S(1)}, u32[]{:S(2)}, u32[]{:S(2)}) async-start(f32[16,32,128]{2,1,0:T(8,128)} %reduce_sum.9), calls=%async_computation.1 | async-start | bytes 524288 | tf_op jit(solution)/shard_map/all_to_all | solution.py:162
  35.5 0.0 collective-permute-done.1
  35.5 4.7 %collective-permute-start.2 = (f32[4,128,128]{2,1,0:T(8,128)S(1)}, f32[4,128,128]{2,1,0:T(8,128)S(1)}, u32[]{:S(2)}, u32[]{:S(2)}) collective-permute-start(f32[4,128,128]{2,1,0:T(8,128)S(1)} %pad_maximum_fusion.1), channel_id=1, source_target_pairs={{0,256},{64,320},{128,384},{192,448},{256,0},{320,64},{384,128},{4... | collective-permute-start | bytes 786440 | tf_op jit(solution)/shard_map/ppermute | solution.py:184
  40.2 5.7 %collective-permute-done.2 = f32[4,128,128]{2,1,0:T(8,128)S(1)} collective-permute-done((f32[4,128,128]{2,1,0:T(8,128)S(1)}, f32[4,128,128]{2,1,0:T(8,128)S(1)}, u32[]{:S(2)}, u32[]{:S(2)}) %collective-permute-start.2) | collective-permute-done | bytes 262176 | tf_op jit(solution)/shard_map/ppermute | solution.py:184
  45.9 2.0 %all-to-all-done.1.received_ref = f32[16,32,128]{2,1,0:T(8,128)S(1)} async-done(((f32[16,32,128]{2,1,0:T(8,128)}), f32[16,32,128]{2,1,0:T(8,128)S(1)}, u32[]{:S(2)}, u32[]{:S(2)}) %all-to-all-start.1) | async-done | bytes 262176 | tf_op jit(solution)/shard_map/all_to_all | solution.py:162
  47.8 0.0 copy-done.2
  47.8 0.2 reduce_right.1
  48.0 12.5 %all_to_all.25.right_ref = f32[8,32,128]{2,1,0:T(8,128)S(1)} all-to-all(f32[8,32,128]{2,1,0:T(8,128)S(1)} %reduce_right.1), channel_id=1, replica_groups=mesh['leaf'=8,'front'=64] {'leaf'}, dimensions={0} | all-to-all | bytes 262144 | tf_op jit(solution)/shard_map/all_to_all | solution.py:244
  60.5 2.7 %chain.1 = (f32[32,128]{1,0:T(8,128)}, f32[16,32,128]{2,1,0:T(8,128)}) custom-call(s32[1]{0:T(128)} %bitcast.9.group_ref, f32[8,32,128]{2,1,0:T(8,128)S(1)} %all_to_all.25.right_ref, f32[8,128,128]{2,1,0:T(8,128)S(1)} %pad_maximum_fusion.coupled_ref, f32[128,128]{1,0:T(8,128)S(1)} %bitcast.15), custom_call_target="tpu_custom_call" | custom-call | tf_op jit(solution)/shard_map/chain/pallas_call | solution.py:245
  63.1 8.2 %all-to-all-start.3 = ((f32[16,32,128]{2,1,0:T(8,128)}), f32[16,32,128]{2,1,0:T(8,128)S(1)}, u32[]{:S(2)}, u32[]{:S(2)}) async-start(f32[16,32,128]{2,1,0:T(8,128)} %get-tuple-element.18), calls=%async_computation.3 | async-start | bytes 524288 | tf_op jit(solution)/shard_map/all_to_all | solution.py:162
  71.4 8.5 %leaf_prepare.1.mapped_ref = bf16[28,160,256]{2,1,0:T(8,128)(2,1)S(1)} custom-call(f32[28,32,128]{2,1,0:T(8,128)S(1)} %get-tuple-element.13.after_ref.y_ref, f32[28,128,128]{2,1,0:T(8,128)} %bitcast.21, f32[28,128,128]{2,1,0:T(8,128)} %bitcast.23, s32[28,1,128]{2,1,0:T(1,128)} %bitcast.29), custom_call_target="tpu_custom_call" | custom-call | tf_op jit(solution)/shard_map/leaf_prepare/pallas_call | solution.py:229
  79.8 0.0 copy-start.3
  79.9 3.9 %all-to-all-done.3 = f32[16,32,128]{2,1,0:T(8,128)S(1)} async-done(((f32[16,32,128]{2,1,0:T(8,128)}), f32[16,32,128]{2,1,0:T(8,128)S(1)}, u32[]{:S(2)}, u32[]{:S(2)}) %all-to-all-start.3) | async-done | bytes 262176 | tf_op jit(solution)/shard_map/all_to_all | solution.py:162
  83.7 0.1 broadcast_in_dim.12
  83.9 14.8 %all_to_all.26.x_ref = f32[64,32,128]{2,1,0:T(8,128)S(1)} all-to-all(f32[64,32,128]{2,1,0:T(8,128)S(1)} %bitcast.24), channel_id=1, replica_groups={{0,1,8,9},{2,3,10,11},{4,5,12,13},{6,7,14,15},{16,17,24,25},{18,19,26,2..., dimensions={0} | all-to-all | bytes 2097152 | tf_op jit(solution)/shard_map/all_to_all | solution.py:162
  98.7 0.0 copy-done.3
  98.7 1.6 %leaf_backward.1 = f32[32,3584]{1,0:T(8,128)} custom-call(s32[28]{0:T(128)S(1)} %bitcast.19, f32[64,32,128]{2,1,0:T(8,128)S(1)} %all_to_all.26.x_ref, bf16[28,160,256]{2,1,0:T(8,128)(2,1)S(1)} %leaf_prepare.1.mapped_ref), custom_call_target="tpu_custom_call" | custom-call | tf_op jit(solution)/shard_map/leaf_backward/pallas_call | solution.py:255
  (3 shorter events, 0.1 us)
Async XLA Ops:
  5.3 13.9 %copy-start = (f32[1,1,128,128]{3,2,1,0:T(8,128)S(1)}, f32[1,1,128,128]{3,2,1,0:T(8,128)}, u32[]{:S(2)}) copy-start(f32[1,1,128,128]{3,2,1,0:T(8,128)} %param.14) | copy-start | bytes 196612
  5.3 13.9 %copy-start.1 = (f32[1,1,128,128]{3,2,1,0:T(8,128)S(1)}, f32[1,1,128,128]{3,2,1,0:T(8,128)}, u32[]{:S(2)}) copy-start(f32[1,1,128,128]{3,2,1,0:T(8,128)} %param.15) | copy-start | bytes 196612
  5.3 23.4 %all-to-all-start = ((f32[64,32,128]{2,1,0:T(8,128)}), f32[64,32,128]{2,1,0:T(8,128)S(1)}, u32[]{:S(2)}, u32[]{:S(2)}) async-start(f32[64,32,128]{2,1,0:T(8,128)} %get-tuple-element.12), calls=%async_computation | async-start | bytes 2097152 | tf_op jit(solution)/shard_map/all_to_all | solution.py:162
  19.4 28.4 %copy-start.2 = (f32[1,32,128]{2,1,0:T(8,128)S(1)}, f32[1,32,128]{2,1,0:T(8,128)}, u32[]{:S(2)}) copy-start(f32[1,32,128]{2,1,0:T(8,128)} %param.9) | copy-start | bytes 49156
  19.4 3.1 %collective-permute-start = (f32[1,128,128]{2,1,0:T(8,128)S(1)}, f32[1,128,128]{2,1,0:T(8,128)S(1)}, u32[]{:S(2)}, u32[]{:S(2)}) collective-permute-start(f32[1,128,128]{2,1,0:T(8,128)S(1)} %coupled_inverse.1), channel_id=1, source_target_pairs={{0,64},{64,0},{128,192},{192,128},{256,320},{320,256},{384,448},{4... | collective-permute-start | bytes 196616 | tf_op jit(solution)/shard_map/ppermute | solution.py:184
  22.6 12.9 %collective-permute-start.1 = (f32[2,128,128]{2,1,0:T(8,128)S(1)}, f32[2,128,128]{2,1,0:T(8,128)S(1)}, u32[]{:S(2)}, u32[]{:S(2)}) collective-permute-start(f32[2,128,128]{2,1,0:T(8,128)S(1)} %pad_maximum_fusion.2), channel_id=1, source_target_pairs={{0,128},{64,192},{128,0},{192,64},{256,384},{320,448},{384,256},{4... | collective-permute-start | bytes 393224 | tf_op jit(solution)/shard_map/ppermute | solution.py:184
  29.5 18.3 %all-to-all-start.1 = ((f32[16,32,128]{2,1,0:T(8,128)}), f32[16,32,128]{2,1,0:T(8,128)S(1)}, u32[]{:S(2)}, u32[]{:S(2)}) async-start(f32[16,32,128]{2,1,0:T(8,128)} %reduce_sum.9), calls=%async_computation.1 | async-start | bytes 524288 | tf_op jit(solution)/shard_map/all_to_all | solution.py:162
  35.5 10.3 %collective-permute-start.2 = (f32[4,128,128]{2,1,0:T(8,128)S(1)}, f32[4,128,128]{2,1,0:T(8,128)S(1)}, u32[]{:S(2)}, u32[]{:S(2)}) collective-permute-start(f32[4,128,128]{2,1,0:T(8,128)S(1)} %pad_maximum_fusion.1), channel_id=1, source_target_pairs={{0,256},{64,320},{128,384},{192,448},{256,0},{320,64},{384,128},{4... | collective-permute-start | bytes 786440 | tf_op jit(solution)/shard_map/ppermute | solution.py:184
  63.1 20.6 %all-to-all-start.3 = ((f32[16,32,128]{2,1,0:T(8,128)}), f32[16,32,128]{2,1,0:T(8,128)S(1)}, u32[]{:S(2)}, u32[]{:S(2)}) async-start(f32[16,32,128]{2,1,0:T(8,128)} %get-tuple-element.18), calls=%async_computation.3 | async-start | bytes 524288 | tf_op jit(solution)/shard_map/all_to_all | solution.py:162
  79.8 18.8 %copy-start.3 = (s32[1,28,1]{1,2,0:T(1,128)S(1)}, s32[1,28,1]{1,2,0:T(1,128)}, u32[]{:S(2)}) copy-start(s32[1,28,1]{1,2,0:T(1,128)} %param.13) | copy-start | bytes 340

commit v7 on v6

--- a/solution.py
+++ b/solution.py
@@ -103,15 +103,17 @@
         copies_ref[copy] = x_sep
 
 
-def leaf_backward(owner_ref, x_ref, mapped_ref, out_hbm, out_ref, stored):
-    count = mapped_ref.shape[0]
+def leaf_backward(owner_ref, x_ref, early_ref, late_ref, out_hbm, out_ref, stored):
+    half = early_ref.shape[0]
+    count = half + late_ref.shape[0]
     rows = out_ref.shape[0]
     size = out_ref.shape[1] // count
     stores = []
     for f in range(count):
         owned = jnp.concatenate(split(x_ref[slot_of(owner_ref[f])]), axis=0)
-        picked = three_parts(dot(owned, mapped_ref[f, :size], NN), rows, size)
-        own = mapped_ref[f, size:].astype(jnp.float32)
+        mapped_ref, at = (early_ref, f) if f < half else (late_ref, f - half)
+        picked = three_parts(dot(owned, mapped_ref[at, :size], NN), rows, size)
+        own = mapped_ref[at, size:].astype(jnp.float32)
         out_ref[:, f * size : (f + 1) * size] = (own[:, :size] + own[:, size:]) - picked
         if (f + 1) % BACKWARD_CHUNK == 0:
             here = slice((f + 1 - BACKWARD_CHUNK) * size, (f + 1) * size)
@@ -225,21 +227,24 @@
         separator_inverse, separator_couple, leaf_y
     )
     coupled = gather_by_bits(coupled, "leaf")
-    matrices, lines, vectors, columns = specs(PREPARE_STEP)
-    mapped = call(
-        leaf_prepare,
-        [vectors, matrices, matrices, lines],
-        pl.BlockSpec((PREPARE_STEP, size + width, 2 * size), lambda s: (s, 0, 0)),
-        jax.ShapeDtypeStruct((front_count, size + width, 2 * size), jnp.bfloat16),
-        grid=(front_count // PREPARE_STEP,),
-    )(leaf_y, inverse, coupling, rows)
+    steps = front_count // PREPARE_STEP // 2
+
+    def prepare(start):
+        def some(*block):
+            return pl.BlockSpec((PREPARE_STEP, *block), lambda s: (s + start, 0, 0))
+
+        return call(
+            leaf_prepare,
+            [some(width, size), some(size, size), some(size, size), some(1, size)],
+            pl.BlockSpec((PREPARE_STEP, size + width, 2 * size), lambda s: (s, 0, 0)),
+            jax.ShapeDtypeStruct((steps * PREPARE_STEP, size + width, 2 * size), jnp.bfloat16),
+            grid=(steps,),
+        )(leaf_y, inverse, coupling, rows)
+
+    early, late = prepare(0), prepare(steps)
 
     right = call(reduce_right, [VMEM, VMEM, VMEM], VMEM, floats(groups, width, size))(
         received, rhs_sep[0], separator_inverse
-    )
-    group = lax.axis_index("leaf").reshape(1)
-    right, coupled, group, separator_inverse = lax.optimization_barrier(
-        (right, coupled, group, separator_inverse)
     )
     right = lax.all_to_all(right, "leaf", 0, 0, tiled=True)
     x_sep, copies = call(
@@ -248,20 +253,20 @@
         [VMEM, VMEM],
         [floats(width, size), floats(fronts // CLASSES, width, size)],
         scratch_shapes=[pltpu.VMEM((groups, width, size), jnp.float32)],
-    )(group, right, coupled, separator_inverse)
-    gathered, mapped = lax.optimization_barrier((exchange(copies, members), mapped))
+    )(lax.axis_index("leaf").reshape(1), right, coupled, separator_inverse)
+    gathered, early = lax.optimization_barrier((exchange(copies, members), early))
     gathered = jnp.broadcast_to(gathered[None], (CLASSES, *gathered.shape)).reshape(fronts, width, size)
     gathered = exchange(gathered, neighbours)
     x_leaf = call(
         leaf_backward,
-        [SMEM, VMEM, VMEM],
+        [SMEM, VMEM, VMEM, VMEM],
         ANY,
         floats(width, front_count * size),
         scratch_shapes=[
             pltpu.VMEM((width, front_count * size), jnp.float32),
             pltpu.SemaphoreType.DMA((front_count // BACKWARD_CHUNK,)),
         ],
-    )(update_owner.reshape(front_count), gathered, mapped)
+    )(update_owner.reshape(front_count), gathered, early, late)
     return (x_leaf[None], x_sep[None])
 
 

time: 101 us -> 98.4 us (0.974)
  blocking collectives: 27.3 us -> 0 us
  waiting for transfers between devices: 15.7 us -> 28.9 us
  starting transfers between devices: 37.8 us -> 44.6 us
  local copies, waits for them, and re-layouts: 0.14 us -> 2.14 us
  Pallas kernels: 17.8 us -> 19.7 us
    all_to_all x2 -> x0, blocking collectives: 27.3 us -> none  [the longest x1 14.8 us: exchange(): lax.all_to_all(value, ('leaf', 'front'), 0, 0, tiled=True, axis_index_gro...]
    all_to_all x3 -> x4, waiting for transfers between devices: 8.83 us -> 22.5 us  [exchange(): lax.all_to_all(value, ('leaf', 'front'), 0, 0, tiled=True, axis_index_gro...]
    all_to_all x0 -> x1, starting transfers between devices: none -> 7.4 us  [per_device(): right = lax.all_to_all(right, 'leaf', 0, 0, tiled=True)]
    ppermute x3, waiting for transfers between devices: 6.87 us -> 1.23 us  [gather_by_bits(): value = jnp.concatenate([value, lax.ppermute(value, axis, pairs)], axis=0)]
    all_to_all x0 -> x1, waiting for transfers between devices: none -> 5.23 us  [per_device(): right = lax.all_to_all(right, 'leaf', 0, 0, tiled=True)]
    pallas_call x2 -> x3, Pallas kernels: 10.1 us -> 11.3 us  [the longest x2 9.63 us: prepare(): call(leaf_prepare, [some(width, size), some(size, size), some(size, size)...]
    unnamed x8 -> x12, local copies, waits for them, and re-layouts: 0.02 us -> 1.03 us
    all_to_all x3 -> x4, starting transfers between devices: 28.1 us -> 27.5 us  [exchange(): lax.all_to_all(value, ('leaf', 'front'), 0, 0, tiled=True, axis_index_gro...]
  transfers between devices with their start and end apart: 6 -> 8, of which waited for: 5 -> 6; matrix products, arithmetic and copies ran while one was open for 1% -> 1% of each run, Pallas kernels for 9% -> 11%
where the time goes in v7:
time: 98.4 us; the launch traced here: 97 us
  starting transfers between devices  44.6 us (45%)
  waiting for transfers between devices  28.9 us (29%)
  Pallas kernels  19.7 us (20%)
  local copies, waits for them, and re-layouts  2.14 us (2%)
    all_to_all x4, starting transfers between devices, exchange(): lax.all_to_all(value, ('leaf', 'front'), 0, 0, tiled=True, axis_index_gro...  27.5 us
    all_to_all x4, waiting for transfers between devices, exchange(): lax.all_to_all(value, ('leaf', 'front'), 0, 0, tiled=True, axis_index_gro...  22.5 us
    ppermute x3, starting transfers between devices, gather_by_bits(): value = jnp.concatenate([value, lax.ppermute(value, axis, pairs)], axis=0)  9.69 us
    pallas_call x2, Pallas kernels, prepare(): call(leaf_prepare, [some(width, size), some(size, size), some(size, size)...  9.63 us
    all_to_all x1, starting transfers between devices, per_device(): right = lax.all_to_all(right, 'leaf', 0, 0, tiled=True)  7.4 us
    all_to_all x1, waiting for transfers between devices, per_device(): right = lax.all_to_all(right, 'leaf', 0, 0, tiled=True)  5.23 us
    pallas_call x1, Pallas kernels, per_device(): call(leaf_forward, [SMEM, columns, matrices, matrices, lines], [vectors,...  4.71 us
    pallas_call x1, Pallas kernels, per_device(): call(chain, [SMEM, VMEM, VMEM, VMEM], [VMEM, VMEM], [floats(width, size),...  2.69 us
  transfers between devices with their start and end apart: 8, of which 6 were waited for; matrix products, arithmetic and copies ran while one was open for 1% of the time, Pallas kernels for 11%

profile of v7, /device:TPU:1, one launch (start us, length us, event | category | flops | bytes accessed | tf_op | source)
XLA Modules:
  0.0 97.0 jit_solution(7926523821855846605)
XLA Ops:
  0.6 4.7 %leaf_forward.1 = (f32[28,32,128]{2,1,0:T(8,128)S(1)}, f32[64,32,128]{2,1,0:T(8,128)}) custom-call(s32[28]{0:T(128)} %bitcast.18, f32[32,3584]{1,0:T(8,128)} %bitcast.27, f32[28,128,128]{2,1,0:T(8,128)} %bitcast.20, f32[28,128,128]{2,1,0:T(8,128)} %bitcast.23, s32[28,1,128]{2,1,0:T(1,128)} %bitcast.29), custom_call_target="tpu_custom_call" | custom-call | tf_op jit(solution)/shard_map/leaf_forward/pallas_call | solution.py:216
  5.3 0.0 copy-start
  5.3 0.0 copy-start.2
  5.3 0.0 copy-start.3
  5.4 13.9 %all-to-all-start = ((f32[64,32,128]{2,1,0:T(8,128)}), f32[64,32,128]{2,1,0:T(8,128)S(1)}, u32[]{:S(2)}, u32[]{:S(2)}) async-start(f32[64,32,128]{2,1,0:T(8,128)} %get-tuple-element.8), calls=%async_computation | async-start | bytes 2097152 | tf_op jit(solution)/shard_map/all_to_all | solution.py:164
  19.3 0.0 copy-start.4
  19.3 0.0 copy-done.2
  19.3 0.0 copy-done.3
  19.3 0.2 coupled_inverse.1
  19.5 1.9 %collective-permute-start = (f32[1,128,128]{2,1,0:T(8,128)S(1)}, f32[1,128,128]{2,1,0:T(8,128)S(1)}, u32[]{:S(2)}, u32[]{:S(2)}) collective-permute-start(f32[1,128,128]{2,1,0:T(8,128)S(1)} %coupled_inverse.1), channel_id=1, source_target_pairs={{0,64},{64,0},{128,192},{192,128},{256,320},{320,256},{384,448},{4... | collective-permute-start | bytes 196616 | tf_op jit(solution)/shard_map/ppermute | solution.py:186
  21.4 1.2 %collective-permute-done = f32[1,128,128]{2,1,0:T(8,128)S(1)} collective-permute-done((f32[1,128,128]{2,1,0:T(8,128)S(1)}, f32[1,128,128]{2,1,0:T(8,128)S(1)}, u32[]{:S(2)}, u32[]{:S(2)}) %collective-permute-start) | collective-permute-done | bytes 65568 | tf_op jit(solution)/shard_map/ppermute | solution.py:186
  22.6 3.1 %collective-permute-start.1 = (f32[2,128,128]{2,1,0:T(8,128)S(1)}, f32[2,128,128]{2,1,0:T(8,128)S(1)}, u32[]{:S(2)}, u32[]{:S(2)}) collective-permute-start(f32[2,128,128]{2,1,0:T(8,128)S(1)} %pad_maximum_fusion.2), channel_id=1, source_target_pairs={{0,128},{64,192},{128,0},{192,64},{256,384},{320,448},{384,256},{4... | collective-permute-start | bytes 393224 | tf_op jit(solution)/shard_map/ppermute | solution.py:186
  25.7 3.0 %all-to-all-done = f32[64,32,128]{2,1,0:T(8,128)S(1)} async-done(((f32[64,32,128]{2,1,0:T(8,128)}), f32[64,32,128]{2,1,0:T(8,128)S(1)}, u32[]{:S(2)}, u32[]{:S(2)}) %all-to-all-start) | async-done | bytes 1048608 | tf_op jit(solution)/shard_map/all_to_all | solution.py:164
  28.8 0.8 reduce_sum.9
  29.5 5.9 %all-to-all-start.1 = ((f32[16,32,128]{2,1,0:T(8,128)}), f32[16,32,128]{2,1,0:T(8,128)S(1)}, u32[]{:S(2)}, u32[]{:S(2)}) async-start(f32[16,32,128]{2,1,0:T(8,128)} %reduce_sum.9), calls=%async_computation.1 | async-start | bytes 524288 | tf_op jit(solution)/shard_map/all_to_all | solution.py:164
  35.5 0.0 collective-permute-done.1
  35.5 4.7 %collective-permute-start.2 = (f32[4,128,128]{2,1,0:T(8,128)S(1)}, f32[4,128,128]{2,1,0:T(8,128)S(1)}, u32[]{:S(2)}, u32[]{:S(2)}) collective-permute-start(f32[4,128,128]{2,1,0:T(8,128)S(1)} %pad_maximum_fusion.1), channel_id=1, source_target_pairs={{0,256},{64,320},{128,384},{192,448},{256,0},{320,64},{384,128},{4... | collective-permute-start | bytes 786440 | tf_op jit(solution)/shard_map/ppermute | solution.py:186
  40.2 7.6 %all-to-all-done.1.received_ref = f32[16,32,128]{2,1,0:T(8,128)S(1)} async-done(((f32[16,32,128]{2,1,0:T(8,128)}), f32[16,32,128]{2,1,0:T(8,128)S(1)}, u32[]{:S(2)}, u32[]{:S(2)}) %all-to-all-start.1) | async-done | bytes 262176 | tf_op jit(solution)/shard_map/all_to_all | solution.py:164
  47.8 0.0 copy-done.4
  47.8 0.8 reduce_right.1
  48.7 7.4 %all-to-all-start.2 = ((f32[8,32,128]{2,1,0:T(8,128)}), f32[8,32,128]{2,1,0:T(8,128)S(1)}, u32[]{:S(2)}, u32[]{:S(2)}) async-start(f32[8,32,128]{2,1,0:T(8,128)} %reduce_right.1), calls=%async_computation.2 | async-start | bytes 262144 | tf_op jit(solution)/shard_map/all_to_all | solution.py:249
  56.1 0.0 collective-permute-done.2
  56.1 5.2 %all-to-all-done.2.right_ref = f32[8,32,128]{2,1,0:T(8,128)S(1)} async-done(((f32[8,32,128]{2,1,0:T(8,128)}), f32[8,32,128]{2,1,0:T(8,128)S(1)}, u32[]{:S(2)}, u32[]{:S(2)}) %all-to-all-start.2) | async-done | bytes 131104 | tf_op jit(solution)/shard_map/all_to_all | solution.py:249
  61.3 2.7 %chain.1 = (f32[32,128]{1,0:T(8,128)}, f32[16,32,128]{2,1,0:T(8,128)}) custom-call(s32[1]{0:T(128)} %bitcast.1.group_ref, f32[8,32,128]{2,1,0:T(8,128)S(1)} %all-to-all-done.2.right_ref, f32[8,128,128]{2,1,0:T(8,128)S(1)} %pad_maximum_fusion.coupled_ref, f32[128,128]{1,0:T(8,128)S(1)} %bitcast.15), custom_call_target="tpu_custom_call" | custom-call | tf_op jit(solution)/shard_map/chain/pallas_call | solution.py:250
  64.0 4.1 %all-to-all-start.3 = ((f32[16,32,128]{2,1,0:T(8,128)}), f32[16,32,128]{2,1,0:T(8,128)S(1)}, u32[]{:S(2)}, u32[]{:S(2)}) async-start(f32[16,32,128]{2,1,0:T(8,128)} %get-tuple-element.10), calls=%async_computation.3 | async-start | bytes 524288 | tf_op jit(solution)/shard_map/all_to_all | solution.py:164
  68.2 0.0 copy-done
  68.2 4.8 %leaf_prepare.2.early_ref = bf16[14,160,256]{2,1,0:T(8,128)(2,1)S(1)} custom-call(f32[28,32,128]{2,1,0:T(8,128)S(1)} %get-tuple-element.9.after_ref.y_ref, f32[28,128,128]{2,1,0:T(8,128)} %bitcast.21, f32[28,128,128]{2,1,0:T(8,128)} %bitcast.24, s32[28,1,128]{2,1,0:T(1,128)} %bitcast.30), custom_call_target="tpu_custom_call" | custom-call | tf_op jit(solution)/shard_map/leaf_prepare/pallas_call | solution.py:236
  73.0 8.1 %all-to-all-done.3 = f32[16,32,128]{2,1,0:T(8,128)S(1)} async-done(((f32[16,32,128]{2,1,0:T(8,128)}), f32[16,32,128]{2,1,0:T(8,128)S(1)}, u32[]{:S(2)}, u32[]{:S(2)}) %all-to-all-start.3) | async-done | bytes 262176 | tf_op jit(solution)/shard_map/all_to_all | solution.py:164
  81.2 1.1 %broadcast_in_dim.12 = f32[4,16,32,128]{3,2,1,0:T(8,128)} broadcast(f32[16,32,128]{2,1,0:T(8,128)S(1)} %all-to-all-done.3), dimensions={1,2,3} | broadcast | bytes 1310720 | tf_op jit(solution)/shard_map/broadcast_in_dim | solution.py:258
  82.3 3.5 %all-to-all-start.4 = ((f32[64,32,128]{2,1,0:T(8,128)}), f32[64,32,128]{2,1,0:T(8,128)S(1)}, u32[]{:S(2)}, u32[]{:S(2)}) async-start(f32[64,32,128]{2,1,0:T(8,128)} %bitcast.10), calls=%async_computation.4 | async-start | bytes 2097152 | tf_op jit(solution)/shard_map/all_to_all | solution.py:164
  85.8 0.0 copy-start.1
  85.8 1.0 %copy-done.1 = f32[28,32,128]{2,1,0:T(8,128)S(1)} copy-done((f32[28,32,128]{2,1,0:T(8,128)S(1)}, f32[28,32,128]{2,1,0:T(8,128)}, u32[]{:S(2)}) %copy-start.1) | copy-done | bytes 458776
  86.8 0.0 copy-start.5
  86.8 4.8 %leaf_prepare.3.late_ref = bf16[14,160,256]{2,1,0:T(8,128)(2,1)S(1)} custom-call(f32[28,32,128]{2,1,0:T(8,128)S(1)} %copy-done.1, f32[28,128,128]{2,1,0:T(8,128)} %bitcast.22, f32[28,128,128]{2,1,0:T(8,128)} %bitcast.25, s32[28,1,128]{2,1,0:T(1,128)} %bitcast.31), custom_call_target="tpu_custom_call" | custom-call | tf_op jit(solution)/shard_map/leaf_prepare/pallas_call | solution.py:236
  91.6 3.7 %all-to-all-done.4.x_ref = f32[64,32,128]{2,1,0:T(8,128)S(1)} async-done(((f32[64,32,128]{2,1,0:T(8,128)}), f32[64,32,128]{2,1,0:T(8,128)S(1)}, u32[]{:S(2)}, u32[]{:S(2)}) %all-to-all-start.4) | async-done | bytes 1048608 | tf_op jit(solution)/shard_map/all_to_all | solution.py:164
  95.3 0.0 copy-done.5
  95.3 1.6 %leaf_backward.1 = f32[32,3584]{1,0:T(8,128)} custom-call(s32[28]{0:T(128)S(1)} %bitcast.19, f32[64,32,128]{2,1,0:T(8,128)S(1)} %all-to-all-done.4.x_ref, bf16[14,160,256]{2,1,0:T(8,128)(2,1)S(1)} %leaf_prepare.2.early_ref, bf16[14,160,256]{2,1,0:T(8,128)(2,1)S(1)} %leaf_prepare.3.late_ref), custom_call_target="tpu_custom_call" | custom-call | tf_op jit(solution)/shard_map/leaf_backward/pallas_call | solution.py:260
  (3 shorter events, 0.1 us)
Async XLA Ops:
  5.3 62.8 %copy-start = (f32[28,32,128]{2,1,0:T(8,128)}, f32[28,32,128]{2,1,0:T(8,128)S(1)}, u32[]{:S(2)}) copy-start(f32[28,32,128]{2,1,0:T(8,128)S(1)} %get-tuple-element.9.after_ref.y_ref) | copy-start | bytes 1376260
  5.3 13.9 %copy-start.2 = (f32[1,1,128,128]{3,2,1,0:T(8,128)S(1)}, f32[1,1,128,128]{3,2,1,0:T(8,128)}, u32[]{:S(2)}) copy-start(f32[1,1,128,128]{3,2,1,0:T(8,128)} %param.14) | copy-start | bytes 196612
  5.3 13.9 %copy-start.3 = (f32[1,1,128,128]{3,2,1,0:T(8,128)S(1)}, f32[1,1,128,128]{3,2,1,0:T(8,128)}, u32[]{:S(2)}) copy-start(f32[1,1,128,128]{3,2,1,0:T(8,128)} %param.15) | copy-start | bytes 196612
  5.4 23.4 %all-to-all-start = ((f32[64,32,128]{2,1,0:T(8,128)}), f32[64,32,128]{2,1,0:T(8,128)S(1)}, u32[]{:S(2)}, u32[]{:S(2)}) async-start(f32[64,32,128]{2,1,0:T(8,128)} %get-tuple-element.8), calls=%async_computation | async-start | bytes 2097152 | tf_op jit(solution)/shard_map/all_to_all | solution.py:164
  19.3 28.6 %copy-start.4 = (f32[1,32,128]{2,1,0:T(8,128)S(1)}, f32[1,32,128]{2,1,0:T(8,128)}, u32[]{:S(2)}) copy-start(f32[1,32,128]{2,1,0:T(8,128)} %param.9) | copy-start | bytes 49156
  19.5 3.1 %collective-permute-start = (f32[1,128,128]{2,1,0:T(8,128)S(1)}, f32[1,128,128]{2,1,0:T(8,128)S(1)}, u32[]{:S(2)}, u32[]{:S(2)}) collective-permute-start(f32[1,128,128]{2,1,0:T(8,128)S(1)} %coupled_inverse.1), channel_id=1, source_target_pairs={{0,64},{64,0},{128,192},{192,128},{256,320},{320,256},{384,448},{4... | collective-permute-start | bytes 196616 | tf_op jit(solution)/shard_map/ppermute | solution.py:186
  22.6 12.9 %collective-permute-start.1 = (f32[2,128,128]{2,1,0:T(8,128)S(1)}, f32[2,128,128]{2,1,0:T(8,128)S(1)}, u32[]{:S(2)}, u32[]{:S(2)}) collective-permute-start(f32[2,128,128]{2,1,0:T(8,128)S(1)} %pad_maximum_fusion.2), channel_id=1, source_target_pairs={{0,128},{64,192},{128,0},{192,64},{256,384},{320,448},{384,256},{4... | collective-permute-start | bytes 393224 | tf_op jit(solution)/shard_map/ppermute | solution.py:186
  29.5 18.3 %all-to-all-start.1 = ((f32[16,32,128]{2,1,0:T(8,128)}), f32[16,32,128]{2,1,0:T(8,128)S(1)}, u32[]{:S(2)}, u32[]{:S(2)}) async-start(f32[16,32,128]{2,1,0:T(8,128)} %reduce_sum.9), calls=%async_computation.1 | async-start | bytes 524288 | tf_op jit(solution)/shard_map/all_to_all | solution.py:164
  35.5 20.5 %collective-permute-start.2 = (f32[4,128,128]{2,1,0:T(8,128)S(1)}, f32[4,128,128]{2,1,0:T(8,128)S(1)}, u32[]{:S(2)}, u32[]{:S(2)}) collective-permute-start(f32[4,128,128]{2,1,0:T(8,128)S(1)} %pad_maximum_fusion.1), channel_id=1, source_target_pairs={{0,256},{64,320},{128,384},{192,448},{256,0},{320,64},{384,128},{4... | collective-permute-start | bytes 786440 | tf_op jit(solution)/shard_map/ppermute | solution.py:186
  48.7 12.7 %all-to-all-start.2 = ((f32[8,32,128]{2,1,0:T(8,128)}), f32[8,32,128]{2,1,0:T(8,128)S(1)}, u32[]{:S(2)}, u32[]{:S(2)}) async-start(f32[8,32,128]{2,1,0:T(8,128)} %reduce_right.1), calls=%async_computation.2 | async-start | bytes 262144 | tf_op jit(solution)/shard_map/all_to_all | solution.py:249
  64.0 17.1 %all-to-all-start.3 = ((f32[16,32,128]{2,1,0:T(8,128)}), f32[16,32,128]{2,1,0:T(8,128)S(1)}, u32[]{:S(2)}, u32[]{:S(2)}) async-start(f32[16,32,128]{2,1,0:T(8,128)} %get-tuple-element.10), calls=%async_computation.3 | async-start | bytes 524288 | tf_op jit(solution)/shard_map/all_to_all | solution.py:164
  82.3 13.1 %all-to-all-start.4 = ((f32[64,32,128]{2,1,0:T(8,128)}), f32[64,32,128]{2,1,0:T(8,128)S(1)}, u32[]{:S(2)}, u32[]{:S(2)}) async-start(f32[64,32,128]{2,1,0:T(8,128)} %bitcast.10), calls=%async_computation.4 | async-start | bytes 2097152 | tf_op jit(solution)/shard_map/all_to_all | solution.py:164
  85.8 1.0 %copy-start.1 = (f32[28,32,128]{2,1,0:T(8,128)S(1)}, f32[28,32,128]{2,1,0:T(8,128)}, u32[]{:S(2)}) copy-start(f32[28,32,128]{2,1,0:T(8,128)} %copy-done) | copy-start | bytes 1376260
  86.8 8.5 %copy-start.5 = (s32[1,28,1]{1,2,0:T(1,128)S(1)}, s32[1,28,1]{1,2,0:T(1,128)}, u32[]{:S(2)}) copy-start(s32[1,28,1]{1,2,0:T(1,128)} %param.13) | copy-start | bytes 340

commit v8 on v6

--- a/solution.py
+++ b/solution.py
@@ -237,10 +237,6 @@
     right = call(reduce_right, [VMEM, VMEM, VMEM], VMEM, floats(groups, width, size))(
         received, rhs_sep[0], separator_inverse
     )
-    group = lax.axis_index("leaf").reshape(1)
-    right, coupled, group, separator_inverse = lax.optimization_barrier(
-        (right, coupled, group, separator_inverse)
-    )
     right = lax.all_to_all(right, "leaf", 0, 0, tiled=True)
     x_sep, copies = call(
         chain,
@@ -248,7 +244,7 @@
         [VMEM, VMEM],
         [floats(width, size), floats(fronts // CLASSES, width, size)],
         scratch_shapes=[pltpu.VMEM((groups, width, size), jnp.float32)],
-    )(group, right, coupled, separator_inverse)
+    )(lax.axis_index("leaf").reshape(1), right, coupled, separator_inverse)
     gathered, mapped = lax.optimization_barrier((exchange(copies, members), mapped))
     gathered = jnp.broadcast_to(gathered[None], (CLASSES, *gathered.shape)).reshape(fronts, width, size)
     gathered = exchange(gathered, neighbours)

time: 101 us -> 97.5 us (0.965)
  blocking collectives: 27.3 us -> 14 us
  waiting for transfers between devices: 15.7 us -> 21.6 us
  starting transfers between devices: 37.8 us -> 41.1 us
    all_to_all x1 -> x0, blocking collectives: 12.5 us -> none  [per_device(): right = lax.all_to_all(right, 'leaf', 0, 0, tiled=True)]
    all_to_all x0 -> x1, starting transfers between devices: none -> 7.4 us  [per_device(): right = lax.all_to_all(right, 'leaf', 0, 0, tiled=True)]
    all_to_all x3, waiting for transfers between devices: 8.83 us -> 15.2 us  [exchange(): lax.all_to_all(value, ('leaf', 'front'), 0, 0, tiled=True, axis_index_gro...]
    ppermute x3, waiting for transfers between devices: 6.87 us -> 1.23 us  [gather_by_bits(): value = jnp.concatenate([value, lax.ppermute(value, axis, pairs)], axis=0)]
    all_to_all x0 -> x1, waiting for transfers between devices: none -> 5.23 us  [per_device(): right = lax.all_to_all(right, 'leaf', 0, 0, tiled=True)]
    all_to_all x3, starting transfers between devices: 28.1 us -> 24 us  [exchange(): lax.all_to_all(value, ('leaf', 'front'), 0, 0, tiled=True, axis_index_gro...]
  transfers between devices with their start and end apart: 6 -> 7, of which waited for: 5 -> 5; matrix products, arithmetic and copies ran while one was open for 1% -> 1% of each run, Pallas kernels for 9% -> 10%
where the time goes in v8:
time: 97.5 us; the launch traced here: 96.8 us
  starting transfers between devices  41.1 us (42%)
  waiting for transfers between devices  21.6 us (22%)
  Pallas kernels  18.5 us (19%)
  blocking collectives  14 us (14%)
    all_to_all x3, starting transfers between devices, exchange(): lax.all_to_all(value, ('leaf', 'front'), 0, 0, tiled=True, axis_index_gro...  24 us
    all_to_all x3, waiting for transfers between devices, exchange(): lax.all_to_all(value, ('leaf', 'front'), 0, 0, tiled=True, axis_index_gro...  15.2 us
    all_to_all x1, blocking collectives, exchange(): lax.all_to_all(value, ('leaf', 'front'), 0, 0, tiled=True, axis_index_gro...  14 us
    ppermute x3, starting transfers between devices, gather_by_bits(): value = jnp.concatenate([value, lax.ppermute(value, axis, pairs)], axis=0)  9.69 us
    pallas_call x1, Pallas kernels, per_device(): call(leaf_prepare, [vectors, matrices, matrices, lines], pl.BlockSpec((PR...  8.45 us
    all_to_all x1, starting transfers between devices, per_device(): right = lax.all_to_all(right, 'leaf', 0, 0, tiled=True)  7.4 us
    all_to_all x1, waiting for transfers between devices, per_device(): right = lax.all_to_all(right, 'leaf', 0, 0, tiled=True)  5.23 us
    pallas_call x1, Pallas kernels, per_device(): call(leaf_forward, [SMEM, columns, matrices, matrices, lines], [vectors,...  4.71 us
  transfers between devices with their start and end apart: 7, of which 5 were waited for; matrix products, arithmetic and copies ran while one was open for 1% of the time, Pallas kernels for 10%

profile of v8, /device:TPU:1, one launch (start us, length us, event | category | flops | bytes accessed | tf_op | source)
XLA Modules:
  0.0 96.8 jit_solution(16878086613951877849)
XLA Ops:
  0.6 4.7 %leaf_forward.1 = (f32[28,32,128]{2,1,0:T(8,128)S(1)}, f32[64,32,128]{2,1,0:T(8,128)}) custom-call(s32[28]{0:T(128)} %bitcast.18, f32[32,3584]{1,0:T(8,128)} %bitcast.26, f32[28,128,128]{2,1,0:T(8,128)} %bitcast.20, f32[28,128,128]{2,1,0:T(8,128)} %bitcast.22, s32[28,1,128]{2,1,0:T(1,128)} %bitcast.28), custom_call_target="tpu_custom_call" | custom-call | tf_op jit(solution)/shard_map/leaf_forward/pallas_call | solution.py:214
  5.3 0.0 copy-start
  5.3 0.0 copy-start.1
  5.3 13.9 %all-to-all-start = ((f32[64,32,128]{2,1,0:T(8,128)}), f32[64,32,128]{2,1,0:T(8,128)S(1)}, u32[]{:S(2)}, u32[]{:S(2)}) async-start(f32[64,32,128]{2,1,0:T(8,128)} %get-tuple-element.8), calls=%async_computation | async-start | bytes 2097152 | tf_op jit(solution)/shard_map/all_to_all | solution.py:162
  19.3 0.0 copy-start.2
  19.3 0.0 copy-done
  19.3 0.0 copy-done.1
  19.3 0.2 coupled_inverse.1
  19.4 1.9 %collective-permute-start = (f32[1,128,128]{2,1,0:T(8,128)S(1)}, f32[1,128,128]{2,1,0:T(8,128)S(1)}, u32[]{:S(2)}, u32[]{:S(2)}) collective-permute-start(f32[1,128,128]{2,1,0:T(8,128)S(1)} %coupled_inverse.1), channel_id=1, source_target_pairs={{0,64},{64,0},{128,192},{192,128},{256,320},{320,256},{384,448},{4... | collective-permute-start | bytes 196616 | tf_op jit(solution)/shard_map/ppermute | solution.py:184
  21.4 1.2 %collective-permute-done = f32[1,128,128]{2,1,0:T(8,128)S(1)} collective-permute-done((f32[1,128,128]{2,1,0:T(8,128)S(1)}, f32[1,128,128]{2,1,0:T(8,128)S(1)}, u32[]{:S(2)}, u32[]{:S(2)}) %collective-permute-start) | collective-permute-done | bytes 65568 | tf_op jit(solution)/shard_map/ppermute | solution.py:184
  22.6 3.1 %collective-permute-start.1 = (f32[2,128,128]{2,1,0:T(8,128)S(1)}, f32[2,128,128]{2,1,0:T(8,128)S(1)}, u32[]{:S(2)}, u32[]{:S(2)}) collective-permute-start(f32[2,128,128]{2,1,0:T(8,128)S(1)} %pad_maximum_fusion.2), channel_id=1, source_target_pairs={{0,128},{64,192},{128,0},{192,64},{256,384},{320,448},{384,256},{4... | collective-permute-start | bytes 393224 | tf_op jit(solution)/shard_map/ppermute | solution.py:184
  25.7 3.0 %all-to-all-done = f32[64,32,128]{2,1,0:T(8,128)S(1)} async-done(((f32[64,32,128]{2,1,0:T(8,128)}), f32[64,32,128]{2,1,0:T(8,128)S(1)}, u32[]{:S(2)}, u32[]{:S(2)}) %all-to-all-start) | async-done | bytes 1048608 | tf_op jit(solution)/shard_map/all_to_all | solution.py:162
  28.7 0.8 reduce_sum.9
  29.5 5.9 %all-to-all-start.1 = ((f32[16,32,128]{2,1,0:T(8,128)}), f32[16,32,128]{2,1,0:T(8,128)S(1)}, u32[]{:S(2)}, u32[]{:S(2)}) async-start(f32[16,32,128]{2,1,0:T(8,128)} %reduce_sum.9), calls=%async_computation.1 | async-start | bytes 524288 | tf_op jit(solution)/shard_map/all_to_all | solution.py:162
  35.5 0.0 collective-permute-done.1
  35.5 4.7 %collective-permute-start.2 = (f32[4,128,128]{2,1,0:T(8,128)S(1)}, f32[4,128,128]{2,1,0:T(8,128)S(1)}, u32[]{:S(2)}, u32[]{:S(2)}) collective-permute-start(f32[4,128,128]{2,1,0:T(8,128)S(1)} %pad_maximum_fusion.1), channel_id=1, source_target_pairs={{0,256},{64,320},{128,384},{192,448},{256,0},{320,64},{384,128},{4... | collective-permute-start | bytes 786440 | tf_op jit(solution)/shard_map/ppermute | solution.py:184
  40.2 7.6 %all-to-all-done.1.received_ref = f32[16,32,128]{2,1,0:T(8,128)S(1)} async-done(((f32[16,32,128]{2,1,0:T(8,128)}), f32[16,32,128]{2,1,0:T(8,128)S(1)}, u32[]{:S(2)}, u32[]{:S(2)}) %all-to-all-start.1) | async-done | bytes 262176 | tf_op jit(solution)/shard_map/all_to_all | solution.py:162
  47.8 0.0 copy-done.2
  47.8 0.8 reduce_right.1
  48.6 7.4 %all-to-all-start.2 = ((f32[8,32,128]{2,1,0:T(8,128)}), f32[8,32,128]{2,1,0:T(8,128)S(1)}, u32[]{:S(2)}, u32[]{:S(2)}) async-start(f32[8,32,128]{2,1,0:T(8,128)} %reduce_right.1), calls=%async_computation.2 | async-start | bytes 262144 | tf_op jit(solution)/shard_map/all_to_all | solution.py:240
  56.0 0.0 collective-permute-done.2
  56.1 5.2 %all-to-all-done.2.right_ref = f32[8,32,128]{2,1,0:T(8,128)S(1)} async-done(((f32[8,32,128]{2,1,0:T(8,128)}), f32[8,32,128]{2,1,0:T(8,128)S(1)}, u32[]{:S(2)}, u32[]{:S(2)}) %all-to-all-start.2) | async-done | bytes 131104 | tf_op jit(solution)/shard_map/all_to_all | solution.py:240
  61.3 2.7 %chain.1 = (f32[32,128]{1,0:T(8,128)}, f32[16,32,128]{2,1,0:T(8,128)}) custom-call(s32[1]{0:T(128)} %bitcast.1.group_ref, f32[8,32,128]{2,1,0:T(8,128)S(1)} %all-to-all-done.2.right_ref, f32[8,128,128]{2,1,0:T(8,128)S(1)} %pad_maximum_fusion.coupled_ref, f32[128,128]{1,0:T(8,128)S(1)} %bitcast.15), custom_call_target="tpu_custom_call" | custom-call | tf_op jit(solution)/shard_map/chain/pallas_call | solution.py:241
  64.0 4.1 %all-to-all-start.3 = ((f32[16,32,128]{2,1,0:T(8,128)}), f32[16,32,128]{2,1,0:T(8,128)S(1)}, u32[]{:S(2)}, u32[]{:S(2)}) async-start(f32[16,32,128]{2,1,0:T(8,128)} %get-tuple-element.10), calls=%async_computation.3 | async-start | bytes 524288 | tf_op jit(solution)/shard_map/all_to_all | solution.py:162
  68.1 8.5 %leaf_prepare.1.mapped_ref = bf16[28,160,256]{2,1,0:T(8,128)(2,1)S(1)} custom-call(f32[28,32,128]{2,1,0:T(8,128)S(1)} %get-tuple-element.9.after_ref.y_ref, f32[28,128,128]{2,1,0:T(8,128)} %bitcast.21, f32[28,128,128]{2,1,0:T(8,128)} %bitcast.23, s32[28,1,128]{2,1,0:T(1,128)} %bitcast.29), custom_call_target="tpu_custom_call" | custom-call | tf_op jit(solution)/shard_map/leaf_prepare/pallas_call | solution.py:229
  76.6 0.0 copy-start.3
  76.6 4.5 %all-to-all-done.3 = f32[16,32,128]{2,1,0:T(8,128)S(1)} async-done(((f32[16,32,128]{2,1,0:T(8,128)}), f32[16,32,128]{2,1,0:T(8,128)S(1)}, u32[]{:S(2)}, u32[]{:S(2)}) %all-to-all-start.3) | async-done | bytes 262176 | tf_op jit(solution)/shard_map/all_to_all | solution.py:162
  81.1 0.1 broadcast_in_dim.12
  81.2 14.0 %all_to_all.25.x_ref = f32[64,32,128]{2,1,0:T(8,128)S(1)} all-to-all(f32[64,32,128]{2,1,0:T(8,128)S(1)} %bitcast.24), channel_id=1, replica_groups={{0,1,8,9},{2,3,10,11},{4,5,12,13},{6,7,14,15},{16,17,24,25},{18,19,26,2..., dimensions={0} | all-to-all | bytes 2097152 | tf_op jit(solution)/shard_map/all_to_all | solution.py:162
  95.2 0.0 copy-done.3
  95.2 1.6 %leaf_backward.1 = f32[32,3584]{1,0:T(8,128)} custom-call(s32[28]{0:T(128)S(1)} %bitcast.19, f32[64,32,128]{2,1,0:T(8,128)S(1)} %all_to_all.25.x_ref, bf16[28,160,256]{2,1,0:T(8,128)(2,1)S(1)} %leaf_prepare.1.mapped_ref), custom_call_target="tpu_custom_call" | custom-call | tf_op jit(solution)/shard_map/leaf_backward/pallas_call | solution.py:251
  (3 shorter events, 0.1 us)
Async XLA Ops:
  5.3 13.9 %copy-start = (f32[1,1,128,128]{3,2,1,0:T(8,128)S(1)}, f32[1,1,128,128]{3,2,1,0:T(8,128)}, u32[]{:S(2)}) copy-start(f32[1,1,128,128]{3,2,1,0:T(8,128)} %param.14) | copy-start | bytes 196612
  5.3 13.9 %copy-start.1 = (f32[1,1,128,128]{3,2,1,0:T(8,128)S(1)}, f32[1,1,128,128]{3,2,1,0:T(8,128)}, u32[]{:S(2)}) copy-start(f32[1,1,128,128]{3,2,1,0:T(8,128)} %param.15) | copy-start | bytes 196612
  5.3 23.4 %all-to-all-start = ((f32[64,32,128]{2,1,0:T(8,128)}), f32[64,32,128]{2,1,0:T(8,128)S(1)}, u32[]{:S(2)}, u32[]{:S(2)}) async-start(f32[64,32,128]{2,1,0:T(8,128)} %get-tuple-element.8), calls=%async_computation | async-start | bytes 2097152 | tf_op jit(solution)/shard_map/all_to_all | solution.py:162
  19.3 28.6 %copy-start.2 = (f32[1,32,128]{2,1,0:T(8,128)S(1)}, f32[1,32,128]{2,1,0:T(8,128)}, u32[]{:S(2)}) copy-start(f32[1,32,128]{2,1,0:T(8,128)} %param.9) | copy-start | bytes 49156
  19.4 3.1 %collective-permute-start = (f32[1,128,128]{2,1,0:T(8,128)S(1)}, f32[1,128,128]{2,1,0:T(8,128)S(1)}, u32[]{:S(2)}, u32[]{:S(2)}) collective-permute-start(f32[1,128,128]{2,1,0:T(8,128)S(1)} %coupled_inverse.1), channel_id=1, source_target_pairs={{0,64},{64,0},{128,192},{192,128},{256,320},{320,256},{384,448},{4... | collective-permute-start | bytes 196616 | tf_op jit(solution)/shard_map/ppermute | solution.py:184
  22.6 12.9 %collective-permute-start.1 = (f32[2,128,128]{2,1,0:T(8,128)S(1)}, f32[2,128,128]{2,1,0:T(8,128)S(1)}, u32[]{:S(2)}, u32[]{:S(2)}) collective-permute-start(f32[2,128,128]{2,1,0:T(8,128)S(1)} %pad_maximum_fusion.2), channel_id=1, source_target_pairs={{0,128},{64,192},{128,0},{192,64},{256,384},{320,448},{384,256},{4... | collective-permute-start | bytes 393224 | tf_op jit(solution)/shard_map/ppermute | solution.py:184
  29.5 18.3 %all-to-all-start.1 = ((f32[16,32,128]{2,1,0:T(8,128)}), f32[16,32,128]{2,1,0:T(8,128)S(1)}, u32[]{:S(2)}, u32[]{:S(2)}) async-start(f32[16,32,128]{2,1,0:T(8,128)} %reduce_sum.9), calls=%async_computation.1 | async-start | bytes 524288 | tf_op jit(solution)/shard_map/all_to_all | solution.py:162
  35.5 20.5 %collective-permute-start.2 = (f32[4,128,128]{2,1,0:T(8,128)S(1)}, f32[4,128,128]{2,1,0:T(8,128)S(1)}, u32[]{:S(2)}, u32[]{:S(2)}) collective-permute-start(f32[4,128,128]{2,1,0:T(8,128)S(1)} %pad_maximum_fusion.1), channel_id=1, source_target_pairs={{0,256},{64,320},{128,384},{192,448},{256,0},{320,64},{384,128},{4... | collective-permute-start | bytes 786440 | tf_op jit(solution)/shard_map/ppermute | solution.py:184
  48.6 12.7 %all-to-all-start.2 = ((f32[8,32,128]{2,1,0:T(8,128)}), f32[8,32,128]{2,1,0:T(8,128)S(1)}, u32[]{:S(2)}, u32[]{:S(2)}) async-start(f32[8,32,128]{2,1,0:T(8,128)} %reduce_right.1), calls=%async_computation.2 | async-start | bytes 262144 | tf_op jit(solution)/shard_map/all_to_all | solution.py:240
  64.0 17.1 %all-to-all-start.3 = ((f32[16,32,128]{2,1,0:T(8,128)}), f32[16,32,128]{2,1,0:T(8,128)S(1)}, u32[]{:S(2)}, u32[]{:S(2)}) async-start(f32[16,32,128]{2,1,0:T(8,128)} %get-tuple-element.10), calls=%async_computation.3 | async-start | bytes 524288 | tf_op jit(solution)/shard_map/all_to_all | solution.py:162
  76.6 18.6 %copy-start.3 = (s32[1,28,1]{1,2,0:T(1,128)S(1)}, s32[1,28,1]{1,2,0:T(1,128)}, u32[]{:S(2)}) copy-start(s32[1,28,1]{1,2,0:T(1,128)} %param.13) | copy-start | bytes 340

commit v9 on v8

--- a/solution.py
+++ b/solution.py
@@ -69,12 +69,15 @@
 
 def leaf_prepare(y_ref, inv_ref, update_ref, rows_ref, mapped_ref):
     count, size, _ = inv_ref.shape
-    for f in range(count):
-        inverse = inv_ref[f]
-        mapped_ref[f, size:] = jnp.concatenate(split(product(y_ref[f], inverse, NN)), axis=1)
-        mapped = jnp.concatenate(split(product(update_ref[f], inverse, NN)), axis=1)
-        placed = dot(chosen_rows(rows_ref[f], size), mapped, NN)
-        mapped_ref[f, :size] = jnp.concatenate(split(placed[:, :size] + placed[:, size:]), axis=1)
+    fronts = range(count)
+    both = [product(jnp.concatenate([update_ref[f], y_ref[f]], axis=0), inv_ref[f], NN) for f in fronts]
+    mapped = [jnp.concatenate(split(both[f][:size]), axis=1) for f in fronts]
+    for f in fronts:
+        mapped_ref[f, size:] = jnp.concatenate(split(both[f][size:]), axis=1)
+    placed = [dot(chosen_rows(rows_ref[f], size), mapped[f], NN) for f in fronts]
+    for f in fronts:
+        whole = placed[f][:, :size] + placed[f][:, size:]
+        mapped_ref[f, :size] = jnp.concatenate(split(whole), axis=1)
 
 
 def reduce_right(received_ref, rhs_ref, inv_ref, out_ref):
@@ -129,7 +132,7 @@
 CLASSES = 4
 BACKWARD_CHUNK = 7
 FORWARD_STEP = 14
-PREPARE_STEP = 7
+PREPARE_STEP = 14
 VMEM = pl.BlockSpec(memory_space=pltpu.VMEM)
 SMEM = pl.BlockSpec(memory_space=pltpu.SMEM)
 ANY = pl.BlockSpec(memory_space=pl.ANY)

time: 97.5 us -> 97.5 us (level)
  Pallas kernels: 18.5 us -> 13.6 us
  waiting for transfers between devices: 21.6 us -> 26.5 us
    all_to_all x3, waiting for transfers between devices: 15.2 us -> 20.1 us  [exchange(): lax.all_to_all(value, ('leaf', 'front'), 0, 0, tiled=True, axis_index_gro...]
    pallas_call x1, Pallas kernels: 8.45 us -> 3.53 us  [per_device(): call(leaf_prepare, [vectors, matrices, matrices, lines], pl.BlockSpec((PR...]
  transfers between devices with their start and end apart: 7 -> 7, of which waited for: 5 -> 5; matrix products, arithmetic and copies ran while one was open for 1% -> 1% of each run, Pallas kernels for 10% -> 5%
where the time goes in v9:
time: 97.5 us; the launch traced here: 96.8 us
  starting transfers between devices  41.1 us (42%)
  waiting for transfers between devices  26.5 us (27%)
  blocking collectives  14 us (14%)
  Pallas kernels  13.6 us (14%)
    all_to_all x3, starting transfers between devices, exchange(): lax.all_to_all(value, ('leaf', 'front'), 0, 0, tiled=True, axis_index_gro...  24 us
    all_to_all x3, waiting for transfers between devices, exchange(): lax.all_to_all(value, ('leaf', 'front'), 0, 0, tiled=True, axis_index_gro...  20.1 us
    all_to_all x1, blocking collectives, exchange(): lax.all_to_all(value, ('leaf', 'front'), 0, 0, tiled=True, axis_index_gro...  14 us
    ppermute x3, starting transfers between devices, gather_by_bits(): value = jnp.concatenate([value, lax.ppermute(value, axis, pairs)], axis=0)  9.69 us
    all_to_all x1, starting transfers between devices, per_device(): right = lax.all_to_all(right, 'leaf', 0, 0, tiled=True)  7.4 us
    all_to_all x1, waiting for transfers between devices, per_device(): right = lax.all_to_all(right, 'leaf', 0, 0, tiled=True)  5.23 us
    pallas_call x1, Pallas kernels, per_device(): call(leaf_forward, [SMEM, columns, matrices, matrices, lines], [vectors,...  4.71 us
    pallas_call x1, Pallas kernels, per_device(): call(leaf_prepare, [vectors, matrices, matrices, lines], pl.BlockSpec((PR...  3.53 us
  transfers between devices with their start and end apart: 7, of which 5 were waited for; matrix products, arithmetic and copies ran while one was open for 1% of the time, Pallas kernels for 5%

profile of v9, /device:TPU:1, one launch (start us, length us, event | category | flops | bytes accessed | tf_op | source)
XLA Modules:
  0.0 96.8 jit_solution(5204312883663857696)
XLA Ops:
  0.6 4.7 %leaf_forward.1 = (f32[28,32,128]{2,1,0:T(8,128)S(1)}, f32[64,32,128]{2,1,0:T(8,128)}) custom-call(s32[28]{0:T(128)} %bitcast.18, f32[32,3584]{1,0:T(8,128)} %bitcast.26, f32[28,128,128]{2,1,0:T(8,128)} %bitcast.20, f32[28,128,128]{2,1,0:T(8,128)} %bitcast.22, s32[28,1,128]{2,1,0:T(1,128)} %bitcast.28), custom_call_target="tpu_custom_call" | custom-call | tf_op jit(solution)/shard_map/leaf_forward/pallas_call | solution.py:217
  5.3 0.0 copy-start
  5.3 0.0 copy-start.1
  5.3 13.9 %all-to-all-start = ((f32[64,32,128]{2,1,0:T(8,128)}), f32[64,32,128]{2,1,0:T(8,128)S(1)}, u32[]{:S(2)}, u32[]{:S(2)}) async-start(f32[64,32,128]{2,1,0:T(8,128)} %get-tuple-element.8), calls=%async_computation | async-start | bytes 2097152 | tf_op jit(solution)/shard_map/all_to_all | solution.py:165
  19.3 0.0 copy-start.2
  19.3 0.0 copy-done
  19.3 0.0 copy-done.1
  19.3 0.2 coupled_inverse.1
  19.4 1.9 %collective-permute-start = (f32[1,128,128]{2,1,0:T(8,128)S(1)}, f32[1,128,128]{2,1,0:T(8,128)S(1)}, u32[]{:S(2)}, u32[]{:S(2)}) collective-permute-start(f32[1,128,128]{2,1,0:T(8,128)S(1)} %coupled_inverse.1), channel_id=1, source_target_pairs={{0,64},{64,0},{128,192},{192,128},{256,320},{320,256},{384,448},{4... | collective-permute-start | bytes 196616 | tf_op jit(solution)/shard_map/ppermute | solution.py:187
  21.4 1.2 %collective-permute-done = f32[1,128,128]{2,1,0:T(8,128)S(1)} collective-permute-done((f32[1,128,128]{2,1,0:T(8,128)S(1)}, f32[1,128,128]{2,1,0:T(8,128)S(1)}, u32[]{:S(2)}, u32[]{:S(2)}) %collective-permute-start) | collective-permute-done | bytes 65568 | tf_op jit(solution)/shard_map/ppermute | solution.py:187
  22.6 3.1 %collective-permute-start.1 = (f32[2,128,128]{2,1,0:T(8,128)S(1)}, f32[2,128,128]{2,1,0:T(8,128)S(1)}, u32[]{:S(2)}, u32[]{:S(2)}) collective-permute-start(f32[2,128,128]{2,1,0:T(8,128)S(1)} %pad_maximum_fusion.2), channel_id=1, source_target_pairs={{0,128},{64,192},{128,0},{192,64},{256,384},{320,448},{384,256},{4... | collective-permute-start | bytes 393224 | tf_op jit(solution)/shard_map/ppermute | solution.py:187
  25.7 3.0 %all-to-all-done = f32[64,32,128]{2,1,0:T(8,128)S(1)} async-done(((f32[64,32,128]{2,1,0:T(8,128)}), f32[64,32,128]{2,1,0:T(8,128)S(1)}, u32[]{:S(2)}, u32[]{:S(2)}) %all-to-all-start) | async-done | bytes 1048608 | tf_op jit(solution)/shard_map/all_to_all | solution.py:165
  28.7 0.8 reduce_sum.9
  29.5 5.9 %all-to-all-start.1 = ((f32[16,32,128]{2,1,0:T(8,128)}), f32[16,32,128]{2,1,0:T(8,128)S(1)}, u32[]{:S(2)}, u32[]{:S(2)}) async-start(f32[16,32,128]{2,1,0:T(8,128)} %reduce_sum.9), calls=%async_computation.1 | async-start | bytes 524288 | tf_op jit(solution)/shard_map/all_to_all | solution.py:165
  35.5 0.0 collective-permute-done.1
  35.5 4.7 %collective-permute-start.2 = (f32[4,128,128]{2,1,0:T(8,128)S(1)}, f32[4,128,128]{2,1,0:T(8,128)S(1)}, u32[]{:S(2)}, u32[]{:S(2)}) collective-permute-start(f32[4,128,128]{2,1,0:T(8,128)S(1)} %pad_maximum_fusion.1), channel_id=1, source_target_pairs={{0,256},{64,320},{128,384},{192,448},{256,0},{320,64},{384,128},{4... | collective-permute-start | bytes 786440 | tf_op jit(solution)/shard_map/ppermute | solution.py:187
  40.2 7.6 %all-to-all-done.1.received_ref = f32[16,32,128]{2,1,0:T(8,128)S(1)} async-done(((f32[16,32,128]{2,1,0:T(8,128)}), f32[16,32,128]{2,1,0:T(8,128)S(1)}, u32[]{:S(2)}, u32[]{:S(2)}) %all-to-all-start.1) | async-done | bytes 262176 | tf_op jit(solution)/shard_map/all_to_all | solution.py:165
  47.8 0.0 copy-done.2
  47.8 0.8 reduce_right.1
  48.6 7.4 %all-to-all-start.2 = ((f32[8,32,128]{2,1,0:T(8,128)}), f32[8,32,128]{2,1,0:T(8,128)S(1)}, u32[]{:S(2)}, u32[]{:S(2)}) async-start(f32[8,32,128]{2,1,0:T(8,128)} %reduce_right.1), calls=%async_computation.2 | async-start | bytes 262144 | tf_op jit(solution)/shard_map/all_to_all | solution.py:243
  56.0 0.0 collective-permute-done.2
  56.1 5.2 %all-to-all-done.2.right_ref = f32[8,32,128]{2,1,0:T(8,128)S(1)} async-done(((f32[8,32,128]{2,1,0:T(8,128)}), f32[8,32,128]{2,1,0:T(8,128)S(1)}, u32[]{:S(2)}, u32[]{:S(2)}) %all-to-all-start.2) | async-done | bytes 131104 | tf_op jit(solution)/shard_map/all_to_all | solution.py:243
  61.3 2.7 %chain.1 = (f32[32,128]{1,0:T(8,128)}, f32[16,32,128]{2,1,0:T(8,128)}) custom-call(s32[1]{0:T(128)} %bitcast.1.group_ref, f32[8,32,128]{2,1,0:T(8,128)S(1)} %all-to-all-done.2.right_ref, f32[8,128,128]{2,1,0:T(8,128)S(1)} %pad_maximum_fusion.coupled_ref, f32[128,128]{1,0:T(8,128)S(1)} %bitcast.15), custom_call_target="tpu_custom_call" | custom-call | tf_op jit(solution)/shard_map/chain/pallas_call | solution.py:244
  64.0 4.1 %all-to-all-start.3 = ((f32[16,32,128]{2,1,0:T(8,128)}), f32[16,32,128]{2,1,0:T(8,128)S(1)}, u32[]{:S(2)}, u32[]{:S(2)}) async-start(f32[16,32,128]{2,1,0:T(8,128)} %get-tuple-element.10), calls=%async_computation.3 | async-start | bytes 524288 | tf_op jit(solution)/shard_map/all_to_all | solution.py:165
  68.1 3.5 %leaf_prepare.1.mapped_ref = bf16[28,160,256]{2,1,0:T(8,128)(2,1)S(1)} custom-call(f32[28,32,128]{2,1,0:T(8,128)S(1)} %get-tuple-element.9.after_ref.y_ref, f32[28,128,128]{2,1,0:T(8,128)} %bitcast.21, f32[28,128,128]{2,1,0:T(8,128)} %bitcast.23, s32[28,1,128]{2,1,0:T(1,128)} %bitcast.29), custom_call_target="tpu_custom_call" | custom-call | tf_op jit(solution)/shard_map/leaf_prepare/pallas_call | solution.py:232
  71.7 0.0 copy-start.3
  71.7 9.4 %all-to-all-done.3 = f32[16,32,128]{2,1,0:T(8,128)S(1)} async-done(((f32[16,32,128]{2,1,0:T(8,128)}), f32[16,32,128]{2,1,0:T(8,128)S(1)}, u32[]{:S(2)}, u32[]{:S(2)}) %all-to-all-start.3) | async-done | bytes 262176 | tf_op jit(solution)/shard_map/all_to_all | solution.py:165
  81.1 0.1 broadcast_in_dim.12
  81.2 14.0 %all_to_all.25.x_ref = f32[64,32,128]{2,1,0:T(8,128)S(1)} all-to-all(f32[64,32,128]{2,1,0:T(8,128)S(1)} %bitcast.24), channel_id=1, replica_groups={{0,1,8,9},{2,3,10,11},{4,5,12,13},{6,7,14,15},{16,17,24,25},{18,19,26,2..., dimensions={0} | all-to-all | bytes 2097152 | tf_op jit(solution)/shard_map/all_to_all | solution.py:165
  95.2 0.0 copy-done.3
  95.2 1.6 %leaf_backward.1 = f32[32,3584]{1,0:T(8,128)} custom-call(s32[28]{0:T(128)S(1)} %bitcast.19, f32[64,32,128]{2,1,0:T(8,128)S(1)} %all_to_all.25.x_ref, bf16[28,160,256]{2,1,0:T(8,128)(2,1)S(1)} %leaf_prepare.1.mapped_ref), custom_call_target="tpu_custom_call" | custom-call | tf_op jit(solution)/shard_map/leaf_backward/pallas_call | solution.py:254
  (3 shorter events, 0.1 us)
Async XLA Ops:
  5.3 13.9 %copy-start = (f32[1,1,128,128]{3,2,1,0:T(8,128)S(1)}, f32[1,1,128,128]{3,2,1,0:T(8,128)}, u32[]{:S(2)}) copy-start(f32[1,1,128,128]{3,2,1,0:T(8,128)} %param.14) | copy-start | bytes 196612
  5.3 13.9 %copy-start.1 = (f32[1,1,128,128]{3,2,1,0:T(8,128)S(1)}, f32[1,1,128,128]{3,2,1,0:T(8,128)}, u32[]{:S(2)}) copy-start(f32[1,1,128,128]{3,2,1,0:T(8,128)} %param.15) | copy-start | bytes 196612
  5.3 23.4 %all-to-all-start = ((f32[64,32,128]{2,1,0:T(8,128)}), f32[64,32,128]{2,1,0:T(8,128)S(1)}, u32[]{:S(2)}, u32[]{:S(2)}) async-start(f32[64,32,128]{2,1,0:T(8,128)} %get-tuple-element.8), calls=%async_computation | async-start | bytes 2097152 | tf_op jit(solution)/shard_map/all_to_all | solution.py:165
  19.3 28.6 %copy-start.2 = (f32[1,32,128]{2,1,0:T(8,128)S(1)}, f32[1,32,128]{2,1,0:T(8,128)}, u32[]{:S(2)}) copy-start(f32[1,32,128]{2,1,0:T(8,128)} %param.9) | copy-start | bytes 49156
  19.4 3.1 %collective-permute-start = (f32[1,128,128]{2,1,0:T(8,128)S(1)}, f32[1,128,128]{2,1,0:T(8,128)S(1)}, u32[]{:S(2)}, u32[]{:S(2)}) collective-permute-start(f32[1,128,128]{2,1,0:T(8,128)S(1)} %coupled_inverse.1), channel_id=1, source_target_pairs={{0,64},{64,0},{128,192},{192,128},{256,320},{320,256},{384,448},{4... | collective-permute-start | bytes 196616 | tf_op jit(solution)/shard_map/ppermute | solution.py:187
  22.6 12.9 %collective-permute-start.1 = (f32[2,128,128]{2,1,0:T(8,128)S(1)}, f32[2,128,128]{2,1,0:T(8,128)S(1)}, u32[]{:S(2)}, u32[]{:S(2)}) collective-permute-start(f32[2,128,128]{2,1,0:T(8,128)S(1)} %pad_maximum_fusion.2), channel_id=1, source_target_pairs={{0,128},{64,192},{128,0},{192,64},{256,384},{320,448},{384,256},{4... | collective-permute-start | bytes 393224 | tf_op jit(solution)/shard_map/ppermute | solution.py:187
  29.5 18.3 %all-to-all-start.1 = ((f32[16,32,128]{2,1,0:T(8,128)}), f32[16,32,128]{2,1,0:T(8,128)S(1)}, u32[]{:S(2)}, u32[]{:S(2)}) async-start(f32[16,32,128]{2,1,0:T(8,128)} %reduce_sum.9), calls=%async_computation.1 | async-start | bytes 524288 | tf_op jit(solution)/shard_map/all_to_all | solution.py:165
  35.5 20.5 %collective-permute-start.2 = (f32[4,128,128]{2,1,0:T(8,128)S(1)}, f32[4,128,128]{2,1,0:T(8,128)S(1)}, u32[]{:S(2)}, u32[]{:S(2)}) collective-permute-start(f32[4,128,128]{2,1,0:T(8,128)S(1)} %pad_maximum_fusion.1), channel_id=1, source_target_pairs={{0,256},{64,320},{128,384},{192,448},{256,0},{320,64},{384,128},{4... | collective-permute-start | bytes 786440 | tf_op jit(solution)/shard_map/ppermute | solution.py:187
  48.6 12.7 %all-to-all-start.2 = ((f32[8,32,128]{2,1,0:T(8,128)}), f32[8,32,128]{2,1,0:T(8,128)S(1)}, u32[]{:S(2)}, u32[]{:S(2)}) async-start(f32[8,32,128]{2,1,0:T(8,128)} %reduce_right.1), calls=%async_computation.2 | async-start | bytes 262144 | tf_op jit(solution)/shard_map/all_to_all | solution.py:243
  64.0 17.1 %all-to-all-start.3 = ((f32[16,32,128]{2,1,0:T(8,128)}), f32[16,32,128]{2,1,0:T(8,128)S(1)}, u32[]{:S(2)}, u32[]{:S(2)}) async-start(f32[16,32,128]{2,1,0:T(8,128)} %get-tuple-element.10), calls=%async_computation.3 | async-start | bytes 524288 | tf_op jit(solution)/shard_map/all_to_all | solution.py:165
  71.7 23.5 %copy-start.3 = (s32[1,28,1]{1,2,0:T(1,128)S(1)}, s32[1,28,1]{1,2,0:T(1,128)}, u32[]{:S(2)}) copy-start(s32[1,28,1]{1,2,0:T(1,128)} %param.13) | copy-start | bytes 340

commit v10 on v9

--- a/solution.py
+++ b/solution.py
@@ -240,7 +240,7 @@
     right = call(reduce_right, [VMEM, VMEM, VMEM], VMEM, floats(groups, width, size))(
         received, rhs_sep[0], separator_inverse
     )
-    right = lax.all_to_all(right, "leaf", 0, 0, tiled=True)
+    right, mapped = lax.optimization_barrier((lax.all_to_all(right, "leaf", 0, 0, tiled=True), mapped))
     x_sep, copies = call(
         chain,
         [SMEM, VMEM, VMEM, VMEM],
@@ -248,7 +248,7 @@
         [floats(width, size), floats(fronts // CLASSES, width, size)],
         scratch_shapes=[pltpu.VMEM((groups, width, size), jnp.float32)],
     )(lax.axis_index("leaf").reshape(1), right, coupled, separator_inverse)
-    gathered, mapped = lax.optimization_barrier((exchange(copies, members), mapped))
+    gathered = exchange(copies, members)
     gathered = jnp.broadcast_to(gathered[None], (CLASSES, *gathered.shape)).reshape(fronts, width, size)
     gathered = exchange(gathered, neighbours)
     x_leaf = call(

time: 97.5 us -> 100 us (1.026)
  blocking collectives: 14 us -> 34 us
  waiting for transfers between devices: 26.5 us -> 11.9 us
  starting transfers between devices: 41.1 us -> 36.9 us
  other arithmetic: 0.85 us -> 2.51 us
    all_to_all x1 -> x2, blocking collectives: 14 us -> 34 us  [exchange(): lax.all_to_all(value, ('leaf', 'front'), 0, 0, tiled=True, axis_index_gro...]
    all_to_all x3 -> x2, waiting for transfers between devices: 20.1 us -> 6.42 us  [exchange(): lax.all_to_all(value, ('leaf', 'front'), 0, 0, tiled=True, axis_index_gro...]
    all_to_all x3 -> x2, starting transfers between devices: 24 us -> 19.8 us  [exchange(): lax.all_to_all(value, ('leaf', 'front'), 0, 0, tiled=True, axis_index_gro...]
    concatenate x3, other arithmetic: 0.06 us -> 1.72 us  [gather_by_bits(): value = jnp.concatenate([value, lax.ppermute(value, axis, pairs)], axis=0)]
  transfers between devices with their start and end apart: 7 -> 6, of which waited for: 5 -> 4; matrix products, arithmetic and copies ran while one was open for 1% -> 3% of each run, Pallas kernels for 5% -> 5%
where the time goes in v10:
time: 100 us; the launch traced here: 99.7 us
  starting transfers between devices  36.9 us (37%)
  blocking collectives  34 us (34%)
  Pallas kernels  13.4 us (13%)
  waiting for transfers between devices  11.9 us (12%)
  other arithmetic  2.51 us (3%)
    all_to_all x2, blocking collectives, exchange(): lax.all_to_all(value, ('leaf', 'front'), 0, 0, tiled=True, axis_index_gro...  34 us
    all_to_all x2, starting transfers between devices, exchange(): lax.all_to_all(value, ('leaf', 'front'), 0, 0, tiled=True, axis_index_gro...  19.8 us
    ppermute x3, starting transfers between devices, gather_by_bits(): value = jnp.concatenate([value, lax.ppermute(value, axis, pairs)], axis=0)  9.68 us
    all_to_all x1, starting transfers between devices, per_device(): lax.all_to_all(right, 'leaf', 0, 0, tiled=True)  7.4 us
    all_to_all x2, waiting for transfers between devices, exchange(): lax.all_to_all(value, ('leaf', 'front'), 0, 0, tiled=True, axis_index_gro...  6.42 us
    pallas_call x1, Pallas kernels, per_device(): call(leaf_forward, [SMEM, columns, matrices, matrices, lines], [vectors,...  4.71 us
    all_to_all x1, waiting for transfers between devices, per_device(): lax.all_to_all(right, 'leaf', 0, 0, tiled=True)  4.28 us
    pallas_call x1, Pallas kernels, per_device(): call(leaf_prepare, [vectors, matrices, matrices, lines], pl.BlockSpec((PR...  3.53 us
  transfers between devices with their start and end apart: 6, of which 4 were waited for; matrix products, arithmetic and copies ran while one was open for 3% of the time, Pallas kernels for 5%

profile of v10, /device:TPU:1, one launch (start us, length us, event | category | flops | bytes accessed | tf_op | source)
XLA Modules:
  0.0 99.7 jit_solution(15362553592241812910)
XLA Ops:
  0.6 4.7 %leaf_forward.1 = (f32[28,32,128]{2,1,0:T(8,128)S(1)}, f32[64,32,128]{2,1,0:T(8,128)}) custom-call(s32[28]{0:T(128)} %bitcast.18, f32[32,3584]{1,0:T(8,128)} %bitcast.26, f32[28,128,128]{2,1,0:T(8,128)} %bitcast.20, f32[28,128,128]{2,1,0:T(8,128)} %bitcast.22, s32[28,1,128]{2,1,0:T(1,128)} %bitcast.28), custom_call_target="tpu_custom_call" | custom-call | tf_op jit(solution)/shard_map/leaf_forward/pallas_call | solution.py:217
  5.3 0.0 copy-start
  5.3 0.0 copy-start.1
  5.3 13.9 %all-to-all-start = ((f32[64,32,128]{2,1,0:T(8,128)}), f32[64,32,128]{2,1,0:T(8,128)S(1)}, u32[]{:S(2)}, u32[]{:S(2)}) async-start(f32[64,32,128]{2,1,0:T(8,128)} %get-tuple-element.8), calls=%async_computation | async-start | bytes 2097152 | tf_op jit(solution)/shard_map/all_to_all | solution.py:165
  19.2 0.0 copy-done
  19.2 0.0 copy-done.1
  19.2 0.2 coupled_inverse.1
  19.4 1.9 %collective-permute-start = (f32[1,128,128]{2,1,0:T(8,128)S(1)}, f32[1,128,128]{2,1,0:T(8,128)S(1)}, u32[]{:S(2)}, u32[]{:S(2)}) collective-permute-start(f32[1,128,128]{2,1,0:T(8,128)S(1)} %coupled_inverse.1), channel_id=1, source_target_pairs={{0,64},{64,0},{128,192},{192,128},{256,320},{320,256},{384,448},{4... | collective-permute-start | bytes 196616 | tf_op jit(solution)/shard_map/ppermute | solution.py:187
  21.4 1.2 %collective-permute-done = f32[1,128,128]{2,1,0:T(8,128)S(1)} collective-permute-done((f32[1,128,128]{2,1,0:T(8,128)S(1)}, f32[1,128,128]{2,1,0:T(8,128)S(1)}, u32[]{:S(2)}, u32[]{:S(2)}) %collective-permute-start) | collective-permute-done | bytes 65568 | tf_op jit(solution)/shard_map/ppermute | solution.py:187
  22.6 3.1 %collective-permute-start.1 = (f32[2,128,128]{2,1,0:T(8,128)S(1)}, f32[2,128,128]{2,1,0:T(8,128)S(1)}, u32[]{:S(2)}, u32[]{:S(2)}) collective-permute-start(f32[2,128,128]{2,1,0:T(8,128)S(1)} %pad_maximum_fusion.2), channel_id=1, source_target_pairs={{0,128},{64,192},{128,0},{192,64},{256,384},{320,448},{384,256},{4... | collective-permute-start | bytes 393224 | tf_op jit(solution)/shard_map/ppermute | solution.py:187
  25.7 3.0 %all-to-all-done = f32[64,32,128]{2,1,0:T(8,128)S(1)} async-done(((f32[64,32,128]{2,1,0:T(8,128)}), f32[64,32,128]{2,1,0:T(8,128)S(1)}, u32[]{:S(2)}, u32[]{:S(2)}) %all-to-all-start) | async-done | bytes 1048608 | tf_op jit(solution)/shard_map/all_to_all | solution.py:165
  28.7 0.8 reduce_sum.9
  29.5 5.9 %all-to-all-start.1 = ((f32[16,32,128]{2,1,0:T(8,128)}), f32[16,32,128]{2,1,0:T(8,128)S(1)}, u32[]{:S(2)}, u32[]{:S(2)}) async-start(f32[16,32,128]{2,1,0:T(8,128)} %reduce_sum.9), calls=%async_computation.1 | async-start | bytes 524288 | tf_op jit(solution)/shard_map/all_to_all | solution.py:165
  35.5 0.0 collective-permute-done.1
  35.5 0.7 pad_maximum_fusion.1
  36.2 4.6 %collective-permute-start.2 = (f32[4,128,128]{2,1,0:T(8,128)}, f32[4,128,128]{2,1,0:T(8,128)}, u32[]{:S(2)}, u32[]{:S(2)}) collective-permute-start(f32[4,128,128]{2,1,0:T(8,128)} %pad_maximum_fusion.1), channel_id=1, source_target_pairs={{0,256},{64,320},{128,384},{192,448},{256,0},{320,64},{384,128},{4... | collective-permute-start | bytes 786440 | tf_op jit(solution)/shard_map/ppermute | solution.py:187
  40.9 0.0 copy-start.2
  40.9 3.5 %leaf_prepare.1.mapped_ref = bf16[28,160,256]{2,1,0:T(8,128)(2,1)S(1)} custom-call(f32[28,32,128]{2,1,0:T(8,128)S(1)} %get-tuple-element.9.y_ref.after_ref, f32[28,128,128]{2,1,0:T(8,128)} %bitcast.21, f32[28,128,128]{2,1,0:T(8,128)} %bitcast.23, s32[28,1,128]{2,1,0:T(1,128)} %bitcast.29), custom_call_target="tpu_custom_call" | custom-call | tf_op jit(solution)/shard_map/leaf_prepare/pallas_call | solution.py:232
  44.4 3.4 %all-to-all-done.1.received_ref = f32[16,32,128]{2,1,0:T(8,128)S(1)} async-done(((f32[16,32,128]{2,1,0:T(8,128)}), f32[16,32,128]{2,1,0:T(8,128)S(1)}, u32[]{:S(2)}, u32[]{:S(2)}) %all-to-all-start.1) | async-done | bytes 262176 | tf_op jit(solution)/shard_map/all_to_all | solution.py:165
  47.8 0.0 copy-done.2
  47.8 0.8 reduce_right.1
  48.6 7.4 %all-to-all-start.2 = ((f32[8,32,128]{2,1,0:T(8,128)}), f32[8,32,128]{2,1,0:T(8,128)S(1)}, u32[]{:S(2)}, u32[]{:S(2)}) async-start(f32[8,32,128]{2,1,0:T(8,128)} %reduce_right.1), calls=%async_computation.2 | async-start | bytes 262144 | tf_op jit(solution)/shard_map/all_to_all | solution.py:243
  56.0 0.0 collective-permute-done.2
  56.0 1.0 pad_maximum_fusion.coupled_ref
  57.0 4.3 %all-to-all-done.2.right_ref = f32[8,32,128]{2,1,0:T(8,128)S(1)} async-done(((f32[8,32,128]{2,1,0:T(8,128)}), f32[8,32,128]{2,1,0:T(8,128)S(1)}, u32[]{:S(2)}, u32[]{:S(2)}) %all-to-all-start.2) | async-done | bytes 131104 | tf_op jit(solution)/shard_map/all_to_all | solution.py:243
  61.3 2.6 %chain.1 = (f32[32,128]{1,0:T(8,128)}, f32[16,32,128]{2,1,0:T(8,128)S(1)}) custom-call(s32[1]{0:T(128)} %bitcast.1.group_ref, f32[8,32,128]{2,1,0:T(8,128)S(1)} %all-to-all-done.2.right_ref, f32[8,128,128]{2,1,0:T(8,128)S(1)} %pad_maximum_fusion.coupled_ref, f32[128,128]{1,0:T(8,128)S(1)} %bitcast.15), custom_call_target="tpu_custom_call" | custom-call | tf_op jit(solution)/shard_map/chain/pallas_call | solution.py:244
  63.9 17.3 %all_to_all.25 = f32[16,32,128]{2,1,0:T(8,128)S(1)} all-to-all(f32[16,32,128]{2,1,0:T(8,128)S(1)} %get-tuple-element.11), channel_id=1, replica_groups={{0,2,4,6,16,18,20,22,32,34,36,38,48,50,52,54},{1,3,5,7,17,19,21,23,33,3..., dimensions={0} | all-to-all | bytes 524288 | tf_op jit(solution)/shard_map/all_to_all | solution.py:165
  81.2 0.0 copy-start.3
  81.2 0.1 broadcast_in_dim.12
  81.3 16.7 %all_to_all.26.x_ref = f32[64,32,128]{2,1,0:T(8,128)S(1)} all-to-all(f32[64,32,128]{2,1,0:T(8,128)S(1)} %bitcast.24), channel_id=1, replica_groups={{0,1,8,9},{2,3,10,11},{4,5,12,13},{6,7,14,15},{16,17,24,25},{18,19,26,2..., dimensions={0} | all-to-all | bytes 2097152 | tf_op jit(solution)/shard_map/all_to_all | solution.py:165
  98.0 0.0 copy-done.3
  98.0 1.6 %leaf_backward.1 = f32[32,3584]{1,0:T(8,128)} custom-call(s32[28]{0:T(128)S(1)} %bitcast.19, f32[64,32,128]{2,1,0:T(8,128)S(1)} %all_to_all.26.x_ref, bf16[28,160,256]{2,1,0:T(8,128)(2,1)S(1)} %leaf_prepare.1.mapped_ref), custom_call_target="tpu_custom_call" | custom-call | tf_op jit(solution)/shard_map/leaf_backward/pallas_call | solution.py:254
  (1 shorter events, 0.0 us)
Async XLA Ops:
  5.3 13.9 %copy-start = (f32[1,1,128,128]{3,2,1,0:T(8,128)S(1)}, f32[1,1,128,128]{3,2,1,0:T(8,128)}, u32[]{:S(2)}) copy-start(f32[1,1,128,128]{3,2,1,0:T(8,128)} %param.14) | copy-start | bytes 196612
  5.3 13.9 %copy-start.1 = (f32[1,1,128,128]{3,2,1,0:T(8,128)S(1)}, f32[1,1,128,128]{3,2,1,0:T(8,128)}, u32[]{:S(2)}) copy-start(f32[1,1,128,128]{3,2,1,0:T(8,128)} %param.15) | copy-start | bytes 196612
  5.3 23.4 %all-to-all-start = ((f32[64,32,128]{2,1,0:T(8,128)}), f32[64,32,128]{2,1,0:T(8,128)S(1)}, u32[]{:S(2)}, u32[]{:S(2)}) async-start(f32[64,32,128]{2,1,0:T(8,128)} %get-tuple-element.8), calls=%async_computation | async-start | bytes 2097152 | tf_op jit(solution)/shard_map/all_to_all | solution.py:165
  19.4 3.1 %collective-permute-start = (f32[1,128,128]{2,1,0:T(8,128)S(1)}, f32[1,128,128]{2,1,0:T(8,128)S(1)}, u32[]{:S(2)}, u32[]{:S(2)}) collective-permute-start(f32[1,128,128]{2,1,0:T(8,128)S(1)} %coupled_inverse.1), channel_id=1, source_target_pairs={{0,64},{64,0},{128,192},{192,128},{256,320},{320,256},{384,448},{4... | collective-permute-start | bytes 196616 | tf_op jit(solution)/shard_map/ppermute | solution.py:187
  22.6 12.9 %collective-permute-start.1 = (f32[2,128,128]{2,1,0:T(8,128)S(1)}, f32[2,128,128]{2,1,0:T(8,128)S(1)}, u32[]{:S(2)}, u32[]{:S(2)}) collective-permute-start(f32[2,128,128]{2,1,0:T(8,128)S(1)} %pad_maximum_fusion.2), channel_id=1, source_target_pairs={{0,128},{64,192},{128,0},{192,64},{256,384},{320,448},{384,256},{4... | collective-permute-start | bytes 393224 | tf_op jit(solution)/shard_map/ppermute | solution.py:187
  29.5 18.3 %all-to-all-start.1 = ((f32[16,32,128]{2,1,0:T(8,128)}), f32[16,32,128]{2,1,0:T(8,128)S(1)}, u32[]{:S(2)}, u32[]{:S(2)}) async-start(f32[16,32,128]{2,1,0:T(8,128)} %reduce_sum.9), calls=%async_computation.1 | async-start | bytes 524288 | tf_op jit(solution)/shard_map/all_to_all | solution.py:165
  36.2 19.8 %collective-permute-start.2 = (f32[4,128,128]{2,1,0:T(8,128)}, f32[4,128,128]{2,1,0:T(8,128)}, u32[]{:S(2)}, u32[]{:S(2)}) collective-permute-start(f32[4,128,128]{2,1,0:T(8,128)} %pad_maximum_fusion.1), channel_id=1, source_target_pairs={{0,256},{64,320},{128,384},{192,448},{256,0},{320,64},{384,128},{4... | collective-permute-start | bytes 786440 | tf_op jit(solution)/shard_map/ppermute | solution.py:187
  40.9 7.0 %copy-start.2 = (f32[1,32,128]{2,1,0:T(8,128)S(1)}, f32[1,32,128]{2,1,0:T(8,128)}, u32[]{:S(2)}) copy-start(f32[1,32,128]{2,1,0:T(8,128)} %param.9) | copy-start | bytes 49156
  48.6 12.7 %all-to-all-start.2 = ((f32[8,32,128]{2,1,0:T(8,128)}), f32[8,32,128]{2,1,0:T(8,128)S(1)}, u32[]{:S(2)}, u32[]{:S(2)}) async-start(f32[8,32,128]{2,1,0:T(8,128)} %reduce_right.1), calls=%async_computation.2 | async-start | bytes 262144 | tf_op jit(solution)/shard_map/all_to_all | solution.py:243
  81.2 16.9 %copy-start.3 = (s32[1,28,1]{1,2,0:T(1,128)S(1)}, s32[1,28,1]{1,2,0:T(1,128)}, u32[]{:S(2)}) copy-start(s32[1,28,1]{1,2,0:T(1,128)} %param.13) | copy-start | bytes 340

commit v11 on v9

--- a/solution.py
+++ b/solution.py
@@ -40,13 +40,18 @@
     return jnp.where(separator_row == row_index, 1.0, 0.0).astype(jnp.bfloat16)
 
 
-def slot_of(owner):
-    y, z = owner >> EDGE_BITS, owner & (EDGE - 1)
+def class_of(index):
+    return (index & 1) ^ (index >> (EDGE_BITS - 1))
+
+
+def slot_of(owner, leaf):
+    y = ((owner >> EDGE_BITS) - (leaf & 1)) & (EDGE - 1)
+    z = (owner - (leaf & 1)) & (EDGE - 1)
     place = ((y >> 1) << (EDGE_BITS - 1)) | (z >> 1)
-    return (((y & 1) << 1) | (z & 1)) * (EDGE * EDGE // CLASSES) + place
-
-
-def leaf_forward(owner_ref, rhs_ref, inv_ref, update_ref, rows_ref, y_ref, dense_ref):
+    return ((class_of(y) << 1) | class_of(z)) * (EDGE * EDGE // CLASSES) + place
+
+
+def leaf_forward(leaf_ref, owner_ref, rhs_ref, inv_ref, update_ref, rows_ref, y_ref, dense_ref):
     step = pl.program_id(0)
     count, size, _ = inv_ref.shape
 
@@ -60,7 +65,7 @@
     updates = [product(leaf_y[f], update_ref[f], NT) for f in range(count)]
     placed = [select(updates[f], chosen_rows(rows_ref[f], size), NT) for f in range(count)]
     for f in range(count):
-        dense_ref[slot_of(owner_ref[step * count + f])] = placed[f]
+        dense_ref[slot_of(owner_ref[step * count + f], leaf_ref[0])] = placed[f]
 
 
 def coupled_inverse(inv_ref, couple_ref, after_ref, out_ref):
@@ -106,13 +111,13 @@
         copies_ref[copy] = x_sep
 
 
-def leaf_backward(owner_ref, x_ref, mapped_ref, out_hbm, out_ref, stored):
+def leaf_backward(leaf_ref, owner_ref, x_ref, mapped_ref, out_hbm, out_ref, stored):
     count = mapped_ref.shape[0]
     rows = out_ref.shape[0]
     size = out_ref.shape[1] // count
     stores = []
     for f in range(count):
-        owned = jnp.concatenate(split(x_ref[slot_of(owner_ref[f])]), axis=0)
+        owned = jnp.concatenate(split(x_ref[slot_of(owner_ref[f], leaf_ref[0])]), axis=0)
         picked = three_parts(dot(owned, mapped_ref[f, :size], NN), rows, size)
         own = mapped_ref[f, size:].astype(jnp.float32)
         out_ref[:, f * size : (f + 1) * size] = (own[:, :size] + own[:, size:]) - picked
@@ -165,19 +170,24 @@
     return lax.all_to_all(value, ("leaf", "front"), 0, 0, tiled=True, axis_index_groups=groups)
 
 
+def device(y, z, leaf):
+    return (y + leaf % 2) % EDGE * EDGE + (z + leaf % 2) % EDGE
+
+
+def of_class(first, kind):
+    return first if class_of(first) == kind else first + 1
+
+
 def neighbours(leaf):
-    groups = []
-    for y in range(leaf % 2, EDGE + leaf % 2, 2):
-        for z in range(leaf % 2, EDGE + leaf % 2, 2):
-            four = [((y + a) % EDGE, (z + b) % EDGE) for a in range(2) for b in range(2)]
-            four.sort(key=lambda at: (at[0] % 2, at[1] % 2))
-            groups.append([a * EDGE + b for a, b in four])
-    return groups
+    kinds = [(a, b) for a in range(2) for b in range(2)]
+    pairs = range(0, EDGE, 2)
+    return [[device(of_class(y, a), of_class(z, b), leaf) for a, b in kinds] for y in pairs for z in pairs]
 
 
 def members(leaf):
-    half = range(EDGE // 2)
-    return [[(2 * i + a) * EDGE + 2 * j + b for i in half for j in half] for a in range(2) for b in range(2)]
+    kinds = [(a, b) for a in range(2) for b in range(2)]
+    pairs = range(0, EDGE, 2)
+    return [[device(of_class(y, a), of_class(z, b), leaf) for y in pairs for z in pairs] for a, b in kinds]
 
 
 def gather_by_bits(value, axis):
@@ -212,15 +222,16 @@
         columns = pl.BlockSpec((width, step * size), lambda s: (0, s))
         return matrices, lines, vectors, columns
 
+    leaf = lax.axis_index("leaf").reshape(1)
     matrices, lines, vectors, columns = specs(FORWARD_STEP)
     whole = pl.BlockSpec((fronts, width, size), lambda s: (0, 0, 0))
     leaf_y, dense = call(
         leaf_forward,
-        [SMEM, columns, matrices, matrices, lines],
+        [SMEM, SMEM, columns, matrices, matrices, lines],
         [vectors, whole],
         [floats(front_count, width, size), floats(fronts, width, size)],
         grid=(front_count // FORWARD_STEP,),
-    )(owners, right_leaf, inverse, coupling, rows)
+    )(leaf, owners, right_leaf, inverse, coupling, rows)
     received = exchange(dense, neighbours).reshape(CLASSES, fronts // CLASSES, width, size)
     received = exchange(jnp.sum(received, axis=0), members)
 
@@ -253,14 +264,14 @@
     gathered = exchange(gathered, neighbours)
     x_leaf = call(
         leaf_backward,
-        [SMEM, VMEM, VMEM],
+        [SMEM, SMEM, VMEM, VMEM],
         ANY,
         floats(width, front_count * size),
         scratch_shapes=[
             pltpu.VMEM((width, front_count * size), jnp.float32),
             pltpu.SemaphoreType.DMA((front_count // BACKWARD_CHUNK,)),
         ],
-    )(update_owner.reshape(front_count), gathered, mapped)
+    )(leaf, update_owner.reshape(front_count), gathered, mapped)
     return (x_leaf[None], x_sep[None])
 
 

time: 97.5 us -> 95 us (0.974)
  waiting for transfers between devices: 26.5 us -> 18.6 us
  starting transfers between devices: 41.1 us -> 44.5 us
  blocking collectives: 14 us -> 16.1 us
    all_to_all x3, waiting for transfers between devices: 20.1 us -> 12.1 us  [exchange(): lax.all_to_all(value, ('leaf', 'front'), 0, 0, tiled=True, axis_index_gro...]
    all_to_all x1, blocking collectives: 14 us -> 16.1 us  [exchange(): lax.all_to_all(value, ('leaf', 'front'), 0, 0, tiled=True, axis_index_gro...]
    all_to_all x3, starting transfers between devices: 24 us -> 26.1 us  [exchange(): lax.all_to_all(value, ('leaf', 'front'), 0, 0, tiled=True, axis_index_gro...]
    all_to_all x1, starting transfers between devices: 7.4 us -> 8.75 us  [per_device(): right = lax.all_to_all(right, 'leaf', 0, 0, tiled=True)]
where the time goes in v11:
time: 95 us; the launch traced here: 94.4 us
  starting transfers between devices  44.5 us (47%)
  waiting for transfers between devices  18.6 us (20%)
  blocking collectives  16.1 us (17%)
  Pallas kernels  13.5 us (14%)
    all_to_all x3, starting transfers between devices, exchange(): lax.all_to_all(value, ('leaf', 'front'), 0, 0, tiled=True, axis_index_gro...  26.1 us
    all_to_all x1, blocking collectives, exchange(): lax.all_to_all(value, ('leaf', 'front'), 0, 0, tiled=True, axis_index_gro...  16.1 us
    all_to_all x3, waiting for transfers between devices, exchange(): lax.all_to_all(value, ('leaf', 'front'), 0, 0, tiled=True, axis_index_gro...  12.1 us
    ppermute x3, starting transfers between devices, gather_by_bits(): value = jnp.concatenate([value, lax.ppermute(value, axis, pairs)], axis=0)  9.69 us
    all_to_all x1, starting transfers between devices, per_device(): right = lax.all_to_all(right, 'leaf', 0, 0, tiled=True)  8.75 us
    all_to_all x1, waiting for transfers between devices, per_device(): right = lax.all_to_all(right, 'leaf', 0, 0, tiled=True)  5.23 us
    pallas_call x1, Pallas kernels, per_device(): call(leaf_forward, [SMEM, SMEM, columns, matrices, matrices, lines], [vec...  4.72 us
    pallas_call x1, Pallas kernels, per_device(): call(leaf_prepare, [vectors, matrices, matrices, lines], pl.BlockSpec((PR...  3.52 us
  transfers between devices with their start and end apart: 7, of which 5 were waited for; matrix products, arithmetic and copies ran while one was open for 1% of the time, Pallas kernels for 5%

profile of v11, /device:TPU:1, one launch (start us, length us, event | category | flops | bytes accessed | tf_op | source)
XLA Modules:
  0.0 94.4 jit_solution(1070963899604870339)
XLA Ops:
  0.6 4.7 %leaf_forward.1 = (f32[28,32,128]{2,1,0:T(8,128)S(1)}, f32[64,32,128]{2,1,0:T(8,128)}) custom-call(s32[1]{0:T(128)} %bitcast.leaf_ref.group_ref, s32[28]{0:T(128)} %bitcast.18, f32[32,3584]{1,0:T(8,128)} %bitcast.26, f32[28,128,128]{2,1,0:T(8,128)} %bitcast.20, f32[28,128,128]{2,1,0:T(8,128)} %bitcast.22, s32[28,1,128]{2,1,0:T(1,128)} %bitcast.28), custom_call_target="tpu_custom_call" | custom-call | tf_op jit(solution)/shard_map/leaf_forward/pallas_call | solution.py:228
  5.4 0.0 copy-start
  5.4 0.0 copy-start.1
  5.4 13.9 %all-to-all-start = ((f32[64,32,128]{2,1,0:T(8,128)}), f32[64,32,128]{2,1,0:T(8,128)S(1)}, u32[]{:S(2)}, u32[]{:S(2)}) async-start(f32[64,32,128]{2,1,0:T(8,128)} %get-tuple-element.8), calls=%async_computation | async-start | bytes 2097152 | tf_op jit(solution)/shard_map/all_to_all | solution.py:170
  19.3 0.0 copy-start.2
  19.3 0.0 copy-done
  19.3 0.0 copy-done.1
  19.3 0.2 coupled_inverse.1
  19.4 1.9 %collective-permute-start = (f32[1,128,128]{2,1,0:T(8,128)S(1)}, f32[1,128,128]{2,1,0:T(8,128)S(1)}, u32[]{:S(2)}, u32[]{:S(2)}) collective-permute-start(f32[1,128,128]{2,1,0:T(8,128)S(1)} %coupled_inverse.1), channel_id=1, source_target_pairs={{0,64},{64,0},{128,192},{192,128},{256,320},{320,256},{384,448},{4... | collective-permute-start | bytes 196616 | tf_op jit(solution)/shard_map/ppermute | solution.py:197
  21.4 1.2 %collective-permute-done = f32[1,128,128]{2,1,0:T(8,128)S(1)} collective-permute-done((f32[1,128,128]{2,1,0:T(8,128)S(1)}, f32[1,128,128]{2,1,0:T(8,128)S(1)}, u32[]{:S(2)}, u32[]{:S(2)}) %collective-permute-start) | collective-permute-done | bytes 65568 | tf_op jit(solution)/shard_map/ppermute | solution.py:197
  22.6 3.1 %collective-permute-start.1 = (f32[2,128,128]{2,1,0:T(8,128)S(1)}, f32[2,128,128]{2,1,0:T(8,128)S(1)}, u32[]{:S(2)}, u32[]{:S(2)}) collective-permute-start(f32[2,128,128]{2,1,0:T(8,128)S(1)} %pad_maximum_fusion.2), channel_id=1, source_target_pairs={{0,128},{64,192},{128,0},{192,64},{256,384},{320,448},{384,256},{4... | collective-permute-start | bytes 393224 | tf_op jit(solution)/shard_map/ppermute | solution.py:197
  25.7 3.0 %all-to-all-done = f32[64,32,128]{2,1,0:T(8,128)S(1)} async-done(((f32[64,32,128]{2,1,0:T(8,128)}), f32[64,32,128]{2,1,0:T(8,128)S(1)}, u32[]{:S(2)}, u32[]{:S(2)}) %all-to-all-start) | async-done | bytes 1048608 | tf_op jit(solution)/shard_map/all_to_all | solution.py:170
  28.7 0.8 reduce_sum.9
  29.5 5.5 %all-to-all-start.1 = ((f32[16,32,128]{2,1,0:T(8,128)}), f32[16,32,128]{2,1,0:T(8,128)S(1)}, u32[]{:S(2)}, u32[]{:S(2)}) async-start(f32[16,32,128]{2,1,0:T(8,128)} %reduce_sum.9), calls=%async_computation.1 | async-start | bytes 524288 | tf_op jit(solution)/shard_map/all_to_all | solution.py:170
  35.0 0.0 collective-permute-done.1
  35.0 4.6 %collective-permute-start.2 = (f32[4,128,128]{2,1,0:T(8,128)S(1)}, f32[4,128,128]{2,1,0:T(8,128)S(1)}, u32[]{:S(2)}, u32[]{:S(2)}) collective-permute-start(f32[4,128,128]{2,1,0:T(8,128)S(1)} %pad_maximum_fusion.1), channel_id=1, source_target_pairs={{0,256},{64,320},{128,384},{192,448},{256,0},{320,64},{384,128},{4... | collective-permute-start | bytes 786440 | tf_op jit(solution)/shard_map/ppermute | solution.py:197
  39.7 3.8 %all-to-all-done.1.received_ref = f32[16,32,128]{2,1,0:T(8,128)S(1)} async-done(((f32[16,32,128]{2,1,0:T(8,128)}), f32[16,32,128]{2,1,0:T(8,128)S(1)}, u32[]{:S(2)}, u32[]{:S(2)}) %all-to-all-start.1) | async-done | bytes 262176 | tf_op jit(solution)/shard_map/all_to_all | solution.py:170
  43.5 0.0 copy-done.2
  43.5 0.8 reduce_right.1
  44.3 8.7 %all-to-all-start.2 = ((f32[8,32,128]{2,1,0:T(8,128)}), f32[8,32,128]{2,1,0:T(8,128)S(1)}, u32[]{:S(2)}, u32[]{:S(2)}) async-start(f32[8,32,128]{2,1,0:T(8,128)} %reduce_right.1), calls=%async_computation.2 | async-start | bytes 262144 | tf_op jit(solution)/shard_map/all_to_all | solution.py:254
  53.1 0.0 collective-permute-done.2
  53.1 5.2 %all-to-all-done.2.right_ref = f32[8,32,128]{2,1,0:T(8,128)S(1)} async-done(((f32[8,32,128]{2,1,0:T(8,128)}), f32[8,32,128]{2,1,0:T(8,128)S(1)}, u32[]{:S(2)}, u32[]{:S(2)}) %all-to-all-start.2) | async-done | bytes 131104 | tf_op jit(solution)/shard_map/all_to_all | solution.py:254
  58.3 2.7 %chain.1 = (f32[32,128]{1,0:T(8,128)}, f32[16,32,128]{2,1,0:T(8,128)}) custom-call(s32[1]{0:T(128)} %bitcast.leaf_ref.group_ref, f32[8,32,128]{2,1,0:T(8,128)S(1)} %all-to-all-done.2.right_ref, f32[8,128,128]{2,1,0:T(8,128)S(1)} %pad_maximum_fusion.coupled_ref, f32[128,128]{1,0:T(8,128)S(1)} %bitcast.15), custom_call_target="tpu_custom_call" | custom-call | tf_op jit(solution)/shard_map/chain/pallas_call | solution.py:255
  61.0 6.7 %all-to-all-start.3 = ((f32[16,32,128]{2,1,0:T(8,128)}), f32[16,32,128]{2,1,0:T(8,128)S(1)}, u32[]{:S(2)}, u32[]{:S(2)}) async-start(f32[16,32,128]{2,1,0:T(8,128)} %get-tuple-element.10), calls=%async_computation.3 | async-start | bytes 524288 | tf_op jit(solution)/shard_map/all_to_all | solution.py:170
  67.7 3.5 %leaf_prepare.1.mapped_ref = bf16[28,160,256]{2,1,0:T(8,128)(2,1)S(1)} custom-call(f32[28,32,128]{2,1,0:T(8,128)S(1)} %get-tuple-element.9.after_ref.y_ref, f32[28,128,128]{2,1,0:T(8,128)} %bitcast.21, f32[28,128,128]{2,1,0:T(8,128)} %bitcast.23, s32[28,1,128]{2,1,0:T(1,128)} %bitcast.29), custom_call_target="tpu_custom_call" | custom-call | tf_op jit(solution)/shard_map/leaf_prepare/pallas_call | solution.py:243
  71.3 0.0 copy-start.3
  71.3 5.3 %all-to-all-done.3 = f32[16,32,128]{2,1,0:T(8,128)S(1)} async-done(((f32[16,32,128]{2,1,0:T(8,128)}), f32[16,32,128]{2,1,0:T(8,128)S(1)}, u32[]{:S(2)}, u32[]{:S(2)}) %all-to-all-start.3) | async-done | bytes 262176 | tf_op jit(solution)/shard_map/all_to_all | solution.py:170
  76.6 0.1 broadcast_in_dim.12
  76.7 16.1 %all_to_all.25.x_ref = f32[64,32,128]{2,1,0:T(8,128)S(1)} all-to-all(f32[64,32,128]{2,1,0:T(8,128)S(1)} %bitcast.24), channel_id=1, replica_groups={{0,1,8,9},{2,3,10,11},{5,4,13,12},{7,6,15,14},{16,17,24,25},{18,19,26,2..., dimensions={0} | all-to-all | bytes 2097152 | tf_op jit(solution)/shard_map/all_to_all | solution.py:170
  92.8 0.0 copy-done.3
  92.8 1.6 %leaf_backward.1 = f32[32,3584]{1,0:T(8,128)} custom-call(s32[1]{0:T(128)} %bitcast.leaf_ref.group_ref, s32[28]{0:T(128)S(1)} %bitcast.19, f32[64,32,128]{2,1,0:T(8,128)S(1)} %all_to_all.25.x_ref, bf16[28,160,256]{2,1,0:T(8,128)(2,1)S(1)} %leaf_prepare.1.mapped_ref), custom_call_target="tpu_custom_call" | custom-call | tf_op jit(solution)/shard_map/leaf_backward/pallas_call | solution.py:265
  (3 shorter events, 0.1 us)
Async XLA Ops:
  5.4 13.9 %copy-start = (f32[1,1,128,128]{3,2,1,0:T(8,128)S(1)}, f32[1,1,128,128]{3,2,1,0:T(8,128)}, u32[]{:S(2)}) copy-start(f32[1,1,128,128]{3,2,1,0:T(8,128)} %param.14) | copy-start | bytes 196612
  5.4 13.9 %copy-start.1 = (f32[1,1,128,128]{3,2,1,0:T(8,128)S(1)}, f32[1,1,128,128]{3,2,1,0:T(8,128)}, u32[]{:S(2)}) copy-start(f32[1,1,128,128]{3,2,1,0:T(8,128)} %param.15) | copy-start | bytes 196612
  5.4 23.4 %all-to-all-start = ((f32[64,32,128]{2,1,0:T(8,128)}), f32[64,32,128]{2,1,0:T(8,128)S(1)}, u32[]{:S(2)}, u32[]{:S(2)}) async-start(f32[64,32,128]{2,1,0:T(8,128)} %get-tuple-element.8), calls=%async_computation | async-start | bytes 2097152 | tf_op jit(solution)/shard_map/all_to_all | solution.py:170
  19.3 24.2 %copy-start.2 = (f32[1,32,128]{2,1,0:T(8,128)S(1)}, f32[1,32,128]{2,1,0:T(8,128)}, u32[]{:S(2)}) copy-start(f32[1,32,128]{2,1,0:T(8,128)} %param.9) | copy-start | bytes 49156
  19.4 3.1 %collective-permute-start = (f32[1,128,128]{2,1,0:T(8,128)S(1)}, f32[1,128,128]{2,1,0:T(8,128)S(1)}, u32[]{:S(2)}, u32[]{:S(2)}) collective-permute-start(f32[1,128,128]{2,1,0:T(8,128)S(1)} %coupled_inverse.1), channel_id=1, source_target_pairs={{0,64},{64,0},{128,192},{192,128},{256,320},{320,256},{384,448},{4... | collective-permute-start | bytes 196616 | tf_op jit(solution)/shard_map/ppermute | solution.py:197
  22.6 12.4 %collective-permute-start.1 = (f32[2,128,128]{2,1,0:T(8,128)S(1)}, f32[2,128,128]{2,1,0:T(8,128)S(1)}, u32[]{:S(2)}, u32[]{:S(2)}) collective-permute-start(f32[2,128,128]{2,1,0:T(8,128)S(1)} %pad_maximum_fusion.2), channel_id=1, source_target_pairs={{0,128},{64,192},{128,0},{192,64},{256,384},{320,448},{384,256},{4... | collective-permute-start | bytes 393224 | tf_op jit(solution)/shard_map/ppermute | solution.py:197
  29.5 14.0 %all-to-all-start.1 = ((f32[16,32,128]{2,1,0:T(8,128)}), f32[16,32,128]{2,1,0:T(8,128)S(1)}, u32[]{:S(2)}, u32[]{:S(2)}) async-start(f32[16,32,128]{2,1,0:T(8,128)} %reduce_sum.9), calls=%async_computation.1 | async-start | bytes 524288 | tf_op jit(solution)/shard_map/all_to_all | solution.py:170
  35.0 18.0 %collective-permute-start.2 = (f32[4,128,128]{2,1,0:T(8,128)S(1)}, f32[4,128,128]{2,1,0:T(8,128)S(1)}, u32[]{:S(2)}, u32[]{:S(2)}) collective-permute-start(f32[4,128,128]{2,1,0:T(8,128)S(1)} %pad_maximum_fusion.1), channel_id=1, source_target_pairs={{0,256},{64,320},{128,384},{192,448},{256,0},{320,64},{384,128},{4... | collective-permute-start | bytes 786440 | tf_op jit(solution)/shard_map/ppermute | solution.py:197
  44.3 14.0 %all-to-all-start.2 = ((f32[8,32,128]{2,1,0:T(8,128)}), f32[8,32,128]{2,1,0:T(8,128)S(1)}, u32[]{:S(2)}, u32[]{:S(2)}) async-start(f32[8,32,128]{2,1,0:T(8,128)} %reduce_right.1), calls=%async_computation.2 | async-start | bytes 262144 | tf_op jit(solution)/shard_map/all_to_all | solution.py:254
  61.0 15.5 %all-to-all-start.3 = ((f32[16,32,128]{2,1,0:T(8,128)}), f32[16,32,128]{2,1,0:T(8,128)S(1)}, u32[]{:S(2)}, u32[]{:S(2)}) async-start(f32[16,32,128]{2,1,0:T(8,128)} %get-tuple-element.10), calls=%async_computation.3 | async-start | bytes 524288 | tf_op jit(solution)/shard_map/all_to_all | solution.py:170
  71.3 21.5 %copy-start.3 = (s32[1,28,1]{1,2,0:T(1,128)S(1)}, s32[1,28,1]{1,2,0:T(1,128)}, u32[]{:S(2)}) copy-start(s32[1,28,1]{1,2,0:T(1,128)} %param.13) | copy-start | bytes 340

commit v12 on v11

--- a/solution.py
+++ b/solution.py
@@ -45,8 +45,9 @@
 
 
 def slot_of(owner, leaf):
-    y = ((owner >> EDGE_BITS) - (leaf & 1)) & (EDGE - 1)
-    z = (owner - (leaf & 1)) & (EDGE - 1)
+    shift = 1 - (leaf & 1)
+    y = ((owner >> EDGE_BITS) - shift) & (EDGE - 1)
+    z = (owner - shift) & (EDGE - 1)
     place = ((y >> 1) << (EDGE_BITS - 1)) | (z >> 1)
     return ((class_of(y) << 1) | class_of(z)) * (EDGE * EDGE // CLASSES) + place
 
@@ -171,7 +172,8 @@
 
 
 def device(y, z, leaf):
-    return (y + leaf % 2) % EDGE * EDGE + (z + leaf % 2) % EDGE
+    shift = 1 - leaf % 2
+    return (y + shift) % EDGE * EDGE + (z + shift) % EDGE
 
 
 def of_class(first, kind):

time: 95 us -> 97.5 us (1.026)
  the two profiles are of different devices: /device:TPU:1 before, /device:TPU:2 now
where the time goes in v12:
time: 97.5 us; the launch traced here: 96.9 us
  starting transfers between devices  40 us (41%)
  waiting for transfers between devices  23.7 us (24%)
  blocking collectives  17.9 us (18%)
  Pallas kernels  13.6 us (14%)
    all_to_all x3, starting transfers between devices, exchange(): lax.all_to_all(value, ('leaf', 'front'), 0, 0, tiled=True, axis_index_gro...  26.8 us
    all_to_all x1, blocking collectives, exchange(): lax.all_to_all(value, ('leaf', 'front'), 0, 0, tiled=True, axis_index_gro...  17.9 us
    all_to_all x3, waiting for transfers between devices, exchange(): lax.all_to_all(value, ('leaf', 'front'), 0, 0, tiled=True, axis_index_gro...  17.8 us
    ppermute x3, starting transfers between devices, gather_by_bits(): value = jnp.concatenate([value, lax.ppermute(value, axis, pairs)], axis=0)  8.39 us
    all_to_all x1, starting transfers between devices, per_device(): right = lax.all_to_all(right, 'leaf', 0, 0, tiled=True)  4.84 us
    pallas_call x1, Pallas kernels, per_device(): call(leaf_forward, [SMEM, SMEM, columns, matrices, matrices, lines], [vec...  4.72 us
    all_to_all x1, waiting for transfers between devices, per_device(): right = lax.all_to_all(right, 'leaf', 0, 0, tiled=True)  4.64 us
    pallas_call x1, Pallas kernels, per_device(): call(leaf_prepare, [vectors, matrices, matrices, lines], pl.BlockSpec((PR...  3.52 us
  transfers between devices with their start and end apart: 7, of which 5 were waited for; matrix products, arithmetic and copies ran while one was open for 1% of the time, Pallas kernels for 5%

profile of v12, /device:TPU:2, one launch (start us, length us, event | category | flops | bytes accessed | tf_op | source)
XLA Modules:
  0.0 96.9 jit_solution(1295191334203821185)
XLA Ops:
  0.6 4.7 %leaf_forward.1 = (f32[28,32,128]{2,1,0:T(8,128)S(1)}, f32[64,32,128]{2,1,0:T(8,128)}) custom-call(s32[1]{0:T(128)} %bitcast.leaf_ref.group_ref, s32[28]{0:T(128)} %bitcast.18, f32[32,3584]{1,0:T(8,128)} %bitcast.26, f32[28,128,128]{2,1,0:T(8,128)} %bitcast.20, f32[28,128,128]{2,1,0:T(8,128)} %bitcast.22, s32[28,1,128]{2,1,0:T(1,128)} %bitcast.28), custom_call_target="tpu_custom_call" | custom-call | tf_op jit(solution)/shard_map/leaf_forward/pallas_call | solution.py:230
  5.4 0.0 copy-start
  5.4 0.0 copy-start.1
  5.4 13.4 %all-to-all-start = ((f32[64,32,128]{2,1,0:T(8,128)}), f32[64,32,128]{2,1,0:T(8,128)S(1)}, u32[]{:S(2)}, u32[]{:S(2)}) async-start(f32[64,32,128]{2,1,0:T(8,128)} %get-tuple-element.8), calls=%async_computation | async-start | bytes 2097152 | tf_op jit(solution)/shard_map/all_to_all | solution.py:171
  18.7 0.0 copy-start.2
  18.7 0.0 copy-done
  18.7 0.0 copy-done.1
  18.7 0.2 coupled_inverse.1
  18.9 1.9 %collective-permute-start = (f32[1,128,128]{2,1,0:T(8,128)S(1)}, f32[1,128,128]{2,1,0:T(8,128)S(1)}, u32[]{:S(2)}, u32[]{:S(2)}) collective-permute-start(f32[1,128,128]{2,1,0:T(8,128)S(1)} %coupled_inverse.1), channel_id=1, source_target_pairs={{0,64},{64,0},{128,192},{192,128},{256,320},{320,256},{384,448},{4... | collective-permute-start | bytes 196616 | tf_op jit(solution)/shard_map/ppermute | solution.py:199
  20.8 1.2 %collective-permute-done = f32[1,128,128]{2,1,0:T(8,128)S(1)} collective-permute-done((f32[1,128,128]{2,1,0:T(8,128)S(1)}, f32[1,128,128]{2,1,0:T(8,128)S(1)}, u32[]{:S(2)}, u32[]{:S(2)}) %collective-permute-start) | collective-permute-done | bytes 65568 | tf_op jit(solution)/shard_map/ppermute | solution.py:199
  22.1 2.4 %collective-permute-start.1 = (f32[2,128,128]{2,1,0:T(8,128)S(1)}, f32[2,128,128]{2,1,0:T(8,128)S(1)}, u32[]{:S(2)}, u32[]{:S(2)}) collective-permute-start(f32[2,128,128]{2,1,0:T(8,128)S(1)} %pad_maximum_fusion.2), channel_id=1, source_target_pairs={{0,128},{64,192},{128,0},{192,64},{256,384},{320,448},{384,256},{4... | collective-permute-start | bytes 393224 | tf_op jit(solution)/shard_map/ppermute | solution.py:199
  24.5 4.8 %all-to-all-done = f32[64,32,128]{2,1,0:T(8,128)S(1)} async-done(((f32[64,32,128]{2,1,0:T(8,128)}), f32[64,32,128]{2,1,0:T(8,128)S(1)}, u32[]{:S(2)}, u32[]{:S(2)}) %all-to-all-start) | async-done | bytes 1048608 | tf_op jit(solution)/shard_map/all_to_all | solution.py:171
  29.4 0.8 reduce_sum.9
  30.1 5.7 %all-to-all-start.1 = ((f32[16,32,128]{2,1,0:T(8,128)}), f32[16,32,128]{2,1,0:T(8,128)S(1)}, u32[]{:S(2)}, u32[]{:S(2)}) async-start(f32[16,32,128]{2,1,0:T(8,128)} %reduce_sum.9), calls=%async_computation.1 | async-start | bytes 524288 | tf_op jit(solution)/shard_map/all_to_all | solution.py:171
  35.9 0.0 collective-permute-done.1
  35.9 4.0 %collective-permute-start.2 = (f32[4,128,128]{2,1,0:T(8,128)S(1)}, f32[4,128,128]{2,1,0:T(8,128)S(1)}, u32[]{:S(2)}, u32[]{:S(2)}) collective-permute-start(f32[4,128,128]{2,1,0:T(8,128)S(1)} %pad_maximum_fusion.1), channel_id=1, source_target_pairs={{0,256},{64,320},{128,384},{192,448},{256,0},{320,64},{384,128},{4... | collective-permute-start | bytes 786440 | tf_op jit(solution)/shard_map/ppermute | solution.py:199
  40.0 6.3 %all-to-all-done.1.received_ref = f32[16,32,128]{2,1,0:T(8,128)S(1)} async-done(((f32[16,32,128]{2,1,0:T(8,128)}), f32[16,32,128]{2,1,0:T(8,128)S(1)}, u32[]{:S(2)}, u32[]{:S(2)}) %all-to-all-start.1) | async-done | bytes 262176 | tf_op jit(solution)/shard_map/all_to_all | solution.py:171
  46.2 0.0 copy-done.2
  46.2 0.8 reduce_right.1
  47.1 4.8 %all-to-all-start.2 = ((f32[8,32,128]{2,1,0:T(8,128)}), f32[8,32,128]{2,1,0:T(8,128)S(1)}, u32[]{:S(2)}, u32[]{:S(2)}) async-start(f32[8,32,128]{2,1,0:T(8,128)} %reduce_right.1), calls=%async_computation.2 | async-start | bytes 262144 | tf_op jit(solution)/shard_map/all_to_all | solution.py:256
  51.9 0.0 collective-permute-done.2
  51.9 4.6 %all-to-all-done.2.right_ref = f32[8,32,128]{2,1,0:T(8,128)S(1)} async-done(((f32[8,32,128]{2,1,0:T(8,128)}), f32[8,32,128]{2,1,0:T(8,128)S(1)}, u32[]{:S(2)}, u32[]{:S(2)}) %all-to-all-start.2) | async-done | bytes 131104 | tf_op jit(solution)/shard_map/all_to_all | solution.py:256
  56.6 2.7 %chain.1 = (f32[32,128]{1,0:T(8,128)}, f32[16,32,128]{2,1,0:T(8,128)}) custom-call(s32[1]{0:T(128)} %bitcast.leaf_ref.group_ref, f32[8,32,128]{2,1,0:T(8,128)S(1)} %all-to-all-done.2.right_ref, f32[8,128,128]{2,1,0:T(8,128)S(1)} %pad_maximum_fusion.coupled_ref, f32[128,128]{1,0:T(8,128)S(1)} %bitcast.15), custom_call_target="tpu_custom_call" | custom-call | tf_op jit(solution)/shard_map/chain/pallas_call | solution.py:257
  59.3 7.7 %all-to-all-start.3 = ((f32[16,32,128]{2,1,0:T(8,128)}), f32[16,32,128]{2,1,0:T(8,128)S(1)}, u32[]{:S(2)}, u32[]{:S(2)}) async-start(f32[16,32,128]{2,1,0:T(8,128)} %get-tuple-element.10), calls=%async_computation.3 | async-start | bytes 524288 | tf_op jit(solution)/shard_map/all_to_all | solution.py:171
  67.0 3.5 %leaf_prepare.1.mapped_ref = bf16[28,160,256]{2,1,0:T(8,128)(2,1)S(1)} custom-call(f32[28,32,128]{2,1,0:T(8,128)S(1)} %get-tuple-element.9.after_ref.y_ref, f32[28,128,128]{2,1,0:T(8,128)} %bitcast.21, f32[28,128,128]{2,1,0:T(8,128)} %bitcast.23, s32[28,1,128]{2,1,0:T(1,128)} %bitcast.29), custom_call_target="tpu_custom_call" | custom-call | tf_op jit(solution)/shard_map/leaf_prepare/pallas_call | solution.py:245
  70.5 0.0 copy-start.3
  70.5 6.7 %all-to-all-done.3 = f32[16,32,128]{2,1,0:T(8,128)S(1)} async-done(((f32[16,32,128]{2,1,0:T(8,128)}), f32[16,32,128]{2,1,0:T(8,128)S(1)}, u32[]{:S(2)}, u32[]{:S(2)}) %all-to-all-start.3) | async-done | bytes 262176 | tf_op jit(solution)/shard_map/all_to_all | solution.py:171
  77.2 0.1 broadcast_in_dim.12
  77.3 17.9 %all_to_all.25.x_ref = f32[64,32,128]{2,1,0:T(8,128)S(1)} all-to-all(f32[64,32,128]{2,1,0:T(8,128)S(1)} %bitcast.24), channel_id=1, replica_groups={{9,10,17,18},{11,12,19,20},{14,13,22,21},{8,15,16,23},{25,26,33,34},{27..., dimensions={0} | all-to-all | bytes 2097152 | tf_op jit(solution)/shard_map/all_to_all | solution.py:171
  95.2 0.0 copy-done.3
  95.3 1.6 %leaf_backward.1 = f32[32,3584]{1,0:T(8,128)} custom-call(s32[1]{0:T(128)} %bitcast.leaf_ref.group_ref, s32[28]{0:T(128)S(1)} %bitcast.19, f32[64,32,128]{2,1,0:T(8,128)S(1)} %all_to_all.25.x_ref, bf16[28,160,256]{2,1,0:T(8,128)(2,1)S(1)} %leaf_prepare.1.mapped_ref), custom_call_target="tpu_custom_call" | custom-call | tf_op jit(solution)/shard_map/leaf_backward/pallas_call | solution.py:267
  (3 shorter events, 0.1 us)
Async XLA Ops:
  5.4 13.4 %copy-start = (f32[1,1,128,128]{3,2,1,0:T(8,128)S(1)}, f32[1,1,128,128]{3,2,1,0:T(8,128)}, u32[]{:S(2)}) copy-start(f32[1,1,128,128]{3,2,1,0:T(8,128)} %param.14) | copy-start | bytes 196612
  5.4 13.4 %copy-start.1 = (f32[1,1,128,128]{3,2,1,0:T(8,128)S(1)}, f32[1,1,128,128]{3,2,1,0:T(8,128)}, u32[]{:S(2)}) copy-start(f32[1,1,128,128]{3,2,1,0:T(8,128)} %param.15) | copy-start | bytes 196612
  5.4 24.0 %all-to-all-start = ((f32[64,32,128]{2,1,0:T(8,128)}), f32[64,32,128]{2,1,0:T(8,128)S(1)}, u32[]{:S(2)}, u32[]{:S(2)}) async-start(f32[64,32,128]{2,1,0:T(8,128)} %get-tuple-element.8), calls=%async_computation | async-start | bytes 2097152 | tf_op jit(solution)/shard_map/all_to_all | solution.py:171
  18.7 27.5 %copy-start.2 = (f32[1,32,128]{2,1,0:T(8,128)S(1)}, f32[1,32,128]{2,1,0:T(8,128)}, u32[]{:S(2)}) copy-start(f32[1,32,128]{2,1,0:T(8,128)} %param.9) | copy-start | bytes 49156
  18.9 3.1 %collective-permute-start = (f32[1,128,128]{2,1,0:T(8,128)S(1)}, f32[1,128,128]{2,1,0:T(8,128)S(1)}, u32[]{:S(2)}, u32[]{:S(2)}) collective-permute-start(f32[1,128,128]{2,1,0:T(8,128)S(1)} %coupled_inverse.1), channel_id=1, source_target_pairs={{0,64},{64,0},{128,192},{192,128},{256,320},{320,256},{384,448},{4... | collective-permute-start | bytes 196616 | tf_op jit(solution)/shard_map/ppermute | solution.py:199
  22.1 13.8 %collective-permute-start.1 = (f32[2,128,128]{2,1,0:T(8,128)S(1)}, f32[2,128,128]{2,1,0:T(8,128)S(1)}, u32[]{:S(2)}, u32[]{:S(2)}) collective-permute-start(f32[2,128,128]{2,1,0:T(8,128)S(1)} %pad_maximum_fusion.2), channel_id=1, source_target_pairs={{0,128},{64,192},{128,0},{192,64},{256,384},{320,448},{384,256},{4... | collective-permute-start | bytes 393224 | tf_op jit(solution)/shard_map/ppermute | solution.py:199
  30.1 16.1 %all-to-all-start.1 = ((f32[16,32,128]{2,1,0:T(8,128)}), f32[16,32,128]{2,1,0:T(8,128)S(1)}, u32[]{:S(2)}, u32[]{:S(2)}) async-start(f32[16,32,128]{2,1,0:T(8,128)} %reduce_sum.9), calls=%async_computation.1 | async-start | bytes 524288 | tf_op jit(solution)/shard_map/all_to_all | solution.py:171
  35.9 16.0 %collective-permute-start.2 = (f32[4,128,128]{2,1,0:T(8,128)S(1)}, f32[4,128,128]{2,1,0:T(8,128)S(1)}, u32[]{:S(2)}, u32[]{:S(2)}) collective-permute-start(f32[4,128,128]{2,1,0:T(8,128)S(1)} %pad_maximum_fusion.1), channel_id=1, source_target_pairs={{0,256},{64,320},{128,384},{192,448},{256,0},{320,64},{384,128},{4... | collective-permute-start | bytes 786440 | tf_op jit(solution)/shard_map/ppermute | solution.py:199
  47.1 9.5 %all-to-all-start.2 = ((f32[8,32,128]{2,1,0:T(8,128)}), f32[8,32,128]{2,1,0:T(8,128)S(1)}, u32[]{:S(2)}, u32[]{:S(2)}) async-start(f32[8,32,128]{2,1,0:T(8,128)} %reduce_right.1), calls=%async_computation.2 | async-start | bytes 262144 | tf_op jit(solution)/shard_map/all_to_all | solution.py:256
  59.3 17.9 %all-to-all-start.3 = ((f32[16,32,128]{2,1,0:T(8,128)}), f32[16,32,128]{2,1,0:T(8,128)S(1)}, u32[]{:S(2)}, u32[]{:S(2)}) async-start(f32[16,32,128]{2,1,0:T(8,128)} %get-tuple-element.10), calls=%async_computation.3 | async-start | bytes 524288 | tf_op jit(solution)/shard_map/all_to_all | solution.py:171
  70.5 24.8 %copy-start.3 = (s32[1,28,1]{1,2,0:T(1,128)S(1)}, s32[1,28,1]{1,2,0:T(1,128)}, u32[]{:S(2)}) copy-start(s32[1,28,1]{1,2,0:T(1,128)} %param.13) | copy-start | bytes 340

commit v13 on v12

--- a/solution.py
+++ b/solution.py
@@ -45,7 +45,7 @@
 
 
 def slot_of(owner, leaf):
-    shift = 1 - (leaf & 1)
+    shift = 2 - (leaf & 1)
     y = ((owner >> EDGE_BITS) - shift) & (EDGE - 1)
     z = (owner - shift) & (EDGE - 1)
     place = ((y >> 1) << (EDGE_BITS - 1)) | (z >> 1)
@@ -172,7 +172,7 @@
 
 
 def device(y, z, leaf):
-    shift = 1 - leaf % 2
+    shift = 2 - leaf % 2
     return (y + shift) % EDGE * EDGE + (z + shift) % EDGE
 
 

time: 97.5 us -> 96.4 us (0.989)
  the two profiles are of different devices: /device:TPU:2 before, /device:TPU:1 now
where the time goes in v13:
time: 96.4 us; the launch traced here: 95.8 us
  starting transfers between devices  44.7 us (46%)
  waiting for transfers between devices  18.4 us (19%)
  blocking collectives  17.4 us (18%)
  Pallas kernels  13.6 us (14%)
    all_to_all x3, starting transfers between devices, exchange(): lax.all_to_all(value, ('leaf', 'front'), 0, 0, tiled=True, axis_index_gro...  25.3 us
    all_to_all x1, blocking collectives, exchange(): lax.all_to_all(value, ('leaf', 'front'), 0, 0, tiled=True, axis_index_gro...  17.4 us
    all_to_all x3, waiting for transfers between devices, exchange(): lax.all_to_all(value, ('leaf', 'front'), 0, 0, tiled=True, axis_index_gro...  12 us
    all_to_all x1, starting transfers between devices, per_device(): right = lax.all_to_all(right, 'leaf', 0, 0, tiled=True)  9.76 us
    ppermute x3, starting transfers between devices, gather_by_bits(): value = jnp.concatenate([value, lax.ppermute(value, axis, pairs)], axis=0)  9.69 us
    all_to_all x1, waiting for transfers between devices, per_device(): right = lax.all_to_all(right, 'leaf', 0, 0, tiled=True)  5.23 us
    pallas_call x1, Pallas kernels, per_device(): call(leaf_forward, [SMEM, SMEM, columns, matrices, matrices, lines], [vec...  4.72 us
    pallas_call x1, Pallas kernels, per_device(): call(leaf_prepare, [vectors, matrices, matrices, lines], pl.BlockSpec((PR...  3.52 us
  transfers between devices with their start and end apart: 7, of which 5 were waited for; matrix products, arithmetic and copies ran while one was open for 1% of the time, Pallas kernels for 5%

profile of v13, /device:TPU:1, one launch (start us, length us, event | category | flops | bytes accessed | tf_op | source)
XLA Modules:
  0.0 95.8 jit_solution(17523482616526555670)
XLA Ops:
  0.6 4.7 %leaf_forward.1 = (f32[28,32,128]{2,1,0:T(8,128)S(1)}, f32[64,32,128]{2,1,0:T(8,128)}) custom-call(s32[1]{0:T(128)} %bitcast.leaf_ref.group_ref, s32[28]{0:T(128)} %bitcast.18, f32[32,3584]{1,0:T(8,128)} %bitcast.26, f32[28,128,128]{2,1,0:T(8,128)} %bitcast.20, f32[28,128,128]{2,1,0:T(8,128)} %bitcast.22, s32[28,1,128]{2,1,0:T(1,128)} %bitcast.28), custom_call_target="tpu_custom_call" | custom-call | tf_op jit(solution)/shard_map/leaf_forward/pallas_call | solution.py:230
  5.4 0.0 copy-start
  5.4 0.0 copy-start.1
  5.4 13.9 %all-to-all-start = ((f32[64,32,128]{2,1,0:T(8,128)}), f32[64,32,128]{2,1,0:T(8,128)S(1)}, u32[]{:S(2)}, u32[]{:S(2)}) async-start(f32[64,32,128]{2,1,0:T(8,128)} %get-tuple-element.8), calls=%async_computation | async-start | bytes 2097152 | tf_op jit(solution)/shard_map/all_to_all | solution.py:171
  19.3 0.0 copy-start.2
  19.3 0.0 copy-done
  19.3 0.0 copy-done.1
  19.3 0.2 coupled_inverse.1
  19.4 1.9 %collective-permute-start = (f32[1,128,128]{2,1,0:T(8,128)S(1)}, f32[1,128,128]{2,1,0:T(8,128)S(1)}, u32[]{:S(2)}, u32[]{:S(2)}) collective-permute-start(f32[1,128,128]{2,1,0:T(8,128)S(1)} %coupled_inverse.1), channel_id=1, source_target_pairs={{0,64},{64,0},{128,192},{192,128},{256,320},{320,256},{384,448},{4... | collective-permute-start | bytes 196616 | tf_op jit(solution)/shard_map/ppermute | solution.py:199
  21.4 1.2 %collective-permute-done = f32[1,128,128]{2,1,0:T(8,128)S(1)} collective-permute-done((f32[1,128,128]{2,1,0:T(8,128)S(1)}, f32[1,128,128]{2,1,0:T(8,128)S(1)}, u32[]{:S(2)}, u32[]{:S(2)}) %collective-permute-start) | collective-permute-done | bytes 65568 | tf_op jit(solution)/shard_map/ppermute | solution.py:199
  22.6 3.1 %collective-permute-start.1 = (f32[2,128,128]{2,1,0:T(8,128)S(1)}, f32[2,128,128]{2,1,0:T(8,128)S(1)}, u32[]{:S(2)}, u32[]{:S(2)}) collective-permute-start(f32[2,128,128]{2,1,0:T(8,128)S(1)} %pad_maximum_fusion.2), channel_id=1, source_target_pairs={{0,128},{64,192},{128,0},{192,64},{256,384},{320,448},{384,256},{4... | collective-permute-start | bytes 393224 | tf_op jit(solution)/shard_map/ppermute | solution.py:199
  25.7 3.0 %all-to-all-done = f32[64,32,128]{2,1,0:T(8,128)S(1)} async-done(((f32[64,32,128]{2,1,0:T(8,128)}), f32[64,32,128]{2,1,0:T(8,128)S(1)}, u32[]{:S(2)}, u32[]{:S(2)}) %all-to-all-start) | async-done | bytes 1048608 | tf_op jit(solution)/shard_map/all_to_all | solution.py:171
  28.7 0.8 reduce_sum.9
  29.5 5.5 %all-to-all-start.1 = ((f32[16,32,128]{2,1,0:T(8,128)}), f32[16,32,128]{2,1,0:T(8,128)S(1)}, u32[]{:S(2)}, u32[]{:S(2)}) async-start(f32[16,32,128]{2,1,0:T(8,128)} %reduce_sum.9), calls=%async_computation.1 | async-start | bytes 524288 | tf_op jit(solution)/shard_map/all_to_all | solution.py:171
  35.0 0.0 collective-permute-done.1
  35.0 4.6 %collective-permute-start.2 = (f32[4,128,128]{2,1,0:T(8,128)S(1)}, f32[4,128,128]{2,1,0:T(8,128)S(1)}, u32[]{:S(2)}, u32[]{:S(2)}) collective-permute-start(f32[4,128,128]{2,1,0:T(8,128)S(1)} %pad_maximum_fusion.1), channel_id=1, source_target_pairs={{0,256},{64,320},{128,384},{192,448},{256,0},{320,64},{384,128},{4... | collective-permute-start | bytes 786440 | tf_op jit(solution)/shard_map/ppermute | solution.py:199
  39.7 3.6 %all-to-all-done.1.received_ref = f32[16,32,128]{2,1,0:T(8,128)S(1)} async-done(((f32[16,32,128]{2,1,0:T(8,128)}), f32[16,32,128]{2,1,0:T(8,128)S(1)}, u32[]{:S(2)}, u32[]{:S(2)}) %all-to-all-start.1) | async-done | bytes 262176 | tf_op jit(solution)/shard_map/all_to_all | solution.py:171
  43.3 0.0 copy-done.2
  43.3 0.8 reduce_right.1
  44.1 9.8 %all-to-all-start.2 = ((f32[8,32,128]{2,1,0:T(8,128)}), f32[8,32,128]{2,1,0:T(8,128)S(1)}, u32[]{:S(2)}, u32[]{:S(2)}) async-start(f32[8,32,128]{2,1,0:T(8,128)} %reduce_right.1), calls=%async_computation.2 | async-start | bytes 262144 | tf_op jit(solution)/shard_map/all_to_all | solution.py:256
  53.9 0.0 collective-permute-done.2
  53.9 5.2 %all-to-all-done.2.right_ref = f32[8,32,128]{2,1,0:T(8,128)S(1)} async-done(((f32[8,32,128]{2,1,0:T(8,128)}), f32[8,32,128]{2,1,0:T(8,128)S(1)}, u32[]{:S(2)}, u32[]{:S(2)}) %all-to-all-start.2) | async-done | bytes 131104 | tf_op jit(solution)/shard_map/all_to_all | solution.py:256
  59.2 2.7 %chain.1 = (f32[32,128]{1,0:T(8,128)}, f32[16,32,128]{2,1,0:T(8,128)}) custom-call(s32[1]{0:T(128)} %bitcast.leaf_ref.group_ref, f32[8,32,128]{2,1,0:T(8,128)S(1)} %all-to-all-done.2.right_ref, f32[8,128,128]{2,1,0:T(8,128)S(1)} %pad_maximum_fusion.coupled_ref, f32[128,128]{1,0:T(8,128)S(1)} %bitcast.15), custom_call_target="tpu_custom_call" | custom-call | tf_op jit(solution)/shard_map/chain/pallas_call | solution.py:257
  61.9 5.9 %all-to-all-start.3 = ((f32[16,32,128]{2,1,0:T(8,128)}), f32[16,32,128]{2,1,0:T(8,128)S(1)}, u32[]{:S(2)}, u32[]{:S(2)}) async-start(f32[16,32,128]{2,1,0:T(8,128)} %get-tuple-element.10), calls=%async_computation.3 | async-start | bytes 524288 | tf_op jit(solution)/shard_map/all_to_all | solution.py:171
  67.8 3.5 %leaf_prepare.1.mapped_ref = bf16[28,160,256]{2,1,0:T(8,128)(2,1)S(1)} custom-call(f32[28,32,128]{2,1,0:T(8,128)S(1)} %get-tuple-element.9.after_ref.y_ref, f32[28,128,128]{2,1,0:T(8,128)} %bitcast.21, f32[28,128,128]{2,1,0:T(8,128)} %bitcast.23, s32[28,1,128]{2,1,0:T(1,128)} %bitcast.29), custom_call_target="tpu_custom_call" | custom-call | tf_op jit(solution)/shard_map/leaf_prepare/pallas_call | solution.py:245
  71.3 0.0 copy-start.3
  71.3 5.3 %all-to-all-done.3 = f32[16,32,128]{2,1,0:T(8,128)S(1)} async-done(((f32[16,32,128]{2,1,0:T(8,128)}), f32[16,32,128]{2,1,0:T(8,128)S(1)}, u32[]{:S(2)}, u32[]{:S(2)}) %all-to-all-start.3) | async-done | bytes 262176 | tf_op jit(solution)/shard_map/all_to_all | solution.py:171
  76.6 0.1 broadcast_in_dim.12
  76.7 17.4 %all_to_all.25.x_ref = f32[64,32,128]{2,1,0:T(8,128)S(1)} all-to-all(f32[64,32,128]{2,1,0:T(8,128)S(1)} %bitcast.24), channel_id=1, replica_groups={{18,19,26,27},{20,21,28,29},{23,22,31,30},{17,16,25,24},{34,35,42,43},{..., dimensions={0} | all-to-all | bytes 2097152 | tf_op jit(solution)/shard_map/all_to_all | solution.py:171
  94.2 0.0 copy-done.3
  94.2 1.6 %leaf_backward.1 = f32[32,3584]{1,0:T(8,128)} custom-call(s32[1]{0:T(128)} %bitcast.leaf_ref.group_ref, s32[28]{0:T(128)S(1)} %bitcast.19, f32[64,32,128]{2,1,0:T(8,128)S(1)} %all_to_all.25.x_ref, bf16[28,160,256]{2,1,0:T(8,128)(2,1)S(1)} %leaf_prepare.1.mapped_ref), custom_call_target="tpu_custom_call" | custom-call | tf_op jit(solution)/shard_map/leaf_backward/pallas_call | solution.py:267
  (3 shorter events, 0.1 us)
Async XLA Ops:
  5.4 13.9 %copy-start = (f32[1,1,128,128]{3,2,1,0:T(8,128)S(1)}, f32[1,1,128,128]{3,2,1,0:T(8,128)}, u32[]{:S(2)}) copy-start(f32[1,1,128,128]{3,2,1,0:T(8,128)} %param.14) | copy-start | bytes 196612
  5.4 13.9 %copy-start.1 = (f32[1,1,128,128]{3,2,1,0:T(8,128)S(1)}, f32[1,1,128,128]{3,2,1,0:T(8,128)}, u32[]{:S(2)}) copy-start(f32[1,1,128,128]{3,2,1,0:T(8,128)} %param.15) | copy-start | bytes 196612
  5.4 23.4 %all-to-all-start = ((f32[64,32,128]{2,1,0:T(8,128)}), f32[64,32,128]{2,1,0:T(8,128)S(1)}, u32[]{:S(2)}, u32[]{:S(2)}) async-start(f32[64,32,128]{2,1,0:T(8,128)} %get-tuple-element.8), calls=%async_computation | async-start | bytes 2097152 | tf_op jit(solution)/shard_map/all_to_all | solution.py:171
  19.3 24.1 %copy-start.2 = (f32[1,32,128]{2,1,0:T(8,128)S(1)}, f32[1,32,128]{2,1,0:T(8,128)}, u32[]{:S(2)}) copy-start(f32[1,32,128]{2,1,0:T(8,128)} %param.9) | copy-start | bytes 49156
  19.4 3.1 %collective-permute-start = (f32[1,128,128]{2,1,0:T(8,128)S(1)}, f32[1,128,128]{2,1,0:T(8,128)S(1)}, u32[]{:S(2)}, u32[]{:S(2)}) collective-permute-start(f32[1,128,128]{2,1,0:T(8,128)S(1)} %coupled_inverse.1), channel_id=1, source_target_pairs={{0,64},{64,0},{128,192},{192,128},{256,320},{320,256},{384,448},{4... | collective-permute-start | bytes 196616 | tf_op jit(solution)/shard_map/ppermute | solution.py:199
  22.6 12.4 %collective-permute-start.1 = (f32[2,128,128]{2,1,0:T(8,128)S(1)}, f32[2,128,128]{2,1,0:T(8,128)S(1)}, u32[]{:S(2)}, u32[]{:S(2)}) collective-permute-start(f32[2,128,128]{2,1,0:T(8,128)S(1)} %pad_maximum_fusion.2), channel_id=1, source_target_pairs={{0,128},{64,192},{128,0},{192,64},{256,384},{320,448},{384,256},{4... | collective-permute-start | bytes 393224 | tf_op jit(solution)/shard_map/ppermute | solution.py:199
  29.5 13.8 %all-to-all-start.1 = ((f32[16,32,128]{2,1,0:T(8,128)}), f32[16,32,128]{2,1,0:T(8,128)S(1)}, u32[]{:S(2)}, u32[]{:S(2)}) async-start(f32[16,32,128]{2,1,0:T(8,128)} %reduce_sum.9), calls=%async_computation.1 | async-start | bytes 524288 | tf_op jit(solution)/shard_map/all_to_all | solution.py:171
  35.0 18.9 %collective-permute-start.2 = (f32[4,128,128]{2,1,0:T(8,128)S(1)}, f32[4,128,128]{2,1,0:T(8,128)S(1)}, u32[]{:S(2)}, u32[]{:S(2)}) collective-permute-start(f32[4,128,128]{2,1,0:T(8,128)S(1)} %pad_maximum_fusion.1), channel_id=1, source_target_pairs={{0,256},{64,320},{128,384},{192,448},{256,0},{320,64},{384,128},{4... | collective-permute-start | bytes 786440 | tf_op jit(solution)/shard_map/ppermute | solution.py:199
  44.1 15.0 %all-to-all-start.2 = ((f32[8,32,128]{2,1,0:T(8,128)}), f32[8,32,128]{2,1,0:T(8,128)S(1)}, u32[]{:S(2)}, u32[]{:S(2)}) async-start(f32[8,32,128]{2,1,0:T(8,128)} %reduce_right.1), calls=%async_computation.2 | async-start | bytes 262144 | tf_op jit(solution)/shard_map/all_to_all | solution.py:256
  61.9 14.7 %all-to-all-start.3 = ((f32[16,32,128]{2,1,0:T(8,128)}), f32[16,32,128]{2,1,0:T(8,128)S(1)}, u32[]{:S(2)}, u32[]{:S(2)}) async-start(f32[16,32,128]{2,1,0:T(8,128)} %get-tuple-element.10), calls=%async_computation.3 | async-start | bytes 524288 | tf_op jit(solution)/shard_map/all_to_all | solution.py:171
  71.3 22.9 %copy-start.3 = (s32[1,28,1]{1,2,0:T(1,128)S(1)}, s32[1,28,1]{1,2,0:T(1,128)}, u32[]{:S(2)}) copy-start(s32[1,28,1]{1,2,0:T(1,128)} %param.13) | copy-start | bytes 340

commit v14 on v13

--- a/solution.py
+++ b/solution.py
@@ -45,7 +45,7 @@
 
 
 def slot_of(owner, leaf):
-    shift = 2 - (leaf & 1)
+    shift = 3 * (leaf & 1)
     y = ((owner >> EDGE_BITS) - shift) & (EDGE - 1)
     z = (owner - shift) & (EDGE - 1)
     place = ((y >> 1) << (EDGE_BITS - 1)) | (z >> 1)
@@ -172,7 +172,7 @@
 
 
 def device(y, z, leaf):
-    shift = 2 - leaf % 2
+    shift = 3 * (leaf % 2)
     return (y + shift) % EDGE * EDGE + (z + shift) % EDGE
 
 

time: 96.4 us -> 95.9 us (level)
  waiting for transfers between devices: 18.4 us -> 14.4 us
  starting transfers between devices: 44.7 us -> 46.6 us
  blocking collectives: 17.4 us -> 19.1 us
    all_to_all x3, waiting for transfers between devices: 12 us -> 7.93 us  [exchange(): lax.all_to_all(value, ('leaf', 'front'), 0, 0, tiled=True, axis_index_gro...]
    all_to_all x3, starting transfers between devices: 25.3 us -> 28.9 us  [exchange(): lax.all_to_all(value, ('leaf', 'front'), 0, 0, tiled=True, axis_index_gro...]
    all_to_all x1, starting transfers between devices: 9.76 us -> 7.96 us  [per_device(): right = lax.all_to_all(right, 'leaf', 0, 0, tiled=True)]
    all_to_all x1, blocking collectives: 17.4 us -> 19.1 us  [exchange(): lax.all_to_all(value, ('leaf', 'front'), 0, 0, tiled=True, axis_index_gro...]
where the time goes in v14:
time: 95.9 us; the launch traced here: 95.3 us
  starting transfers between devices  46.6 us (49%)
  blocking collectives  19.1 us (20%)
  waiting for transfers between devices  14.4 us (15%)
  Pallas kernels  13.6 us (14%)
    all_to_all x3, starting transfers between devices, exchange(): lax.all_to_all(value, ('leaf', 'front'), 0, 0, tiled=True, axis_index_gro...  28.9 us
    all_to_all x1, blocking collectives, exchange(): lax.all_to_all(value, ('leaf', 'front'), 0, 0, tiled=True, axis_index_gro...  19.1 us
    ppermute x3, starting transfers between devices, gather_by_bits(): value = jnp.concatenate([value, lax.ppermute(value, axis, pairs)], axis=0)  9.7 us
    all_to_all x1, starting transfers between devices, per_device(): right = lax.all_to_all(right, 'leaf', 0, 0, tiled=True)  7.96 us
    all_to_all x3, waiting for transfers between devices, exchange(): lax.all_to_all(value, ('leaf', 'front'), 0, 0, tiled=True, axis_index_gro...  7.93 us
    all_to_all x1, waiting for transfers between devices, per_device(): right = lax.all_to_all(right, 'leaf', 0, 0, tiled=True)  5.23 us
    pallas_call x1, Pallas kernels, per_device(): call(leaf_forward, [SMEM, SMEM, columns, matrices, matrices, lines], [vec...  4.72 us
    pallas_call x1, Pallas kernels, per_device(): call(leaf_prepare, [vectors, matrices, matrices, lines], pl.BlockSpec((PR...  3.52 us
  transfers between devices with their start and end apart: 7, of which 5 were waited for; matrix products, arithmetic and copies ran while one was open for 1% of the time, Pallas kernels for 5%

profile of v14, /device:TPU:1, one launch (start us, length us, event | category | flops | bytes accessed | tf_op | source)
XLA Modules:
  0.0 95.3 jit_solution(17455786132371289364)
XLA Ops:
  0.6 4.7 %leaf_forward.1 = (f32[28,32,128]{2,1,0:T(8,128)S(1)}, f32[64,32,128]{2,1,0:T(8,128)}) custom-call(s32[1]{0:T(128)} %bitcast.leaf_ref.group_ref, s32[28]{0:T(128)} %bitcast.18, f32[32,3584]{1,0:T(8,128)} %bitcast.26, f32[28,128,128]{2,1,0:T(8,128)} %bitcast.20, f32[28,128,128]{2,1,0:T(8,128)} %bitcast.22, s32[28,1,128]{2,1,0:T(1,128)} %bitcast.28), custom_call_target="tpu_custom_call" | custom-call | tf_op jit(solution)/shard_map/leaf_forward/pallas_call | solution.py:230
  5.4 0.0 copy-start
  5.4 0.0 copy-start.1
  5.4 13.9 %all-to-all-start = ((f32[64,32,128]{2,1,0:T(8,128)}), f32[64,32,128]{2,1,0:T(8,128)S(1)}, u32[]{:S(2)}, u32[]{:S(2)}) async-start(f32[64,32,128]{2,1,0:T(8,128)} %get-tuple-element.8), calls=%async_computation | async-start | bytes 2097152 | tf_op jit(solution)/shard_map/all_to_all | solution.py:171
  19.3 0.0 copy-start.2
  19.3 0.0 copy-done
  19.3 0.0 copy-done.1
  19.3 0.2 coupled_inverse.1
  19.4 1.9 %collective-permute-start = (f32[1,128,128]{2,1,0:T(8,128)S(1)}, f32[1,128,128]{2,1,0:T(8,128)S(1)}, u32[]{:S(2)}, u32[]{:S(2)}) collective-permute-start(f32[1,128,128]{2,1,0:T(8,128)S(1)} %coupled_inverse.1), channel_id=1, source_target_pairs={{0,64},{64,0},{128,192},{192,128},{256,320},{320,256},{384,448},{4... | collective-permute-start | bytes 196616 | tf_op jit(solution)/shard_map/ppermute | solution.py:199
  21.4 1.2 %collective-permute-done = f32[1,128,128]{2,1,0:T(8,128)S(1)} collective-permute-done((f32[1,128,128]{2,1,0:T(8,128)S(1)}, f32[1,128,128]{2,1,0:T(8,128)S(1)}, u32[]{:S(2)}, u32[]{:S(2)}) %collective-permute-start) | collective-permute-done | bytes 65568 | tf_op jit(solution)/shard_map/ppermute | solution.py:199
  22.6 3.1 %collective-permute-start.1 = (f32[2,128,128]{2,1,0:T(8,128)S(1)}, f32[2,128,128]{2,1,0:T(8,128)S(1)}, u32[]{:S(2)}, u32[]{:S(2)}) collective-permute-start(f32[2,128,128]{2,1,0:T(8,128)S(1)} %pad_maximum_fusion.2), channel_id=1, source_target_pairs={{0,128},{64,192},{128,0},{192,64},{256,384},{320,448},{384,256},{4... | collective-permute-start | bytes 393224 | tf_op jit(solution)/shard_map/ppermute | solution.py:199
  25.7 3.0 %all-to-all-done = f32[64,32,128]{2,1,0:T(8,128)S(1)} async-done(((f32[64,32,128]{2,1,0:T(8,128)}), f32[64,32,128]{2,1,0:T(8,128)S(1)}, u32[]{:S(2)}, u32[]{:S(2)}) %all-to-all-start) | async-done | bytes 1048608 | tf_op jit(solution)/shard_map/all_to_all | solution.py:171
  28.7 0.8 reduce_sum.9
  29.5 7.3 %all-to-all-start.1 = ((f32[16,32,128]{2,1,0:T(8,128)}), f32[16,32,128]{2,1,0:T(8,128)S(1)}, u32[]{:S(2)}, u32[]{:S(2)}) async-start(f32[16,32,128]{2,1,0:T(8,128)} %reduce_sum.9), calls=%async_computation.1 | async-start | bytes 524288 | tf_op jit(solution)/shard_map/all_to_all | solution.py:171
  36.8 0.0 collective-permute-done.1
  36.8 4.7 %collective-permute-start.2 = (f32[4,128,128]{2,1,0:T(8,128)S(1)}, f32[4,128,128]{2,1,0:T(8,128)S(1)}, u32[]{:S(2)}, u32[]{:S(2)}) collective-permute-start(f32[4,128,128]{2,1,0:T(8,128)S(1)} %pad_maximum_fusion.1), channel_id=1, source_target_pairs={{0,256},{64,320},{128,384},{192,448},{256,0},{320,64},{384,128},{4... | collective-permute-start | bytes 786440 | tf_op jit(solution)/shard_map/ppermute | solution.py:199
  41.5 2.1 %all-to-all-done.1.received_ref = f32[16,32,128]{2,1,0:T(8,128)S(1)} async-done(((f32[16,32,128]{2,1,0:T(8,128)}), f32[16,32,128]{2,1,0:T(8,128)S(1)}, u32[]{:S(2)}, u32[]{:S(2)}) %all-to-all-start.1) | async-done | bytes 262176 | tf_op jit(solution)/shard_map/all_to_all | solution.py:171
  43.6 0.0 copy-done.2
  43.6 0.8 reduce_right.1
  44.4 8.0 %all-to-all-start.2 = ((f32[8,32,128]{2,1,0:T(8,128)}), f32[8,32,128]{2,1,0:T(8,128)S(1)}, u32[]{:S(2)}, u32[]{:S(2)}) async-start(f32[8,32,128]{2,1,0:T(8,128)} %reduce_right.1), calls=%async_computation.2 | async-start | bytes 262144 | tf_op jit(solution)/shard_map/all_to_all | solution.py:256
  52.3 0.0 collective-permute-done.2
  52.4 5.2 %all-to-all-done.2.right_ref = f32[8,32,128]{2,1,0:T(8,128)S(1)} async-done(((f32[8,32,128]{2,1,0:T(8,128)}), f32[8,32,128]{2,1,0:T(8,128)S(1)}, u32[]{:S(2)}, u32[]{:S(2)}) %all-to-all-start.2) | async-done | bytes 131104 | tf_op jit(solution)/shard_map/all_to_all | solution.py:256
  57.6 2.7 %chain.1 = (f32[32,128]{1,0:T(8,128)}, f32[16,32,128]{2,1,0:T(8,128)}) custom-call(s32[1]{0:T(128)} %bitcast.leaf_ref.group_ref, f32[8,32,128]{2,1,0:T(8,128)S(1)} %all-to-all-done.2.right_ref, f32[8,128,128]{2,1,0:T(8,128)S(1)} %pad_maximum_fusion.coupled_ref, f32[128,128]{1,0:T(8,128)S(1)} %bitcast.15), custom_call_target="tpu_custom_call" | custom-call | tf_op jit(solution)/shard_map/chain/pallas_call | solution.py:257
  60.3 7.8 %all-to-all-start.3 = ((f32[16,32,128]{2,1,0:T(8,128)}), f32[16,32,128]{2,1,0:T(8,128)S(1)}, u32[]{:S(2)}, u32[]{:S(2)}) async-start(f32[16,32,128]{2,1,0:T(8,128)} %get-tuple-element.10), calls=%async_computation.3 | async-start | bytes 524288 | tf_op jit(solution)/shard_map/all_to_all | solution.py:171
  68.1 3.5 %leaf_prepare.1.mapped_ref = bf16[28,160,256]{2,1,0:T(8,128)(2,1)S(1)} custom-call(f32[28,32,128]{2,1,0:T(8,128)S(1)} %get-tuple-element.9.after_ref.y_ref, f32[28,128,128]{2,1,0:T(8,128)} %bitcast.21, f32[28,128,128]{2,1,0:T(8,128)} %bitcast.23, s32[28,1,128]{2,1,0:T(1,128)} %bitcast.29), custom_call_target="tpu_custom_call" | custom-call | tf_op jit(solution)/shard_map/leaf_prepare/pallas_call | solution.py:245
  71.6 0.0 copy-start.3
  71.6 2.8 %all-to-all-done.3 = f32[16,32,128]{2,1,0:T(8,128)S(1)} async-done(((f32[16,32,128]{2,1,0:T(8,128)}), f32[16,32,128]{2,1,0:T(8,128)S(1)}, u32[]{:S(2)}, u32[]{:S(2)}) %all-to-all-start.3) | async-done | bytes 262176 | tf_op jit(solution)/shard_map/all_to_all | solution.py:171
  74.4 0.1 broadcast_in_dim.12
  74.6 19.1 %all_to_all.25.x_ref = f32[64,32,128]{2,1,0:T(8,128)S(1)} all-to-all(f32[64,32,128]{2,1,0:T(8,128)S(1)} %bitcast.24), channel_id=1, replica_groups={{0,1,8,9},{2,3,10,11},{5,4,13,12},{7,6,15,14},{16,17,24,25},{18,19,26,2..., dimensions={0} | all-to-all | bytes 2097152 | tf_op jit(solution)/shard_map/all_to_all | solution.py:171
  93.7 0.0 copy-done.3
  93.7 1.6 %leaf_backward.1 = f32[32,3584]{1,0:T(8,128)} custom-call(s32[1]{0:T(128)} %bitcast.leaf_ref.group_ref, s32[28]{0:T(128)S(1)} %bitcast.19, f32[64,32,128]{2,1,0:T(8,128)S(1)} %all_to_all.25.x_ref, bf16[28,160,256]{2,1,0:T(8,128)(2,1)S(1)} %leaf_prepare.1.mapped_ref), custom_call_target="tpu_custom_call" | custom-call | tf_op jit(solution)/shard_map/leaf_backward/pallas_call | solution.py:267
  (3 shorter events, 0.1 us)
Async XLA Ops:
  5.4 13.9 %copy-start = (f32[1,1,128,128]{3,2,1,0:T(8,128)S(1)}, f32[1,1,128,128]{3,2,1,0:T(8,128)}, u32[]{:S(2)}) copy-start(f32[1,1,128,128]{3,2,1,0:T(8,128)} %param.14) | copy-start | bytes 196612
  5.4 13.9 %copy-start.1 = (f32[1,1,128,128]{3,2,1,0:T(8,128)S(1)}, f32[1,1,128,128]{3,2,1,0:T(8,128)}, u32[]{:S(2)}) copy-start(f32[1,1,128,128]{3,2,1,0:T(8,128)} %param.15) | copy-start | bytes 196612
  5.4 23.4 %all-to-all-start = ((f32[64,32,128]{2,1,0:T(8,128)}), f32[64,32,128]{2,1,0:T(8,128)S(1)}, u32[]{:S(2)}, u32[]{:S(2)}) async-start(f32[64,32,128]{2,1,0:T(8,128)} %get-tuple-element.8), calls=%async_computation | async-start | bytes 2097152 | tf_op jit(solution)/shard_map/all_to_all | solution.py:171
  19.3 24.3 %copy-start.2 = (f32[1,32,128]{2,1,0:T(8,128)S(1)}, f32[1,32,128]{2,1,0:T(8,128)}, u32[]{:S(2)}) copy-start(f32[1,32,128]{2,1,0:T(8,128)} %param.9) | copy-start | bytes 49156
  19.4 3.1 %collective-permute-start = (f32[1,128,128]{2,1,0:T(8,128)S(1)}, f32[1,128,128]{2,1,0:T(8,128)S(1)}, u32[]{:S(2)}, u32[]{:S(2)}) collective-permute-start(f32[1,128,128]{2,1,0:T(8,128)S(1)} %coupled_inverse.1), channel_id=1, source_target_pairs={{0,64},{64,0},{128,192},{192,128},{256,320},{320,256},{384,448},{4... | collective-permute-start | bytes 196616 | tf_op jit(solution)/shard_map/ppermute | solution.py:199
  22.6 14.2 %collective-permute-start.1 = (f32[2,128,128]{2,1,0:T(8,128)S(1)}, f32[2,128,128]{2,1,0:T(8,128)S(1)}, u32[]{:S(2)}, u32[]{:S(2)}) collective-permute-start(f32[2,128,128]{2,1,0:T(8,128)S(1)} %pad_maximum_fusion.2), channel_id=1, source_target_pairs={{0,128},{64,192},{128,0},{192,64},{256,384},{320,448},{384,256},{4... | collective-permute-start | bytes 393224 | tf_op jit(solution)/shard_map/ppermute | solution.py:199
  29.5 14.0 %all-to-all-start.1 = ((f32[16,32,128]{2,1,0:T(8,128)}), f32[16,32,128]{2,1,0:T(8,128)S(1)}, u32[]{:S(2)}, u32[]{:S(2)}) async-start(f32[16,32,128]{2,1,0:T(8,128)} %reduce_sum.9), calls=%async_computation.1 | async-start | bytes 524288 | tf_op jit(solution)/shard_map/all_to_all | solution.py:171
  36.8 15.5 %collective-permute-start.2 = (f32[4,128,128]{2,1,0:T(8,128)S(1)}, f32[4,128,128]{2,1,0:T(8,128)S(1)}, u32[]{:S(2)}, u32[]{:S(2)}) collective-permute-start(f32[4,128,128]{2,1,0:T(8,128)S(1)} %pad_maximum_fusion.1), channel_id=1, source_target_pairs={{0,256},{64,320},{128,384},{192,448},{256,0},{320,64},{384,128},{4... | collective-permute-start | bytes 786440 | tf_op jit(solution)/shard_map/ppermute | solution.py:199
  44.4 13.2 %all-to-all-start.2 = ((f32[8,32,128]{2,1,0:T(8,128)}), f32[8,32,128]{2,1,0:T(8,128)S(1)}, u32[]{:S(2)}, u32[]{:S(2)}) async-start(f32[8,32,128]{2,1,0:T(8,128)} %reduce_right.1), calls=%async_computation.2 | async-start | bytes 262144 | tf_op jit(solution)/shard_map/all_to_all | solution.py:256
  60.3 14.1 %all-to-all-start.3 = ((f32[16,32,128]{2,1,0:T(8,128)}), f32[16,32,128]{2,1,0:T(8,128)S(1)}, u32[]{:S(2)}, u32[]{:S(2)}) async-start(f32[16,32,128]{2,1,0:T(8,128)} %get-tuple-element.10), calls=%async_computation.3 | async-start | bytes 524288 | tf_op jit(solution)/shard_map/all_to_all | solution.py:171
  71.6 22.1 %copy-start.3 = (s32[1,28,1]{1,2,0:T(1,128)S(1)}, s32[1,28,1]{1,2,0:T(1,128)}, u32[]{:S(2)}) copy-start(s32[1,28,1]{1,2,0:T(1,128)} %param.13) | copy-start | bytes 340

commit v15 on v11

--- a/solution.py
+++ b/solution.py
@@ -116,18 +116,20 @@
     rows = out_ref.shape[0]
     size = out_ref.shape[1] // count
     stores = []
-    for f in range(count):
-        owned = jnp.concatenate(split(x_ref[slot_of(owner_ref[f], leaf_ref[0])]), axis=0)
-        picked = three_parts(dot(owned, mapped_ref[f, :size], NN), rows, size)
-        own = mapped_ref[f, size:].astype(jnp.float32)
-        out_ref[:, f * size : (f + 1) * size] = (own[:, :size] + own[:, size:]) - picked
-        if (f + 1) % BACKWARD_CHUNK == 0:
-            here = slice((f + 1 - BACKWARD_CHUNK) * size, (f + 1) * size)
-            store = pltpu.make_async_copy(
-                out_ref.at[:, here], out_hbm.at[:, here], stored.at[f // BACKWARD_CHUNK]
-            )
-            store.start()
-            stores.append(store)
+    for first in range(0, count, BACKWARD_CHUNK):
+        chunk = range(first, first + BACKWARD_CHUNK)
+        owned = [jnp.concatenate(split(x_ref[slot_of(owner_ref[f], leaf_ref[0])]), axis=0) for f in chunk]
+        parts = [dot(value, mapped_ref[f, :size], NN) for f, value in zip(chunk, owned)]
+        for f, part in zip(chunk, parts):
+            own = mapped_ref[f, size:].astype(jnp.float32)
+            own = own[:, :size] + own[:, size:]
+            out_ref[:, f * size : (f + 1) * size] = own - three_parts(part, rows, size)
+        here = slice(first * size, (first + BACKWARD_CHUNK) * size)
+        store = pltpu.make_async_copy(
+            out_ref.at[:, here], out_hbm.at[:, here], stored.at[first // BACKWARD_CHUNK]
+        )
+        store.start()
+        stores.append(store)
     for store in stores:
         store.wait()
 

time: 95 us -> 95 us (level)
  no operation moved by 1% of the time
where the time goes in v15:
time: 95 us; the launch traced here: 94.4 us
  starting transfers between devices  44.5 us (47%)
  waiting for transfers between devices  18.6 us (20%)
  blocking collectives  16.1 us (17%)
  Pallas kernels  13.6 us (14%)
    all_to_all x3, starting transfers between devices, exchange(): lax.all_to_all(value, ('leaf', 'front'), 0, 0, tiled=True, axis_index_gro...  26.1 us
    all_to_all x1, blocking collectives, exchange(): lax.all_to_all(value, ('leaf', 'front'), 0, 0, tiled=True, axis_index_gro...  16.1 us
    all_to_all x3, waiting for transfers between devices, exchange(): lax.all_to_all(value, ('leaf', 'front'), 0, 0, tiled=True, axis_index_gro...  12.1 us
    ppermute x3, starting transfers between devices, gather_by_bits(): value = jnp.concatenate([value, lax.ppermute(value, axis, pairs)], axis=0)  9.69 us
    all_to_all x1, starting transfers between devices, per_device(): right = lax.all_to_all(right, 'leaf', 0, 0, tiled=True)  8.75 us
    all_to_all x1, waiting for transfers between devices, per_device(): right = lax.all_to_all(right, 'leaf', 0, 0, tiled=True)  5.23 us
    pallas_call x1, Pallas kernels, per_device(): call(leaf_forward, [SMEM, SMEM, columns, matrices, matrices, lines], [vec...  4.72 us
    pallas_call x1, Pallas kernels, per_device(): call(leaf_prepare, [vectors, matrices, matrices, lines], pl.BlockSpec((PR...  3.52 us
  transfers between devices with their start and end apart: 7, of which 5 were waited for; matrix products, arithmetic and copies ran while one was open for 1% of the time, Pallas kernels for 5%

profile of v15, /device:TPU:1, one launch (start us, length us, event | category | flops | bytes accessed | tf_op | source)
XLA Modules:
  0.0 94.4 jit_solution(1626019092224292102)
XLA Ops:
  0.6 4.7 %leaf_forward.1 = (f32[28,32,128]{2,1,0:T(8,128)S(1)}, f32[64,32,128]{2,1,0:T(8,128)}) custom-call(s32[1]{0:T(128)} %bitcast.leaf_ref.group_ref, s32[28]{0:T(128)} %bitcast.18, f32[32,3584]{1,0:T(8,128)} %bitcast.26, f32[28,128,128]{2,1,0:T(8,128)} %bitcast.20, f32[28,128,128]{2,1,0:T(8,128)} %bitcast.22, s32[28,1,128]{2,1,0:T(1,128)} %bitcast.28), custom_call_target="tpu_custom_call" | custom-call | tf_op jit(solution)/shard_map/leaf_forward/pallas_call | solution.py:230
  5.4 0.0 copy-start
  5.4 0.0 copy-start.1
  5.4 13.9 %all-to-all-start = ((f32[64,32,128]{2,1,0:T(8,128)}), f32[64,32,128]{2,1,0:T(8,128)S(1)}, u32[]{:S(2)}, u32[]{:S(2)}) async-start(f32[64,32,128]{2,1,0:T(8,128)} %get-tuple-element.8), calls=%async_computation | async-start | bytes 2097152 | tf_op jit(solution)/shard_map/all_to_all | solution.py:172
  19.3 0.0 copy-start.2
  19.3 0.0 copy-done
  19.3 0.0 copy-done.1
  19.3 0.2 coupled_inverse.1
  19.4 1.9 %collective-permute-start = (f32[1,128,128]{2,1,0:T(8,128)S(1)}, f32[1,128,128]{2,1,0:T(8,128)S(1)}, u32[]{:S(2)}, u32[]{:S(2)}) collective-permute-start(f32[1,128,128]{2,1,0:T(8,128)S(1)} %coupled_inverse.1), channel_id=1, source_target_pairs={{0,64},{64,0},{128,192},{192,128},{256,320},{320,256},{384,448},{4... | collective-permute-start | bytes 196616 | tf_op jit(solution)/shard_map/ppermute | solution.py:199
  21.4 1.2 %collective-permute-done = f32[1,128,128]{2,1,0:T(8,128)S(1)} collective-permute-done((f32[1,128,128]{2,1,0:T(8,128)S(1)}, f32[1,128,128]{2,1,0:T(8,128)S(1)}, u32[]{:S(2)}, u32[]{:S(2)}) %collective-permute-start) | collective-permute-done | bytes 65568 | tf_op jit(solution)/shard_map/ppermute | solution.py:199
  22.6 3.1 %collective-permute-start.1 = (f32[2,128,128]{2,1,0:T(8,128)S(1)}, f32[2,128,128]{2,1,0:T(8,128)S(1)}, u32[]{:S(2)}, u32[]{:S(2)}) collective-permute-start(f32[2,128,128]{2,1,0:T(8,128)S(1)} %pad_maximum_fusion.2), channel_id=1, source_target_pairs={{0,128},{64,192},{128,0},{192,64},{256,384},{320,448},{384,256},{4... | collective-permute-start | bytes 393224 | tf_op jit(solution)/shard_map/ppermute | solution.py:199
  25.7 3.0 %all-to-all-done = f32[64,32,128]{2,1,0:T(8,128)S(1)} async-done(((f32[64,32,128]{2,1,0:T(8,128)}), f32[64,32,128]{2,1,0:T(8,128)S(1)}, u32[]{:S(2)}, u32[]{:S(2)}) %all-to-all-start) | async-done | bytes 1048608 | tf_op jit(solution)/shard_map/all_to_all | solution.py:172
  28.7 0.8 reduce_sum.9
  29.5 5.5 %all-to-all-start.1 = ((f32[16,32,128]{2,1,0:T(8,128)}), f32[16,32,128]{2,1,0:T(8,128)S(1)}, u32[]{:S(2)}, u32[]{:S(2)}) async-start(f32[16,32,128]{2,1,0:T(8,128)} %reduce_sum.9), calls=%async_computation.1 | async-start | bytes 524288 | tf_op jit(solution)/shard_map/all_to_all | solution.py:172
  35.0 0.0 collective-permute-done.1
  35.0 4.6 %collective-permute-start.2 = (f32[4,128,128]{2,1,0:T(8,128)S(1)}, f32[4,128,128]{2,1,0:T(8,128)S(1)}, u32[]{:S(2)}, u32[]{:S(2)}) collective-permute-start(f32[4,128,128]{2,1,0:T(8,128)S(1)} %pad_maximum_fusion.1), channel_id=1, source_target_pairs={{0,256},{64,320},{128,384},{192,448},{256,0},{320,64},{384,128},{4... | collective-permute-start | bytes 786440 | tf_op jit(solution)/shard_map/ppermute | solution.py:199
  39.7 3.8 %all-to-all-done.1.received_ref = f32[16,32,128]{2,1,0:T(8,128)S(1)} async-done(((f32[16,32,128]{2,1,0:T(8,128)}), f32[16,32,128]{2,1,0:T(8,128)S(1)}, u32[]{:S(2)}, u32[]{:S(2)}) %all-to-all-start.1) | async-done | bytes 262176 | tf_op jit(solution)/shard_map/all_to_all | solution.py:172
  43.5 0.0 copy-done.2
  43.5 0.8 reduce_right.1
  44.3 8.7 %all-to-all-start.2 = ((f32[8,32,128]{2,1,0:T(8,128)}), f32[8,32,128]{2,1,0:T(8,128)S(1)}, u32[]{:S(2)}, u32[]{:S(2)}) async-start(f32[8,32,128]{2,1,0:T(8,128)} %reduce_right.1), calls=%async_computation.2 | async-start | bytes 262144 | tf_op jit(solution)/shard_map/all_to_all | solution.py:256
  53.1 0.0 collective-permute-done.2
  53.1 5.2 %all-to-all-done.2.right_ref = f32[8,32,128]{2,1,0:T(8,128)S(1)} async-done(((f32[8,32,128]{2,1,0:T(8,128)}), f32[8,32,128]{2,1,0:T(8,128)S(1)}, u32[]{:S(2)}, u32[]{:S(2)}) %all-to-all-start.2) | async-done | bytes 131104 | tf_op jit(solution)/shard_map/all_to_all | solution.py:256
  58.3 2.7 %chain.1 = (f32[32,128]{1,0:T(8,128)}, f32[16,32,128]{2,1,0:T(8,128)}) custom-call(s32[1]{0:T(128)} %bitcast.leaf_ref.group_ref, f32[8,32,128]{2,1,0:T(8,128)S(1)} %all-to-all-done.2.right_ref, f32[8,128,128]{2,1,0:T(8,128)S(1)} %pad_maximum_fusion.coupled_ref, f32[128,128]{1,0:T(8,128)S(1)} %bitcast.15), custom_call_target="tpu_custom_call" | custom-call | tf_op jit(solution)/shard_map/chain/pallas_call | solution.py:257
  61.0 6.7 %all-to-all-start.3 = ((f32[16,32,128]{2,1,0:T(8,128)}), f32[16,32,128]{2,1,0:T(8,128)S(1)}, u32[]{:S(2)}, u32[]{:S(2)}) async-start(f32[16,32,128]{2,1,0:T(8,128)} %get-tuple-element.10), calls=%async_computation.3 | async-start | bytes 524288 | tf_op jit(solution)/shard_map/all_to_all | solution.py:172
  67.7 3.5 %leaf_prepare.1.mapped_ref = bf16[28,160,256]{2,1,0:T(8,128)(2,1)S(1)} custom-call(f32[28,32,128]{2,1,0:T(8,128)S(1)} %get-tuple-element.9.after_ref.y_ref, f32[28,128,128]{2,1,0:T(8,128)} %bitcast.21, f32[28,128,128]{2,1,0:T(8,128)} %bitcast.23, s32[28,1,128]{2,1,0:T(1,128)} %bitcast.29), custom_call_target="tpu_custom_call" | custom-call | tf_op jit(solution)/shard_map/leaf_prepare/pallas_call | solution.py:245
  71.3 0.0 copy-start.3
  71.3 5.3 %all-to-all-done.3 = f32[16,32,128]{2,1,0:T(8,128)S(1)} async-done(((f32[16,32,128]{2,1,0:T(8,128)}), f32[16,32,128]{2,1,0:T(8,128)S(1)}, u32[]{:S(2)}, u32[]{:S(2)}) %all-to-all-start.3) | async-done | bytes 262176 | tf_op jit(solution)/shard_map/all_to_all | solution.py:172
  76.6 0.1 broadcast_in_dim.12
  76.7 16.1 %all_to_all.25.x_ref = f32[64,32,128]{2,1,0:T(8,128)S(1)} all-to-all(f32[64,32,128]{2,1,0:T(8,128)S(1)} %bitcast.24), channel_id=1, replica_groups={{0,1,8,9},{2,3,10,11},{5,4,13,12},{7,6,15,14},{16,17,24,25},{18,19,26,2..., dimensions={0} | all-to-all | bytes 2097152 | tf_op jit(solution)/shard_map/all_to_all | solution.py:172
  92.8 0.0 copy-done.3
  92.8 1.6 %leaf_backward.1 = f32[32,3584]{1,0:T(8,128)} custom-call(s32[1]{0:T(128)} %bitcast.leaf_ref.group_ref, s32[28]{0:T(128)S(1)} %bitcast.19, f32[64,32,128]{2,1,0:T(8,128)S(1)} %all_to_all.25.x_ref, bf16[28,160,256]{2,1,0:T(8,128)(2,1)S(1)} %leaf_prepare.1.mapped_ref), custom_call_target="tpu_custom_call" | custom-call | tf_op jit(solution)/shard_map/leaf_backward/pallas_call | solution.py:267
  (3 shorter events, 0.1 us)
Async XLA Ops:
  5.4 13.9 %copy-start = (f32[1,1,128,128]{3,2,1,0:T(8,128)S(1)}, f32[1,1,128,128]{3,2,1,0:T(8,128)}, u32[]{:S(2)}) copy-start(f32[1,1,128,128]{3,2,1,0:T(8,128)} %param.14) | copy-start | bytes 196612
  5.4 13.9 %copy-start.1 = (f32[1,1,128,128]{3,2,1,0:T(8,128)S(1)}, f32[1,1,128,128]{3,2,1,0:T(8,128)}, u32[]{:S(2)}) copy-start(f32[1,1,128,128]{3,2,1,0:T(8,128)} %param.15) | copy-start | bytes 196612
  5.4 23.4 %all-to-all-start = ((f32[64,32,128]{2,1,0:T(8,128)}), f32[64,32,128]{2,1,0:T(8,128)S(1)}, u32[]{:S(2)}, u32[]{:S(2)}) async-start(f32[64,32,128]{2,1,0:T(8,128)} %get-tuple-element.8), calls=%async_computation | async-start | bytes 2097152 | tf_op jit(solution)/shard_map/all_to_all | solution.py:172
  19.3 24.2 %copy-start.2 = (f32[1,32,128]{2,1,0:T(8,128)S(1)}, f32[1,32,128]{2,1,0:T(8,128)}, u32[]{:S(2)}) copy-start(f32[1,32,128]{2,1,0:T(8,128)} %param.9) | copy-start | bytes 49156
  19.4 3.1 %collective-permute-start = (f32[1,128,128]{2,1,0:T(8,128)S(1)}, f32[1,128,128]{2,1,0:T(8,128)S(1)}, u32[]{:S(2)}, u32[]{:S(2)}) collective-permute-start(f32[1,128,128]{2,1,0:T(8,128)S(1)} %coupled_inverse.1), channel_id=1, source_target_pairs={{0,64},{64,0},{128,192},{192,128},{256,320},{320,256},{384,448},{4... | collective-permute-start | bytes 196616 | tf_op jit(solution)/shard_map/ppermute | solution.py:199
  22.6 12.4 %collective-permute-start.1 = (f32[2,128,128]{2,1,0:T(8,128)S(1)}, f32[2,128,128]{2,1,0:T(8,128)S(1)}, u32[]{:S(2)}, u32[]{:S(2)}) collective-permute-start(f32[2,128,128]{2,1,0:T(8,128)S(1)} %pad_maximum_fusion.2), channel_id=1, source_target_pairs={{0,128},{64,192},{128,0},{192,64},{256,384},{320,448},{384,256},{4... | collective-permute-start | bytes 393224 | tf_op jit(solution)/shard_map/ppermute | solution.py:199
  29.5 14.0 %all-to-all-start.1 = ((f32[16,32,128]{2,1,0:T(8,128)}), f32[16,32,128]{2,1,0:T(8,128)S(1)}, u32[]{:S(2)}, u32[]{:S(2)}) async-start(f32[16,32,128]{2,1,0:T(8,128)} %reduce_sum.9), calls=%async_computation.1 | async-start | bytes 524288 | tf_op jit(solution)/shard_map/all_to_all | solution.py:172
  35.0 18.0 %collective-permute-start.2 = (f32[4,128,128]{2,1,0:T(8,128)S(1)}, f32[4,128,128]{2,1,0:T(8,128)S(1)}, u32[]{:S(2)}, u32[]{:S(2)}) collective-permute-start(f32[4,128,128]{2,1,0:T(8,128)S(1)} %pad_maximum_fusion.1), channel_id=1, source_target_pairs={{0,256},{64,320},{128,384},{192,448},{256,0},{320,64},{384,128},{4... | collective-permute-start | bytes 786440 | tf_op jit(solution)/shard_map/ppermute | solution.py:199
  44.3 14.0 %all-to-all-start.2 = ((f32[8,32,128]{2,1,0:T(8,128)}), f32[8,32,128]{2,1,0:T(8,128)S(1)}, u32[]{:S(2)}, u32[]{:S(2)}) async-start(f32[8,32,128]{2,1,0:T(8,128)} %reduce_right.1), calls=%async_computation.2 | async-start | bytes 262144 | tf_op jit(solution)/shard_map/all_to_all | solution.py:256
  61.0 15.5 %all-to-all-start.3 = ((f32[16,32,128]{2,1,0:T(8,128)}), f32[16,32,128]{2,1,0:T(8,128)S(1)}, u32[]{:S(2)}, u32[]{:S(2)}) async-start(f32[16,32,128]{2,1,0:T(8,128)} %get-tuple-element.10), calls=%async_computation.3 | async-start | bytes 524288 | tf_op jit(solution)/shard_map/all_to_all | solution.py:172
  71.3 21.5 %copy-start.3 = (s32[1,28,1]{1,2,0:T(1,128)S(1)}, s32[1,28,1]{1,2,0:T(1,128)}, u32[]{:S(2)}) copy-start(s32[1,28,1]{1,2,0:T(1,128)} %param.13) | copy-start | bytes 340
